TPU v7x, 32 devices: a whole 2x2x4 slice. The times are simulated.
32 devices in a mesh: seq: 8 (over z, x), head: 4 (over y, core).
Axes of the slice: x: 2, y: 2, z: 4, core: 2. Of those that a mesh axis runs over, the one named last changes fastest.
Arguments:
- hidden_in: bfloat16 [8192, 768], P('seq'), may hold values from -6 to 6
- q_weight: bfloat16 [768, 768], P(None, 'head'), may hold values from -0.3125 to 0.3125
- q_bias: float32 [768], P('head'), may hold values from -3 to 3
- k_weight: bfloat16 [768, 768], P(None, 'head'), may hold values from -0.21875 to 0.21875
- v_weight: bfloat16 [768, 768], P(None, 'head'), may hold values from -0.21875 to 0.21875
- v_bias: float32 [768], P('head'), may hold values from -3 to 3
- o_weight: bfloat16 [768, 768], P('head'), may hold values from -0.875 to 0.875
- o_bias: float32 [768], replicated, may hold values from -3 to 3
- norm1_gain: float32 [768], replicated, may hold values from 0.5 to 1.5
- norm1_shift: float32 [768], replicated, may hold values from -3 to 3
- up_weight: bfloat16 [768, 3072], P(None, 'head'), may hold values from -0.21875 to 0.21875
- up_bias: float32 [3072], P('head'), may hold values from -3 to 3
- down_weight: bfloat16 [3072, 768], P('head'), may hold values from -0.109375 to 0.109375
- down_bias: float32 [768], replicated, may hold values from -3 to 3
- norm2_gain: float32 [768], replicated, may hold values from 0.5 to 1.5
- norm2_shift: float32 [768], replicated, may hold values from -3 to 3
- doc_mask: int32 [8192], replicated, may hold values from 0 to 1, as said below
- doc_blocks: int32 [2], replicated, may hold values from 8 to 64, as said below
- rand_blocks: int32 [128, 3], P('seq'), may hold values from 2 to 63, as said below
- out_grad: float32 [8192, 768], P(('seq', 'head')), may hold values from -6 to 6
Outputs:
- layer_out: float32 [8192, 768], P(('seq', 'head'))
- in_grad: float32 [8192, 768], P(('seq', 'head'))
- q_weight_grad: float32 [768, 768], P(None, 'head')
- q_bias_grad: float32 [768], P('head')
- k_weight_grad: float32 [768, 768], P(None, 'head')
- v_weight_grad: float32 [768, 768], P(None, 'head')
- v_bias_grad: float32 [768], P('head')
- o_weight_grad: float32 [768, 768], P('head')
- o_bias_grad: float32 [768], replicated
- norm1_gain_grad: float32 [768], replicated
- norm1_shift_grad: float32 [768], replicated
- up_weight_grad: float32 [768, 3072], P(None, 'head')
- up_bias_grad: float32 [3072], P('head')
- down_weight_grad: float32 [3072, 768], P('head')
- down_bias_grad: float32 [768], replicated
- norm2_gain_grad: float32 [768], replicated
- norm2_shift_grad: float32 [768], replicated
Inputs may be any that keep to these rules, and one draw needn't show every extreme that they name: `doc_blocks`: some slot has 64 blocks and some slot 8. `doc_mask`: in each slot the ones are exactly its first positions; their number exceeds 64 times (the slot's doc_blocks - 1) and is at most 64 times its doc_blocks. `rand_blocks`: A row holds three different block indices of its block's slot, each below that slot's doc_blocks and more than one away from the row's own block index within the slot.
All inputs are finite; a program needn't handle non-finite values.
Results may differ from a plain program's by a relative error of at most 0.019.
Values may be sent and summed in bfloat16 or wider, within the bound.
A program may use at most 256 MiB of HBM per device.

v0:
```python
import jax
import jax.numpy as jnp
from jax import lax
from jax.sharding import PartitionSpec as P

HD = 64
BLOCK = 64
SLOT_LEN = 4096


NEG = -1e30
EPS = 1e-12


def partner_2(value, axis, apart):
    mask = 2**apart
    pairs = [(source, source ^ mask) for source in range(lax.axis_size(axis))]
    return lax.ppermute(value, axis, pairs)


def norm_forward(values_in, gain_vec, shift_vec):
    row_mean = jnp.mean(values_in, axis=1, keepdims=True)
    centred = values_in - row_mean
    inv_std = lax.rsqrt(jnp.mean(centred * centred, axis=1, keepdims=True) + EPS)
    normed = centred * inv_std
    return (normed * gain_vec + shift_vec, normed, inv_std)


def norm_backward(gradient, normed, inv_std, gain_vec):
    scaled = gradient * gain_vec
    inner_term = (
        scaled
        - jnp.mean(scaled, axis=1, keepdims=True)
        - normed * jnp.mean(scaled * normed, axis=1, keepdims=True)
    )
    return (inner_term * inv_std, jnp.sum(gradient * normed, axis=0), jnp.sum(gradient, axis=0))


def contract_rows(left, right):
    return lax.dot_general(
        left, right, (((0,), (0,)), ((), ())), preferred_element_type=jnp.float32
    )


def contract_cols(left, right):
    return lax.dot_general(
        left, right, (((1,), (1,)), ((), ())), preferred_element_type=jnp.float32
    )


def softmax_rows(scores):
    row_max = jnp.max(scores, axis=-1, keepdims=True)
    expo = jnp.exp(scores - row_max)
    total = jnp.sum(expo, axis=-1, keepdims=True)
    return (expo / total, row_max + jnp.log(total))


def gelu_grad(pre_act, act_grad):
    gelu_value, gelu_pull = jax.vjp(
        lambda inner_val: jax.nn.gelu(inner_val, approximate=True), pre_act
    )
    return gelu_pull(act_grad)[0].astype(jnp.bfloat16)


def per_device(
    hidden_in,
    q_weight,
    q_bias,
    k_weight,
    v_weight,
    v_bias,
    o_weight,
    o_bias,
    norm1_gain,
    norm1_shift,
    up_weight,
    up_bias,
    down_weight,
    down_bias,
    norm2_gain,
    norm2_shift,
    doc_mask,
    doc_blocks,
    rand_blocks,
    out_grad,
):
    tok_dev = hidden_in.shape[0]
    local_width = q_weight.shape[1]
    local_heads = local_width // HD
    share_rows = out_grad.shape[0]
    slot_span = SLOT_LEN // tok_dev
    group_bits = slot_span.bit_length() - 1
    seq_index = lax.axis_index("seq")
    head_index = lax.axis_index("head")
    slot_place = seq_index % slot_span
    slot_index = seq_index // slot_span
    local_blocks = tok_dev // BLOCK
    slot_blocks = SLOT_LEN // BLOCK
    key_window = 8 * BLOCK
    head_rows = 2 * BLOCK
    scale = HD ** (-0.5)
    query = (jnp.dot(hidden_in, q_weight, preferred_element_type=jnp.float32) + q_bias).astype(
        jnp.bfloat16
    )
    key_rows = jnp.dot(hidden_in, k_weight, preferred_element_type=jnp.float32).astype(jnp.bfloat16)
    value_rows = (jnp.dot(hidden_in, v_weight, preferred_element_type=jnp.float32) + v_bias).astype(
        jnp.bfloat16
    )
    own_pair = jnp.concatenate([key_rows, value_rows], axis=1)
    slot_pair = own_pair
    for bit_index in range(group_bits):
        partner = partner_2(slot_pair, "seq", bit_index)
        upper_half = seq_index // 2**bit_index % 2 == 1
        slot_pair = jnp.where(
            upper_half,
            jnp.concatenate([partner, slot_pair], axis=0),
            jnp.concatenate([slot_pair, partner], axis=0),
        )
    slot_mask = lax.dynamic_slice_in_dim(doc_mask, slot_index * SLOT_LEN, SLOT_LEN, 0)
    doc_count = doc_blocks[slot_index]
    positions = jnp.arange(SLOT_LEN, dtype=jnp.int32)
    key_valid = (slot_mask == 1) & (positions // BLOCK < doc_count)
    query_block = slot_place * local_blocks + jnp.arange(local_blocks, dtype=jnp.int32)
    near = query_block[:, None] + jnp.arange(-1, 2, dtype=jnp.int32)[None, :]
    near_valid = (near >= 2) & (near < slot_blocks)
    near_clip = jnp.clip(near, 0, slot_blocks - 1)
    global_ids = jnp.zeros((local_blocks, 2), jnp.int32) + jnp.arange(2, dtype=jnp.int32)[None, :]
    block_ids = jnp.concatenate([near_clip, rand_blocks, global_ids], axis=1)
    block_valid = jnp.concatenate([near_valid, jnp.ones((local_blocks, 5), dtype=bool)], axis=1)
    sparse_valid = (
        key_valid.reshape(slot_blocks, BLOCK)[block_ids] & block_valid[:, :, None]
    ).reshape(local_blocks, key_window)
    picked = slot_pair.reshape(slot_blocks, BLOCK, 2 * local_width)[block_ids].reshape(
        local_blocks, key_window, 2 * local_width
    )
    picked_keys = picked[:, :, :local_width].reshape(local_blocks, key_window, local_heads, HD)
    picked_values = picked[:, :, local_width:].reshape(local_blocks, key_window, local_heads, HD)
    query_blocks = query.reshape(local_blocks, BLOCK, local_heads, HD)
    slot_keys = slot_pair[:, :local_width].reshape(SLOT_LEN, local_heads, HD)
    slot_values = slot_pair[:, local_width:].reshape(SLOT_LEN, local_heads, HD)
    head_query = query[:head_rows].reshape(head_rows, local_heads, HD)

    def sparse_scores():
        raw = (
            jnp.einsum(
                "nqhd,nkhd->nhqk", query_blocks, picked_keys, preferred_element_type=jnp.float32
            )
            * scale
        )
        return jnp.where(sparse_valid[:, None, None, :], raw, NEG)

    def global_scores():
        raw = (
            jnp.einsum("qhd,khd->hqk", head_query, slot_keys, preferred_element_type=jnp.float32)
            * scale
        )
        return jnp.where(key_valid[None, None, :], raw, NEG)

    probs, sparse_lse = softmax_rows(sparse_scores())
    sparse_ctx = jnp.einsum(
        "nhqk,nkhd->nqhd",
        probs.astype(jnp.bfloat16),
        picked_values,
        preferred_element_type=jnp.float32,
    )
    global_probs, global_lse = softmax_rows(global_scores())
    global_ctx = jnp.einsum(
        "hqk,khd->qhd",
        global_probs.astype(jnp.bfloat16),
        slot_values,
        preferred_element_type=jnp.float32,
    )
    is_first = slot_place == 0
    context = sparse_ctx.reshape(tok_dev, local_width)
    context = jnp.concatenate(
        [
            jnp.where(is_first, global_ctx.reshape(head_rows, local_width), context[:head_rows]),
            context[head_rows:],
        ],
        axis=0,
    )
    context_low = context.astype(jnp.bfloat16)
    attn_share = lax.psum_scatter(
        jnp.dot(context_low, o_weight, preferred_element_type=jnp.float32).astype(jnp.bfloat16),
        "head",
        scatter_dimension=0,
        tiled=True,
    ).astype(jnp.float32)
    token_share = lax.dynamic_slice_in_dim(
        hidden_in, head_index * share_rows, share_rows, 0
    ).astype(jnp.float32)
    first_sum = token_share + attn_share + o_bias
    normed_one, unit_one, inv_one = norm_forward(first_sum, norm1_gain, norm1_shift)
    normed_low = normed_one.astype(jnp.bfloat16)
    up_full, up_bias_full, down_full = (
        lax.all_gather(up_weight, "head", axis=1, tiled=True),
        lax.all_gather(up_bias.astype(jnp.bfloat16), "head", axis=0, tiled=True).astype(
            up_bias.dtype
        ),
        lax.all_gather(down_weight, "head", axis=0, tiled=True),
    )
    pre_act = jnp.dot(normed_low, up_full, preferred_element_type=jnp.float32) + up_bias_full
    act_low = jax.nn.gelu(pre_act, approximate=True).astype(jnp.bfloat16)
    ffn_share = jnp.dot(act_low, down_full, preferred_element_type=jnp.float32)
    second_sum = normed_one + ffn_share + down_bias
    layer_out, unit_two, inv_two = norm_forward(second_sum, norm2_gain, norm2_shift)
    second_grad, gain_two_grad, shift_two_grad = norm_backward(
        out_grad, unit_two, inv_two, norm2_gain
    )
    down_bias_grad = jnp.sum(second_grad, axis=0)
    second_low = second_grad.astype(jnp.bfloat16)
    down_grad_full = contract_rows(act_low, second_low)
    pre_grad = gelu_grad(pre_act, contract_cols(second_low, down_full))
    up_bias_full_grad = jnp.sum(pre_grad.astype(jnp.float32), axis=0)
    up_grad_full = contract_rows(normed_low, pre_grad)
    branch_grad = contract_cols(pre_grad, up_full)
    up_grad, up_bias_grad, down_grad = (
        lax.psum_scatter(
            up_grad_full.astype(jnp.bfloat16), "head", scatter_dimension=1, tiled=True
        ).astype(jnp.float32),
        lax.psum_scatter(
            up_bias_full_grad.astype(jnp.bfloat16), "head", scatter_dimension=0, tiled=True
        ).astype(jnp.float32),
        lax.psum_scatter(
            down_grad_full.astype(jnp.bfloat16), "head", scatter_dimension=0, tiled=True
        ).astype(jnp.float32),
    )
    first_grad, gain_one_grad, shift_one_grad = norm_backward(
        second_grad + branch_grad, unit_one, inv_one, norm1_gain
    )
    o_bias_grad = jnp.sum(first_grad, axis=0)
    first_full = lax.all_gather(first_grad.astype(jnp.bfloat16), "head", axis=0, tiled=True)
    o_grad = contract_rows(context_low, first_full)
    context_grad = contract_cols(first_full, o_weight).astype(jnp.bfloat16)
    keep_blocks = jnp.logical_not(is_first & (jnp.arange(local_blocks) < 2))
    out_blocks = jnp.where(
        keep_blocks[:, None, None, None],
        context_grad.reshape(local_blocks, BLOCK, local_heads, HD),
        jnp.zeros((), jnp.bfloat16),
    )
    probs = jnp.exp(sparse_scores() - sparse_lse)
    prob_grad = jnp.einsum(
        "nqhd,nkhd->nhqk", out_blocks, picked_values, preferred_element_type=jnp.float32
    )
    row_dot = jnp.sum(prob_grad * probs, axis=-1, keepdims=True)
    score_grad = (probs * (prob_grad - row_dot)).astype(jnp.bfloat16)
    query_grad = (
        jnp.einsum("nhqk,nkhd->nqhd", score_grad, picked_keys, preferred_element_type=jnp.float32)
        * scale
    )
    key_part = (
        jnp.einsum("nhqk,nqhd->nkhd", score_grad, query_blocks, preferred_element_type=jnp.float32)
        * scale
    )
    value_part = jnp.einsum(
        "nhqk,nqhd->nkhd",
        probs.astype(jnp.bfloat16),
        out_blocks,
        preferred_element_type=jnp.float32,
    )
    pair_part = jnp.concatenate(
        [
            key_part.reshape(local_blocks, 8, BLOCK, local_width),
            value_part.reshape(local_blocks, 8, BLOCK, local_width),
        ],
        axis=-1,
    )
    slot_grad = (
        jnp.zeros((slot_blocks, BLOCK, 2 * local_width), jnp.float32).at[block_ids].add(pair_part)
    )
    head_out = jnp.where(is_first, context_grad[:head_rows], jnp.zeros((), jnp.bfloat16)).reshape(
        head_rows, local_heads, HD
    )
    global_probs = jnp.exp(global_scores() - global_lse)
    global_prob_grad = jnp.einsum(
        "qhd,khd->hqk", head_out, slot_values, preferred_element_type=jnp.float32
    )
    global_dot = jnp.sum(global_prob_grad * global_probs, axis=-1, keepdims=True)
    global_score_grad = (global_probs * (global_prob_grad - global_dot)).astype(jnp.bfloat16)
    head_query_grad = (
        jnp.einsum("hqk,khd->qhd", global_score_grad, slot_keys, preferred_element_type=jnp.float32)
        * scale
    )
    slot_key_grad = (
        jnp.einsum(
            "hqk,qhd->khd", global_score_grad, head_query, preferred_element_type=jnp.float32
        )
        * scale
    )
    slot_value_grad = jnp.einsum(
        "hqk,qhd->khd",
        global_probs.astype(jnp.bfloat16),
        head_out,
        preferred_element_type=jnp.float32,
    )
    slot_grad = slot_grad.reshape(SLOT_LEN, 2 * local_width) + jnp.concatenate(
        [
            slot_key_grad.reshape(SLOT_LEN, local_width),
            slot_value_grad.reshape(SLOT_LEN, local_width),
        ],
        axis=1,
    )
    query_grad = query_grad.reshape(tok_dev, local_width)
    query_grad = jnp.concatenate(
        [
            query_grad[:head_rows] + head_query_grad.reshape(head_rows, local_width),
            query_grad[head_rows:],
        ],
        axis=0,
    )
    own_grad = slot_grad
    for bit_index in reversed(range(group_bits)):
        half_len = own_grad.shape[0] // 2
        upper_half = seq_index // 2**bit_index % 2 == 1
        lower_part = own_grad[:half_len]
        upper_part = own_grad[half_len:]
        kept_half = jnp.where(upper_half, upper_part, lower_part)
        given_half = jnp.where(upper_half, lower_part, upper_part)
        own_grad = kept_half + partner_2(given_half.astype(jnp.bfloat16), "seq", bit_index).astype(
            given_half.dtype
        )
    query_low = query_grad.astype(jnp.bfloat16)
    key_low = own_grad[:, :local_width].astype(jnp.bfloat16)
    value_low = own_grad[:, local_width:].astype(jnp.bfloat16)
    q_grad = contract_rows(hidden_in, query_low)
    q_bias_grad = jnp.sum(query_low.astype(jnp.float32), axis=0)
    k_grad = contract_rows(hidden_in, key_low)
    v_grad = contract_rows(hidden_in, value_low)
    v_bias_grad = jnp.sum(value_low.astype(jnp.float32), axis=0)
    in_grad = first_grad + lax.psum_scatter(
        (
            contract_cols(query_low, q_weight)
            + contract_cols(key_low, k_weight)
            + contract_cols(value_low, v_weight)
        ).astype(jnp.bfloat16),
        "head",
        scatter_dimension=0,
        tiled=True,
    ).astype(jnp.float32)
    summed = lax.psum(
        (
            q_grad,
            q_bias_grad,
            k_grad,
            v_grad,
            v_bias_grad,
            o_grad,
            up_grad,
            up_bias_grad,
            down_grad,
        ),
        "seq",
    )
    norm_sums = lax.psum(
        (o_bias_grad, gain_one_grad, shift_one_grad, down_bias_grad, gain_two_grad, shift_two_grad),
        ("seq", "head"),
    )
    return (
        layer_out,
        in_grad,
        summed[0],
        summed[1],
        summed[2],
        summed[3],
        summed[4],
        summed[5],
        norm_sums[0],
        norm_sums[1],
        norm_sums[2],
        summed[6],
        summed[7],
        summed[8],
        norm_sums[3],
        norm_sums[4],
        norm_sums[5],
    )


def solution(mesh):
    in_specs = (
        P("seq", None),
        P(None, "head"),
        P("head"),
        P(None, "head"),
        P(None, "head"),
        P("head"),
        P("head", None),
        P(),
        P(),
        P(),
        P(None, "head"),
        P("head"),
        P("head", None),
        P(),
        P(),
        P(),
        P(),
        P(),
        P("seq", None),
        P(("seq", "head"), None),
    )
    out_specs = (
        P(("seq", "head"), None),
        P(("seq", "head"), None),
        P(None, "head"),
        P("head"),
        P(None, "head"),
        P(None, "head"),
        P("head"),
        P("head", None),
        P(),
        P(),
        P(),
        P(None, "head"),
        P("head"),
        P("head", None),
        P(),
        P(),
        P(),
    )
    return jax.shard_map(
        per_device, mesh=mesh, in_specs=in_specs, out_specs=out_specs, check_vma=False
    )
```

profile of v0, /device:TPU:0, one launch (start us, length us, event | category | flops | bytes accessed | tf_op | source)
XLA Modules:
  0.0 839.4 jit_solution(10411404737990984709)
XLA Ops:
  15.5 17.7 %collective-permute-done = bf16[1024,384]{0,1:T(8,128)(2,1)} collective-permute-done((bf16[1024,384]{0,1:T(8,128)(2,1)S(1)}, bf16[1024,384]{0,1:T(8,128)(2,1)}, u32[]{:S(2)}, u32[]{:S(2)}) %collective-permute-start) | collective-permute-done | bytes 786464 | tf_op jit(solution)/shard_map/ppermute | solution.py:18
  45.8 25.7 %collective-permute-done.1 = bf16[2048,384]{0,1:T(8,128)(2,1)} collective-permute-done((bf16[2048,384]{0,1:T(8,128)(2,1)S(1)}, bf16[2048,384]{0,1:T(8,128)(2,1)}, u32[]{:S(2)}, u32[]{:S(2)}) %collective-permute-start.1) | collective-permute-done | bytes 1572896 | tf_op jit(solution)/shard_map/ppermute | solution.py:18
  80.1 5.9 gather_fusion
  86.0 6.6 fusion.61
  97.5 6.7 copy.65
  128.8 22.6 %reduce-scatter.5.cloned.1.call-done = bf16[256,768]{1,0:T(8,128)(2,1)} async-done(((bf16[1024,768]{1,0:T(8,128)(2,1)}), bf16[256,768]{1,0:T(8,128)(2,1)}) %reduce-scatter.5.cloned.1.call-update) | async-done | bytes 393232 | tf_op jit(solution)/shard_map/reduce_scatter | solution.py:183
  153.9 36.5 %all-gather.5.cloned.1.call-done = bf16[768,3072]{1,0:T(8,128)(2,1)} async-done(((bf16[768,768]{1,0:T(8,128)(2,1)}), bf16[768,3072]{1,0:T(8,128)(2,1)}) %all-gather.5.cloned.1.call-update) | async-done | bytes 4718608 | tf_op jit(solution)/shard_map/all_gather | solution.py:196
  196.2 33.3 %all-gather.7.cloned.1.call-done = bf16[3072,768]{1,0:T(8,128)(2,1)} async-done(((bf16[768,768]{1,0:T(8,128)(2,1)}), bf16[3072,768]{1,0:T(8,128)(2,1)}) %all-gather.7.cloned.1.call-update) | async-done | bytes 4718608 | tf_op jit(solution)/shard_map/all_gather | solution.py:200
  247.0 19.7 %all-gather.9.cloned.1.call-done = bf16[1024,768]{1,0:T(8,128)(2,1)} async-done(((bf16[256,768]{1,0:T(8,128)(2,1)}), bf16[1024,768]{1,0:T(8,128)(2,1)}) %all-gather.9.cloned.1.call-update) | async-done | bytes 1572880 | tf_op jit(solution)/shard_map/all_gather | solution.py:232
  271.4 8.7 %multiply_reduce_fusion.1 = (f32[16,3,64]{2,1,0:T(4,128)S(1)}, f32[16,3,64,512]{3,2,1,0:T(8,128)}) fusion(f32[16,3,64,512]{3,2,1,0:T(8,128)} %copy-done.3, f32[16,3,64]{2,1,0:T(4,128)S(1)} %log_add_fusion, bf16[16,512,3,64]{1,3,2,0:T(8,128)(2,1)} %bitcast.123, bf16[16,64,3,64]{1,0,3,2:T(8,128)(2,1)S(1)} %reshape.367, pred[16]{0:T(512)(128)(4,1)S(1)} %and_not_fusion), kind=kOutput, calls=%fused_computation.10 | convolution fusion | flops 206238720 | bytes 16146448 | tf_op jit(solution)/shard_map/nqhd,nkhd->nhqk/dot_general | solution.py:242
  280.1 6.6 fusion.19
  318.0 10.3 %reshape.370 = f32[16,8,64,192]{2,1,3,0:T(8,128)} reshape(f32[16,512,3,64]{1,3,2,0:T(8,128)} %multiply_bitcast_fusion) | data formatting | bytes 12582912 | tf_op jit(solution)/shard_map/reshape | solution.py:263
  328.3 10.5 %reshape.371 = f32[16,8,64,192]{2,1,3,0:T(8,128)} reshape(f32[16,512,3,64]{1,3,2,0:T(8,128)} %fusion.19) | data formatting | bytes 12582912 | tf_op jit(solution)/shard_map/reshape | solution.py:264
  338.8 18.3 %pad_maximum_fusion = f32[16,8,64,384]{2,1,3,0:T(8,128)} fusion(f32[16,8,64,192]{2,1,3,0:T(8,128)} %reshape.371, f32[16,8,64,192]{2,1,3,0:T(8,128)} %reshape.370), kind=kLoop, calls=%fused_computation.3 | loop fusion | flops 3145728 | bytes 25165824 | tf_op jit(solution)/shard_map/concatenate | solution.py:261
  357.1 18.7 %copy.76 = f32[16,8,64,384]{3,2,1,0:T(8,128)} copy(f32[16,8,64,384]{2,1,3,0:T(8,128)} %pad_maximum_fusion) | data formatting | bytes 25165824 | tf_op jit(solution)/shard_map/concatenate | solution.py:261
  379.3 31.8 %scatter_fusion = f32[64,64,384]{2,1,0:T(8,128)} fusion(f32[64,64,384]{2,1,0:T(8,128)} %broadcast_in_dim.52, s32[128]{0:T(128)S(1)} %reshape.377, f32[128,64,384]{2,1,0:T(8,128)} %bitcast.113), kind=kCustom, calls=%fused_computation.2 | custom fusion | flops 3145728 | bytes 37749248 | tf_op jit(solution)/shard_map/scatter-add | solution.py:269
  411.0 6.5 maximum_add_fusion
  426.1 29.8 %collective-permute-done.2 = bf16[2048,384]{1,0:T(8,128)(2,1)} collective-permute-done((bf16[2048,384]{1,0:T(8,128)(2,1)}, bf16[2048,384]{1,0:T(8,128)(2,1)}, u32[]{:S(2)}, u32[]{:S(2)}) %collective-permute-start.2) | collective-permute-done | bytes 1572896 | tf_op jit(solution)/shard_map/ppermute | solution.py:18
  463.3 15.4 %collective-permute-done.3 = bf16[1024,384]{1,0:T(8,128)(2,1)S(1)} collective-permute-done((bf16[1024,384]{1,0:T(8,128)(2,1)S(1)}, bf16[1024,384]{1,0:T(8,128)(2,1)S(1)}, u32[]{:S(2)}, u32[]{:S(2)}) %collective-permute-start.3) | collective-permute-done | bytes 786464 | tf_op jit(solution)/shard_map/ppermute | solution.py:18
  482.1 6.3 convolution_convert_fusion
  503.6 40.7 %all-reduce.2 = (f32[768]{0:T(1024)}, f32[768]{0:T(1024)}, f32[768]{0:T(1024)}, f32[768]{0:T(1024)}, f32[768]{0:T(1024)}, /*index=5*/f32[768]{0:T(1024)}) all-reduce(f32[768]{0:T(1024)S(1)} %copy-done.52, f32[768]{0:T(1024)S(1)} %copy-done.58, f32[768]{0:T(1024)S(1)} %copy-done.59, ...), channel_id=1, replica_groups=mesh['seq'=8,'head'=4] {'seq','head'}, use_global_device_ids=true, to_apply=%region_26.27 | all-reduce | flops 4608 | bytes 36864 | tf_op jit(solution)/shard_map/psum | solution.py:354
  544.2 7.9 all-reduce.1
  561.5 50.3 %reduce-scatter.9.cloned.1.call-done = bf16[768,768]{1,0:T(8,128)(2,1)} async-done(((bf16[768,3072]{1,0:T(8,128)(2,1)}), bf16[768,768]{1,0:T(8,128)(2,1)}) %reduce-scatter.9.cloned.1.call-update) | async-done | bytes 1179664 | tf_op jit(solution)/shard_map/reduce_scatter | solution.py:218
  611.8 213.7 %all-reduce.9 = (f32[192]{0:T(256)}, f32[192]{0:T(256)}, f32[768,768]{1,0:T(8,128)}, f32[768]{0:T(1024)}, f32[768,768]{1,0:T(8,128)}) all-reduce(f32[192]{0:T(256)S(1)} %convert_reduce_fusion.1, f32[192]{0:T(256)S(1)} %convert_reduce_fusion, ...), channel_id=1, replica_groups=mesh['seq'=8,'head'=4] {'seq'}, use_global_device_ids=true, to_apply=%region_19.20 | all-reduce | flops 1180800 | bytes 7087104 | tf_op jit(solution)/shard_map/psum | solution.py:340
  (286 shorter events, 173.0 us)
Async XLA Ops:
  7.2 112.9 %copy-start = (bf16[192,768]{1,0:T(8,128)(2,1)S(1)}, bf16[192,768]{1,0:T(8,128)(2,1)}, u32[]{:S(2)}) copy-start(bf16[192,768]{1,0:T(8,128)(2,1)} %param.26) | copy-start | bytes 884740
  7.2 144.2 %reduce-scatter.5.cloned.1.call-start = ((), (), s32[]{:S(2)}) async-start(), calls=%async_computation.4 | async-start | bytes 1966080 | tf_op jit(solution)/shard_map/reduce_scatter | solution.py:183
  12.5 20.6 %collective-permute-start = (bf16[1024,384]{0,1:T(8,128)(2,1)S(1)}, bf16[1024,384]{0,1:T(8,128)(2,1)}, u32[]{:S(2)}, u32[]{:S(2)}) collective-permute-start(bf16[1024,384]{0,1:T(8,128)(2,1)S(1)} %pad_maximum_fusion.1), channel_id=1, source_target_pairs={{0,4},{4,0},{8,12},{12,8},{16,20},{20,16},{24,28},{28,24},{1,5},{5... | collective-permute-start | bytes 2359304 | tf_op jit(solution)/shard_map/ppermute | solution.py:18
  35.7 35.7 %collective-permute-start.1 = (bf16[2048,384]{0,1:T(8,128)(2,1)S(1)}, bf16[2048,384]{0,1:T(8,128)(2,1)}, u32[]{:S(2)}, u32[]{:S(2)}) collective-permute-start(bf16[2048,384]{0,1:T(8,128)(2,1)S(1)} %maximum_select_fusion.1), channel_id=1, source_target_pairs={{0,8},{4,12},{8,0},{12,4},{16,24},{20,28},{24,16},{28,20},{1,9},{5... | collective-permute-start | bytes 4718600 | tf_op jit(solution)/shard_map/ppermute | solution.py:18
  122.0 68.5 %copy-start.44 = (f32[768]{0:T(1024)S(1)}, f32[768]{0:T(1024)}, u32[]{:S(2)}) copy-start(f32[768]{0:T(1024)} %param.28) | copy-start | bytes 9220
  122.0 68.5 %copy-start.45 = (f32[768]{0:T(1024)S(1)}, f32[768]{0:T(1024)}, u32[]{:S(2)}) copy-start(f32[768]{0:T(1024)} %param.29) | copy-start | bytes 9220
  122.0 68.5 %all-gather.5.cloned.1.call-start = ((), (), s32[]{:S(2)}) async-start(), calls=%async_computation.5 | async-start | bytes 5898240 | tf_op jit(solution)/shard_map/all_gather | solution.py:196
  122.7 106.7 %all-gather.7.cloned.1.call-start = ((), (), s32[]{:S(2)}) async-start(), calls=%async_computation.6 | async-start | bytes 5898240 | tf_op jit(solution)/shard_map/all_gather | solution.py:200
  123.5 143.2 %all-gather.9.cloned.1.call-start = ((), (), s32[]{:S(2)}) async-start(), calls=%async_computation.7 | async-start | bytes 1966080 | tf_op jit(solution)/shard_map/all_gather | solution.py:232
  152.6 91.5 %copy-start.46 = (f32[256]{0:T(256)}, f32[256]{0:T(256)S(1)}, u32[]{:S(2)}) copy-start(f32[256]{0:T(256)S(1)} %broadcast_multiply_fusion.5) | copy-start | bytes 3076
  153.9 90.2 %copy-start.53 = (f32[256]{0:T(256)}, f32[256]{0:T(256)S(1)}, u32[]{:S(2)}) copy-start(f32[256]{0:T(256)S(1)} %add_rsqrt_fusion.1) | copy-start | bytes 3076
  196.1 39.1 %copy-start.25 = (f32[256,768]{1,0:T(8,128)S(1)}, f32[256,768]{1,0:T(8,128)}, u32[]{:S(2)}) copy-start(f32[256,768]{1,0:T(8,128)} %param.39) | copy-start | bytes 2359300
  196.2 39.1 %copy-start.48 = (f32[768]{0:T(1024)S(1)}, f32[768]{0:T(1024)}, u32[]{:S(2)}) copy-start(f32[768]{0:T(1024)} %param.34) | copy-start | bytes 9220
  196.2 40.1 %copy-start.56 = (f32[768]{0:T(1024)S(1)}, f32[768]{0:T(1024)}, u32[]{:S(2)}) copy-start(f32[768]{0:T(1024)} %param.35) | copy-start | bytes 9220
  246.8 306.8 %reduce-scatter.7.cloned.1.call-start = ((), (), s32[]{:S(2)}) async-start(), calls=%async_computation.8 | async-start | bytes 1966080 | tf_op jit(solution)/shard_map/reduce_scatter | solution.py:330
  419.1 36.8 %collective-permute-start.2 = (bf16[2048,384]{1,0:T(8,128)(2,1)}, bf16[2048,384]{1,0:T(8,128)(2,1)}, u32[]{:S(2)}, u32[]{:S(2)}) collective-permute-start(bf16[2048,384]{1,0:T(8,128)(2,1)} %select_convert_fusion), channel_id=1, source_target_pairs={{0,8},{4,12},{8,0},{12,4},{16,24},{20,28},{24,16},{28,20},{1,9},{5... | collective-permute-start | bytes 4718600 | tf_op jit(solution)/shard_map/ppermute | solution.py:18
  426.1 69.3 %copy-start.24 = (bf16[896,192]{0,1:T(8,128)(2,1)}, bf16[896,192]{0,1:T(8,128)(2,1)S(1)}, u32[]{:S(2)}) copy-start(bf16[896,192]{0,1:T(8,128)(2,1)S(1)} %slice.77) | copy-start | bytes 1032196
  459.8 18.9 %collective-permute-start.3 = (bf16[1024,384]{1,0:T(8,128)(2,1)S(1)}, bf16[1024,384]{1,0:T(8,128)(2,1)S(1)}, u32[]{:S(2)}, u32[]{:S(2)}) collective-permute-start(bf16[1024,384]{1,0:T(8,128)(2,1)S(1)} %select_convert_fusion.1), channel_id=1, source_target_pairs={{0,4},{4,0},{8,12},{12,8},{16,20},{20,16},{24,28},{28,24},{1,5},{5... | collective-permute-start | bytes 2359304 | tf_op jit(solution)/shard_map/ppermute | solution.py:18
  481.8 79.7 %reduce-scatter.11.cloned.1.call-start = ((), (), s32[]{:S(2)}) async-start(), calls=%async_computation.10 | async-start | bytes 5898240 | tf_op jit(solution)/shard_map/reduce_scatter | solution.py:224
  488.4 123.4 %reduce-scatter.9.cloned.1.call-start = ((), (), s32[]{:S(2)}) async-start(), calls=%async_computation.9 | async-start | bytes 5898240 | tf_op jit(solution)/shard_map/reduce_scatter | solution.py:218
  495.3 330.2 %all-reduce.8.cloned.1.call-start = ((), (), s32[]{:S(2)}) async-start(), calls=%async_computation.11 | async-start | bytes 4718592 | tf_op jit(solution)/shard_map/psum | solution.py:340
  500.9 43.3 %copy-start.55 = (bf16[3072]{0:T(1024)(128)(2,1)S(1)}, bf16[3072]{0:T(1024)(128)(2,1)}, u32[]{:S(2)}) copy-start(bf16[3072]{0:T(1024)(128)(2,1)} %get-tuple-element.60) | copy-start | bytes 18436
  500.9 52.8 %copy-start.20 = (f32[256,768]{1,0:T(8,128)S(1)}, f32[256,768]{1,0:T(8,128)}, u32[]{:S(2)}) copy-start(f32[256,768]{1,0:T(8,128)} %copy-done.19) | copy-start | bytes 2359300
  553.7 278.4 %copy-start.1 = (bf16[192,768]{1,0:T(8,128)(2,1)S(1)}, bf16[192,768]{1,0:T(8,128)(2,1)}, u32[]{:S(2)}) copy-start(bf16[192,768]{1,0:T(8,128)(2,1)} %param.26) | copy-start | bytes 884740
  (63 other events, 564.4 us)
Sparse Core Ops, SparseCore 0:
  122.1 29.2 reduce-scatter.4
  153.0 37.4 all-gather.4
  192.0 37.4 all-gather.6
  247.0 19.6 all-gather.8
  481.9 28.0 reduce-scatter.6
  512.4 49.0 reduce-scatter.10
  564.0 47.7 reduce-scatter.8
  616.3 172.8 all-reduce.7
where the time goes:
time: 848 us; the launch traced here: 839 us
  blocking collectives  267 us (31%)
  waiting for transfers between devices  258 us (30%)
  local copies, waits for them, and re-layouts  110 us (13%)
  other arithmetic  91.3 us (11%)
  matrix products  87.1 us (10%)
  between operations  16.3 us (2%)
  starting transfers between devices  8.72 us (1%)
    psum x1, blocking collectives, per_device(): lax.psum((q_grad, q_bias_grad, k_grad, v_grad, v_bias_grad, o_grad, up_gr...  214 us
    ppermute x4, waiting for transfers between devices, partner_2(): return lax.ppermute(value, axis, pairs)  88.5 us
    reduce_scatter x1, waiting for transfers between devices, per_device(): lax.psum_scatter(up_grad_full.astype(jnp.bfloat16), 'head', scatter_dimen...  50.3 us
    psum x1, blocking collectives, per_device(): lax.psum((o_bias_grad, gain_one_grad, shift_one_grad, down_bias_grad, gai...  40.7 us
    all_gather x1, waiting for transfers between devices, per_device(): lax.all_gather(up_weight, 'head', axis=1, tiled=True)  36.5 us
    all_gather x1, waiting for transfers between devices, per_device(): lax.all_gather(down_weight, 'head', axis=0, tiled=True)  33.3 us
    scatter-add x1, other arithmetic, per_device(): jnp.zeros((slot_blocks, BLOCK, 2 * local_width), jnp.float32).at[block_ids]  31.8 us
    reduce_scatter x1, waiting for transfers between devices, per_device(): lax.psum_scatter(jnp.dot(context_low, o_weight, preferred_element_type=jn...  22.6 us
  transfers between devices with their start and end apart: 12, of which 10 were waited for; matrix products, arithmetic and copies ran while one was open for 5% of the time, Pallas kernels for 0%

commit v1 on v0

v1 whole, which is shorter than its diff:
```python
import jax
import jax.numpy as jnp
from jax import lax
from jax.experimental import pallas as pl
from jax.experimental.pallas import tpu as pltpu
from jax.sharding import PartitionSpec as P

HD = 64
BLOCK = 64
SLOT_LEN = 4096
NEG = -1e30
EPS = 1e-12
WIN = 8


def dot_nt(left, right):
    return lax.dot_general(left, right, (((1,), (1,)), ((), ())), preferred_element_type=jnp.float32)


def dot_tn(left, right):
    return lax.dot_general(left, right, (((0,), (0,)), ((), ())), preferred_element_type=jnp.float32)


def dot_nn(left, right):
    return jnp.dot(left, right, preferred_element_type=jnp.float32)


def head_pick(rows, first):
    lane = lax.broadcasted_iota(jnp.int32, (1, rows.shape[1]), 1) // HD
    return [jnp.where(lane == first + head, rows, jnp.zeros_like(rows)) for head in range(3)]


def spread_heads(rows, first):
    return jnp.concatenate(head_pick(rows, first), axis=0)


def fold_heads(stacked, first):
    size = stacked.shape[0] // 3
    lane = lax.broadcasted_iota(jnp.int32, (1, stacked.shape[1]), 1) // HD
    total = None
    for head in range(3):
        part = jnp.where(lane == first + head, stacked[head * size : (head + 1) * size], 0.0)
        total = part if total is None else total + part
    return total


def window_ids(scal_ref, rand_ref, step, local_blocks):
    place, count = scal_ref[0], scal_ref[1]
    mine = place * local_blocks + step
    last = SLOT_LEN // BLOCK - 1
    ids, limits = [], []
    for shift in (-1, 0, 1):
        near = mine + shift
        good = (near >= 2) & (near <= last)
        at = jnp.clip(near, 0, last)
        ids.append(at)
        limits.append(jnp.where(good, jnp.clip(count - at * BLOCK, 0, BLOCK), 0))
    for slot in range(3):
        at = rand_ref[step * 3 + slot]
        ids.append(at)
        limits.append(jnp.clip(count - at * BLOCK, 0, BLOCK))
    for at in (0, 1):
        ids.append(jnp.int32(at))
        limits.append(jnp.clip(count - at * BLOCK, 0, BLOCK))
    return ids, limits


def take_blocks(ref, ids, low):
    parts = [ref[pl.ds(pl.multiple_of(at * BLOCK, BLOCK), BLOCK), low : low + 256] for at in ids]
    return jnp.concatenate(parts, axis=0)


def attend_fwd_kernel(scal_ref, rand_ref, q_ref, kv_ref, ctx_ref, p_ref, pg_ref, wide_ref):
    local_blocks = q_ref.shape[0] // BLOCK
    place, count = scal_ref[0], scal_ref[1]
    half = lax.broadcasted_iota(jnp.int32, (1, 128), 1)

    def one_block(step):
        ids, limits = window_ids(scal_ref, rand_ref, step, local_blocks)
        rows = pl.ds(pl.multiple_of(step * BLOCK, BLOCK), BLOCK)
        q_all = spread_heads(q_ref[rows, :], 0)
        raw = dot_nt(q_all, take_blocks(kv_ref, ids, 0))
        cut = jnp.concatenate(
            [jnp.where(half < BLOCK, limits[2 * t], limits[2 * t + 1]) for t in range(WIN // 2)], axis=1
        )
        inside = lax.broadcasted_iota(jnp.int32, (1, WIN * BLOCK), 1) % BLOCK
        raw = jnp.where(inside < cut, raw, NEG)
        expo = jnp.exp(raw - jnp.max(raw, axis=1, keepdims=True))
        probs = (expo * (1.0 / jnp.sum(expo, axis=1, keepdims=True))).astype(jnp.bfloat16)
        p_ref[step] = probs
        out = dot_nn(probs, take_blocks(kv_ref, ids, 128))
        ctx_ref[rows, :] = fold_heads(out, 1).astype(jnp.bfloat16)

    @pl.when(place == 0)
    def _():
        q_all = spread_heads(q_ref[0 : 2 * BLOCK, :], 0)
        chunk = WIN * BLOCK
        rows_all = q_all.shape[0]

        def scan_scores(part, top):
            at = pl.multiple_of(part * chunk, chunk)
            raw = dot_nt(q_all, kv_ref[pl.ds(at, chunk), 0:256])
            where_at = at + lax.broadcasted_iota(jnp.int32, (1, chunk), 1)
            raw = jnp.where(where_at < count, raw, NEG)
            wide_ref[part] = raw
            return jnp.maximum(top, jnp.max(raw, axis=1, keepdims=True))

        parts = SLOT_LEN // chunk
        top = lax.fori_loop(0, parts, scan_scores, jnp.full((rows_all, 1), NEG, jnp.float32))

        def scan_sum(part, total):
            expo = jnp.exp(wide_ref[part] - top)
            wide_ref[part] = expo
            return total + jnp.sum(expo, axis=1, keepdims=True)

        total = lax.fori_loop(0, parts, scan_sum, jnp.zeros((rows_all, 1), jnp.float32))
        inv = 1.0 / total

        def scan_out(part, out):
            probs = (wide_ref[part] * inv).astype(jnp.bfloat16)
            pg_ref[part] = probs
            at = pl.multiple_of(part * chunk, chunk)
            return out + dot_nn(probs, kv_ref[pl.ds(at, chunk), 128:384])

        out = lax.fori_loop(0, parts, scan_out, jnp.zeros((rows_all, 256), jnp.float32))
        ctx_ref[0 : 2 * BLOCK, :] = fold_heads(out, 1).astype(jnp.bfloat16)

    def pair(at, carry):
        one_block(2 * at)
        one_block(2 * at + 1)
        return carry

    lax.fori_loop(jnp.where(place == 0, 1, 0), local_blocks // 2, pair, 0)


def attend_forward(scal, rand, q_rows, kv_slot):
    tokens = q_rows.shape[0]
    blocks = tokens // BLOCK
    vmem = pl.BlockSpec(memory_space=pltpu.VMEM)
    smem = pl.BlockSpec(memory_space=pltpu.SMEM)
    return pl.pallas_call(
        attend_fwd_kernel,
        name="attend_forward",
        out_shape=(
            jax.ShapeDtypeStruct((tokens, 256), jnp.bfloat16),
            jax.ShapeDtypeStruct((blocks, 3 * BLOCK, WIN * BLOCK), jnp.bfloat16),
            jax.ShapeDtypeStruct((SLOT_LEN // (WIN * BLOCK), 6 * BLOCK, WIN * BLOCK), jnp.bfloat16),
        ),
        in_specs=[smem, smem, vmem, vmem],
        out_specs=(vmem, vmem, vmem),
        scratch_shapes=[pltpu.VMEM((SLOT_LEN // (WIN * BLOCK), 6 * BLOCK, WIN * BLOCK), jnp.float32)],
        compiler_params=pltpu.CompilerParams(vmem_limit_bytes=40 << 20),
    )(scal, rand, q_rows, kv_slot)


def attend_bwd_kernel(scal_ref, rand_ref, q_ref, kv_ref, p_ref, pg_ref, do_ref, dq_ref, dkv_ref, acc_ref):
    local_blocks = q_ref.shape[0] // BLOCK
    place = scal_ref[0]
    scale = HD ** (-0.5)
    acc_ref[...] = jnp.zeros_like(acc_ref)

    def add_rows(at, size, d_key, d_value):
        where_at = pl.ds(pl.multiple_of(at, BLOCK), size)
        acc_ref[where_at, 0:128] += d_key[:, 0:128]
        acc_ref[where_at, 128:256] += d_key[:, 128:256] + d_value[:, 0:128]
        acc_ref[where_at, 256:384] += d_value[:, 128:256]

    def one_block(step):
        ids, _ = window_ids(scal_ref, rand_ref, step, local_blocks)
        rows = pl.ds(pl.multiple_of(step * BLOCK, BLOCK), BLOCK)
        q_all = spread_heads(q_ref[rows, :], 0)
        do_all = spread_heads(do_ref[rows, :], 1)
        probs = p_ref[step]
        d_prob = dot_nt(do_all, take_blocks(kv_ref, ids, 128))
        wide = probs.astype(jnp.float32)
        mean = jnp.sum(d_prob * wide, axis=1, keepdims=True)
        d_score = (wide * (d_prob - mean)).astype(jnp.bfloat16)
        dq = dot_nn(d_score, take_blocks(kv_ref, ids, 0))
        dq_ref[rows, :] = (fold_heads(dq, 0) * scale).astype(jnp.bfloat16)
        d_key = dot_tn(d_score, q_all)
        d_value = dot_tn(probs, do_all)
        for slot in range(WIN):
            cut = slice(slot * BLOCK, (slot + 1) * BLOCK)
            add_rows(ids[slot] * BLOCK, BLOCK, d_key[cut], d_value[cut])

    @pl.when(place == 0)
    def _():
        chunk = WIN * BLOCK
        parts = SLOT_LEN // chunk
        q_all = spread_heads(q_ref[0 : 2 * BLOCK, :], 0)
        do_all = spread_heads(do_ref[0 : 2 * BLOCK, :], 1)

        def scan_mean(part, mean):
            at = pl.multiple_of(part * chunk, chunk)
            d_prob = dot_nt(do_all, kv_ref[pl.ds(at, chunk), 128:384])
            return mean + jnp.sum(d_prob * pg_ref[part].astype(jnp.float32), axis=1, keepdims=True)

        mean = lax.fori_loop(0, parts, scan_mean, jnp.zeros((q_all.shape[0], 1), jnp.float32))

        def scan_grad(part, dq):
            at = pl.multiple_of(part * chunk, chunk)
            probs = pg_ref[part]
            d_prob = dot_nt(do_all, kv_ref[pl.ds(at, chunk), 128:384])
            d_score = (probs.astype(jnp.float32) * (d_prob - mean)).astype(jnp.bfloat16)
            add_rows(at, chunk, dot_tn(d_score, q_all), dot_tn(probs, do_all))
            return dq + dot_nn(d_score, kv_ref[pl.ds(at, chunk), 0:256])

        dq = lax.fori_loop(0, parts, scan_grad, jnp.zeros((q_all.shape[0], 256), jnp.float32))
        dq_ref[0 : 2 * BLOCK, :] = (fold_heads(dq, 0) * scale).astype(jnp.bfloat16)

    def pair(at, carry):
        one_block(2 * at)
        one_block(2 * at + 1)
        return carry

    lax.fori_loop(jnp.where(place == 0, 1, 0), local_blocks // 2, pair, 0)
    dkv_ref[...] = acc_ref[...].astype(jnp.bfloat16)


def attend_backward(scal, rand, q_rows, kv_slot, probs, wide_probs, d_ctx):
    tokens = q_rows.shape[0]
    vmem = pl.BlockSpec(memory_space=pltpu.VMEM)
    smem = pl.BlockSpec(memory_space=pltpu.SMEM)
    return pl.pallas_call(
        attend_bwd_kernel,
        name="attend_backward",
        out_shape=(
            jax.ShapeDtypeStruct((tokens, 256), jnp.bfloat16),
            jax.ShapeDtypeStruct((SLOT_LEN, 384), jnp.bfloat16),
        ),
        in_specs=[smem, smem] + [vmem] * 5,
        out_specs=(vmem, vmem),
        scratch_shapes=[pltpu.VMEM((SLOT_LEN, 384), jnp.float32)],
        compiler_params=pltpu.CompilerParams(vmem_limit_bytes=40 << 20),
    )(scal, rand, q_rows, kv_slot, probs, wide_probs, d_ctx)


def norm_forward(values_in, gain_vec, shift_vec):
    row_mean = jnp.mean(values_in, axis=1, keepdims=True)
    centred = values_in - row_mean
    inv_std = lax.rsqrt(jnp.mean(centred * centred, axis=1, keepdims=True) + EPS)
    normed = centred * inv_std
    return (normed * gain_vec + shift_vec, normed, inv_std)


def norm_backward(gradient, normed, inv_std, gain_vec):
    scaled = gradient * gain_vec
    inner_term = (
        scaled
        - jnp.mean(scaled, axis=1, keepdims=True)
        - normed * jnp.mean(scaled * normed, axis=1, keepdims=True)
    )
    return (inner_term * inv_std, jnp.sum(gradient * normed, axis=0), jnp.sum(gradient, axis=0))


def partner_2(value, axis, apart):
    mask = 2**apart
    pairs = [(source, source ^ mask) for source in range(lax.axis_size(axis))]
    return lax.ppermute(value, axis, pairs)


def gelu_grad(pre_act, act_grad):
    _, gelu_pull = jax.vjp(lambda inner_val: jax.nn.gelu(inner_val, approximate=True), pre_act)
    return gelu_pull(act_grad)[0].astype(jnp.bfloat16)


def per_device(
    hidden_in, q_weight, q_bias, k_weight, v_weight, v_bias, o_weight, o_bias, norm1_gain, norm1_shift,
    up_weight, up_bias, down_weight, down_bias, norm2_gain, norm2_shift, doc_mask, doc_blocks, rand_blocks,
    out_grad,
):
    low = jnp.bfloat16
    tok_dev = hidden_in.shape[0]
    local_width = q_weight.shape[1]
    share_rows = out_grad.shape[0]
    slot_span = SLOT_LEN // tok_dev
    group_bits = slot_span.bit_length() - 1
    seq_index = lax.axis_index("seq")
    head_index = lax.axis_index("head")
    slot_place = seq_index % slot_span
    slot_index = seq_index // slot_span
    scale = HD ** (-0.5)
    query = ((dot_nn(hidden_in, q_weight) + q_bias).astype(low) * jnp.asarray(scale, low))
    query = jnp.pad(query, ((0, 0), (0, 256 - local_width)))
    kv_weight = jnp.concatenate([k_weight, v_weight], axis=1)
    kv_bias = jnp.concatenate([jnp.zeros_like(v_bias), v_bias])
    slot_pair = (dot_nn(hidden_in, kv_weight) + kv_bias).astype(low)
    for bit_index in range(group_bits):
        partner = partner_2(slot_pair, "seq", bit_index)
        upper_half = seq_index // 2**bit_index % 2 == 1
        slot_pair = jnp.where(
            upper_half,
            jnp.concatenate([partner, slot_pair], axis=0),
            jnp.concatenate([slot_pair, partner], axis=0),
        )
    slot_mask = lax.dynamic_slice_in_dim(doc_mask, slot_index * SLOT_LEN, SLOT_LEN, 0)
    count = jnp.minimum(jnp.sum(slot_mask), doc_blocks[slot_index] * BLOCK)
    scal = jnp.stack([slot_place, count]).astype(jnp.int32)
    rand = rand_blocks.reshape(-1)
    context, probs, wide_probs = attend_forward(scal, rand, query, slot_pair)
    o_pad = jnp.concatenate([jnp.zeros((256 - local_width, o_weight.shape[1]), low), o_weight], axis=0)
    attn_share = lax.psum_scatter(
        dot_nn(context, o_pad).astype(low), "head", scatter_dimension=0, tiled=True
    ).astype(jnp.float32)
    token_share = lax.dynamic_slice_in_dim(hidden_in, head_index * share_rows, share_rows, 0)
    first_sum = token_share.astype(jnp.float32) + attn_share + o_bias
    normed_one, unit_one, inv_one = norm_forward(first_sum, norm1_gain, norm1_shift)
    normed_low = lax.all_gather(normed_one.astype(low), "head", axis=0, tiled=True)
    pre_act = dot_nn(normed_low, up_weight) + up_bias
    act_low = jax.nn.gelu(pre_act, approximate=True).astype(low)
    ffn_share = lax.psum_scatter(
        dot_nn(act_low, down_weight).astype(low), "head", scatter_dimension=0, tiled=True
    ).astype(jnp.float32)
    second_sum = normed_one + ffn_share + down_bias
    layer_out, unit_two, inv_two = norm_forward(second_sum, norm2_gain, norm2_shift)
    second_grad, gain_two_grad, shift_two_grad = norm_backward(out_grad, unit_two, inv_two, norm2_gain)
    down_bias_grad = jnp.sum(second_grad, axis=0)
    second_low = lax.all_gather(second_grad.astype(low), "head", axis=0, tiled=True)
    pre_grad = gelu_grad(pre_act, dot_nt(second_low, down_weight))
    branch_grad = lax.psum_scatter(
        dot_nt(pre_grad, up_weight).astype(low), "head", scatter_dimension=0, tiled=True
    ).astype(jnp.float32)
    down_grad = dot_tn(act_low, second_low)
    up_grad = dot_tn(normed_low, pre_grad)
    up_bias_grad = jnp.sum(pre_grad.astype(jnp.float32), axis=0)
    first_grad, gain_one_grad, shift_one_grad = norm_backward(
        second_grad + branch_grad, unit_one, inv_one, norm1_gain
    )
    o_bias_grad = jnp.sum(first_grad, axis=0)
    first_full = lax.all_gather(first_grad.astype(low), "head", axis=0, tiled=True)
    o_grad = dot_tn(context, first_full)[256 - local_width :]
    d_ctx = dot_nt(first_full, o_pad).astype(low)
    query_low, slot_grad = attend_backward(scal, rand, query, slot_pair, probs, wide_probs, d_ctx)
    query_low = query_low[:, :local_width]
    own_grad = slot_grad.astype(jnp.float32)
    for bit_index in reversed(range(group_bits)):
        half_len = own_grad.shape[0] // 2
        upper_half = seq_index // 2**bit_index % 2 == 1
        lower_part = own_grad[:half_len]
        upper_part = own_grad[half_len:]
        kept_half = jnp.where(upper_half, upper_part, lower_part)
        given_half = jnp.where(upper_half, lower_part, upper_part)
        own_grad = kept_half + partner_2(given_half.astype(low), "seq", bit_index).astype(jnp.float32)
    kv_low = own_grad.astype(low)
    q_grad = dot_tn(hidden_in, query_low)
    q_bias_grad = jnp.sum(query_low.astype(jnp.float32), axis=0)
    kv_grad = dot_tn(hidden_in, kv_low)
    v_bias_grad = jnp.sum(kv_low[:, local_width:].astype(jnp.float32), axis=0)
    in_grad = first_grad + lax.psum_scatter(
        (dot_nt(query_low, q_weight) + dot_nt(kv_low, kv_weight)).astype(low),
        "head", scatter_dimension=0, tiled=True,
    ).astype(jnp.float32)
    summed = lax.psum(
        tuple(part.astype(low) for part in (q_grad, kv_grad, o_grad, up_grad, down_grad)), "seq"
    )
    summed = [part.astype(jnp.float32) for part in summed]
    bias_sums = lax.psum((q_bias_grad, v_bias_grad, up_bias_grad), "seq")
    norm_sums = lax.psum(
        (o_bias_grad, gain_one_grad, shift_one_grad, down_bias_grad, gain_two_grad, shift_two_grad),
        ("seq", "head"),
    )
    return (
        layer_out, in_grad, summed[0], bias_sums[0], summed[1][:, :local_width], summed[1][:, local_width:],
        bias_sums[1], summed[2], norm_sums[0], norm_sums[1], norm_sums[2], summed[3], bias_sums[2], summed[4],
        norm_sums[3], norm_sums[4], norm_sums[5],
    )


def solution(mesh):
    columns, vector, rows, whole = P(None, "head"), P("head"), P("head", None), P()
    tokens, shares = P("seq", None), P(("seq", "head"), None)
    in_specs = (
        tokens, columns, vector, columns, columns, vector, rows, whole, whole, whole, columns, vector, rows,
        whole, whole, whole, whole, whole, tokens, shares,
    )
    out_specs = (
        shares, shares, columns, vector, columns, columns, vector, rows, whole, whole, whole, columns, vector,
        rows, whole, whole, whole,
    )
    return jax.shard_map(per_device, mesh=mesh, in_specs=in_specs, out_specs=out_specs, check_vma=False)
```

time: 848 us -> 546 us (0.64)
  blocking collectives: 267 us -> 66.1 us
  local copies, waits for them, and re-layouts: 110 us -> 19.2 us
  waiting for transfers between devices: 258 us -> 337 us
  other arithmetic: 91.3 us -> 30.9 us
  matrix products: 87.1 us -> 37.1 us
  Pallas kernels: 0 us -> 33.3 us
    psum x1, blocking collectives: 214 us -> 23.4 us  [per_device(): bias_sums = lax.psum((q_bias_grad, v_bias_grad, up_bias_grad), 'seq')]
    psum x1, waiting for transfers between devices: 0.01 us -> 92.2 us  [per_device(): lax.psum(tuple((part.astype(low) for part in (q_grad, kv_grad, o_grad, up...]
    dot_general x30 -> x15, matrix products: 87.1 us -> 37.1 us  [the longest x5 14.3 us: dot_nt(): lax.dot_general(left, right, (((1,), (1,)), ((), ())), preferred_element_...]
    reshape x7 -> x1, local copies, waits for them, and re-layouts: 33.7 us -> 0.09 us  [per_device(): rand = rand_blocks.reshape(-1)]
    pallas_call x0 -> x2, Pallas kernels: none -> 33.3 us  [the longest x1 20.6 us: attend_backward(): pl.pallas_call(attend_bwd_kernel, name='attend_backward', out_shape=(jax....]
    scatter-add x1 -> x0, other arithmetic: 31.8 us -> none  [per_device(): jnp.zeros((slot_blocks, BLOCK, 2 * local_width), jnp.float32).at[block_ids]]
    all_gather x3, waiting for transfers between devices: 89.5 us -> 59 us  [the longest x1 19.7 us: per_device(): lax.all_gather(first_grad.astype(low), 'head', axis=0, tiled=True)]
    slice x17 -> x2, local copies, waits for them, and re-layouts: 22.6 us -> 1.82 us  [the longest x1 1.09 us: per_device(): summed[1][:, local_width:]]
  transfers between devices with their start and end apart: 12 -> 12, of which waited for: 10 -> 11; matrix products, arithmetic and copies ran while one was open for 5% -> 3% of each run, Pallas kernels for 0% -> 0%
where the time goes in v1:
time: 546 us; the launch traced here: 545 us
  waiting for transfers between devices  337 us (62%)
  blocking collectives  66.1 us (12%)
  matrix products  37.1 us (7%)
  Pallas kernels  33.3 us (6%)
  other arithmetic  30.9 us (6%)
  local copies, waits for them, and re-layouts  19.2 us (4%)
  between operations  16 us (3%)
  starting transfers between devices  5.73 us (1%)
    ppermute x4, waiting for transfers between devices, partner_2(): return lax.ppermute(value, axis, pairs)  102 us
    psum x1, waiting for transfers between devices, per_device(): lax.psum(tuple((part.astype(low) for part in (q_grad, kv_grad, o_grad, up...  92.2 us
    psum x1, blocking collectives, per_device(): lax.psum((o_bias_grad, gain_one_grad, shift_one_grad, down_bias_grad, gai...  42.7 us
    reduce_scatter x1, waiting for transfers between devices, per_device(): lax.psum_scatter(dot_nt(pre_grad, up_weight).astype(low), 'head', scatter...  28.2 us
    reduce_scatter x1, waiting for transfers between devices, per_device(): lax.psum_scatter(dot_nn(act_low, down_weight).astype(low), 'head', scatte...  28.1 us
    reduce_scatter x1, waiting for transfers between devices, per_device(): lax.psum_scatter(dot_nn(context, o_pad).astype(low), 'head', scatter_dime...  27.4 us
    psum x1, blocking collectives, per_device(): bias_sums = lax.psum((q_bias_grad, v_bias_grad, up_bias_grad), 'seq')  23.4 us
    pallas_call x1, Pallas kernels, attend_backward(): pl.pallas_call(attend_bwd_kernel, name='attend_backward', out_shape=(jax....  20.6 us
  transfers between devices with their start and end apart: 12, of which 11 were waited for; matrix products, arithmetic and copies ran while one was open for 3% of the time, Pallas kernels for 0%

profile of v1, /device:TPU:0, one launch (start us, length us, event | category | flops | bytes accessed | tf_op | source)
XLA Modules:
  0.0 545.0 jit_solution(1179195852258304737)
XLA Ops:
  12.8 3.0 collective-permute-start
  15.8 17.6 %collective-permute-done = bf16[1024,384]{1,0:T(8,128)(2,1)} collective-permute-done((bf16[1024,384]{1,0:T(8,128)(2,1)S(1)}, bf16[1024,384]{1,0:T(8,128)(2,1)}, u32[]{:S(2)}, u32[]{:S(2)}) %collective-permute-start) | collective-permute-done | bytes 786464 | tf_op jit(solution)/shard_map/ppermute | solution.py:259
  33.4 2.9 maximum_select_fusion.1
  43.4 28.8 %collective-permute-done.1 = bf16[2048,384]{1,0:T(8,128)(2,1)} collective-permute-done((bf16[2048,384]{1,0:T(8,128)(2,1)}, bf16[2048,384]{1,0:T(8,128)(2,1)}, u32[]{:S(2)}, u32[]{:S(2)}) %collective-permute-start.1) | collective-permute-done | bytes 1572896 | tf_op jit(solution)/shard_map/ppermute | solution.py:259
  72.2 3.8 maximum_select_fusion.kv_ref
  76.0 12.7 %attend_forward.1 = (bf16[1024,256]{1,0:T(8,128)(2,1)S(1)}, bf16[16,192,512]{2,1,0:T(8,128)(2,1)S(1)}, bf16[8,384,512]{2,1,0:T(8,128)(2,1)S(1)}) custom-call(s32[2]{0:T(128)S(1)} %pad_add_fusion.scal_ref, s32[48]{0:T(128)S(1)} %reshape.88.rand_ref, bf16[1024,256]{1,0:T(8,128)(2,1)S(1)} %pad.6.q_ref, bf16[4096,384]{1,0:T(8,128)(2,1)S(1)} %maximum_select_fusion.kv_ref), custom_call_target="tpu_custom_call" | custom-call | tf_op jit(solution)/shard_map/attend_forward/pallas_call | solution.py:141
  96.4 27.4 %reduce-scatter.5.cloned.1.call-done = bf16[256,768]{1,0:T(8,128)(2,1)} async-done(((bf16[1024,768]{1,0:T(8,128)(2,1)}), bf16[256,768]{1,0:T(8,128)(2,1)}) %reduce-scatter.5.cloned.1.call-update) | async-done | bytes 393232 | tf_op jit(solution)/shard_map/reduce_scatter | solution.py:302
  128.3 19.7 %all-gather.4.cloned.1.call-done = bf16[1024,768]{1,0:T(8,128)(2,1)} async-done(((bf16[256,768]{1,0:T(8,128)(2,1)}), bf16[1024,768]{1,0:T(8,128)(2,1)}) %all-gather.4.cloned.1.call-update) | async-done | bytes 1572880 | tf_op jit(solution)/shard_map/all_gather | solution.py:308
  148.1 3.1 fusion.29
  152.8 3.3 convolution_convert_fusion.1
  156.2 28.1 %reduce-scatter.7.cloned.1.call-done = bf16[256,768]{1,0:T(8,128)(2,1)} async-done(((bf16[1024,768]{1,0:T(8,128)(2,1)}), bf16[256,768]{1,0:T(8,128)(2,1)}) %reduce-scatter.7.cloned.1.call-update) | async-done | bytes 393232 | tf_op jit(solution)/shard_map/reduce_scatter | solution.py:311
  188.4 19.6 %all-gather.6.cloned.1.call-done = bf16[1024,768]{1,0:T(8,128)(2,1)} async-done(((bf16[256,768]{1,0:T(8,128)(2,1)}), bf16[1024,768]{1,0:T(8,128)(2,1)}) %all-gather.6.cloned.1.call-update) | async-done | bytes 1572880 | tf_op jit(solution)/shard_map/all_gather | solution.py:318
  207.9 5.6 %convert_reduce_fusion = (f32[768]{0:T(1024)S(1)}, bf16[1024,768]{1,0:T(8,128)(2,1)S(1)}) fusion(f32[1024,768]{1,0:T(8,128)} %copy-done.42, f32[768]{0:T(1024)S(1)} %copy-done.39, bf16[1024,768]{1,0:T(8,128)(2,1)} %all-gather.6.cloned.1.call-done, bf16[768,768]{1,0:T(8,128)(2,1)S(1)} %copy-done), kind=kOutput, calls=%fused_computation.10 | convolution fusion | flops 1226046720 | bytes 7477248 | tf_op jit(solution)/shard_map/dot_general | solution.py:17
  214.7 4.0 convolution_convert_fusion
  218.7 28.2 %reduce-scatter.9.cloned.1.call-done = bf16[256,768]{1,0:T(8,128)(2,1)} async-done(((bf16[1024,768]{1,0:T(8,128)(2,1)}), bf16[256,768]{1,0:T(8,128)(2,1)}) %reduce-scatter.9.cloned.1.call-update) | async-done | bytes 393232 | tf_op jit(solution)/shard_map/reduce_scatter | solution.py:320
  251.6 19.7 %all-gather.8.cloned.1.call-done = bf16[1024,768]{1,0:T(8,128)(2,1)} async-done(((bf16[256,768]{1,0:T(8,128)(2,1)}), bf16[1024,768]{1,0:T(8,128)(2,1)}) %all-gather.8.cloned.1.call-update) | async-done | bytes 1572880 | tf_op jit(solution)/shard_map/all_gather | solution.py:330
  277.2 20.6 %attend_backward.1 = (bf16[1024,256]{1,0:T(8,128)(2,1)S(1)}, bf16[4096,384]{1,0:T(8,128)(2,1)S(1)}) custom-call(s32[2]{0:T(128)S(1)} %pad_add_fusion.scal_ref, s32[48]{0:T(128)S(1)} %reshape.88.rand_ref, bf16[1024,256]{1,0:T(8,128)(2,1)S(1)} %copy-done.5, bf16[4096,384]{1,0:T(8,128)(2,1)S(1)} %copy-done.3, bf16[16,192,512]{2,1,0:T(8,128)(2,1)S(1)} %copy-done.7, ...), custom_call_target="tpu_custom_call" | custom-call | tf_op jit(solution)/shard_map/attend_backward/pallas_call | solution.py:224
  298.7 36.5 %collective-permute-done.2 = bf16[2048,384]{1,0:T(8,128)(2,1)S(1)} collective-permute-done((bf16[2048,384]{1,0:T(8,128)(2,1)S(1)}, bf16[2048,384]{1,0:T(8,128)(2,1)S(1)}, u32[]{:S(2)}, u32[]{:S(2)}) %collective-permute-start.2) | collective-permute-done | bytes 1572896 | tf_op jit(solution)/shard_map/ppermute | solution.py:259
  335.8 18.8 %collective-permute-done.3 = bf16[1024,384]{1,0:T(8,128)(2,1)S(1)} collective-permute-done((bf16[1024,384]{1,0:T(8,128)(2,1)S(1)}, bf16[1024,384]{1,0:T(8,128)(2,1)S(1)}, u32[]{:S(2)}, u32[]{:S(2)}) %collective-permute-start.3) | collective-permute-done | bytes 786464 | tf_op jit(solution)/shard_map/ppermute | solution.py:259
  358.0 4.0 convolution_convert_fusion.4
  362.1 3.0 convolution_convert_fusion.3
  369.5 42.7 %all-reduce.3 = (f32[768]{0:T(1024)}, f32[768]{0:T(1024)}, f32[768]{0:T(1024)}, f32[768]{0:T(1024)}, f32[768]{0:T(1024)}, /*index=5*/f32[768]{0:T(1024)}) all-reduce(f32[768]{0:T(1024)S(1)} %get-tuple-element.50, f32[768]{0:T(1024)S(1)} %get-tuple-element.27, ...), channel_id=1, replica_groups=mesh['seq'=8,'head'=4] {'seq','head'}, use_global_device_ids=true, to_apply=%region_21.22 | all-reduce | flops 4608 | bytes 36864 | tf_op jit(solution)/shard_map/psum | solution.py:358
  412.6 23.4 %all-reduce.4 = (f32[192]{0:T(256)}, f32[192]{0:T(256)}, f32[768]{0:T(1024)}) all-reduce(f32[192]{0:T(256)S(1)} %convert_reduce_fusion.2, f32[192]{0:T(256)S(1)} %convert_reduce_fusion.1, f32[768]{0:T(1024)S(1)} %get-tuple-element.52), channel_id=1, replica_groups=mesh['seq'=8,'head'=4] {'seq'}, use_global_device_ids=true, to_apply=%region_15.16 | all-reduce | flops 1152 | bytes 9216 | tf_op jit(solution)/shard_map/psum | solution.py:357
  437.9 92.2 %all-reduce.8.cloned.1.call-done = (bf16[768,192]{0,1:T(8,128)(2,1)}, bf16[768,384]{0,1:T(8,128)(2,1)}, bf16[192,768]{1,0:T(8,128)(2,1)}, bf16[768,768]{1,0:T(8,128)(2,1)}, bf16[768,768]{1,0:T(8,128)(2,1)}) async-done(((bf16[768,192]{0,1:T(8,128)(2,1)}, bf16[768,384]{0,1:T(8,128)(2,1)}, bf16[192,768]{1,0:T(8,128)(2,1)}, bf16[768,768]{1,0:T(8,128)(2,1)}, bf16[768,768]{1,0:T(8,128)(2,1)}), ...) | async-done | bytes 3538960 | tf_op jit(solution)/shard_map/psum | solution.py:353
  (159 shorter events, 60.4 us)
Async XLA Ops:
  7.2 145.6 %copy-start = (bf16[768,768]{1,0:T(8,128)(2,1)S(1)}, bf16[768,768]{1,0:T(8,128)(2,1)}, u32[]{:S(2)}) copy-start(bf16[768,768]{1,0:T(8,128)(2,1)} %param.32) | copy-start | bytes 3538948
  7.2 116.6 %reduce-scatter.5.cloned.1.call-start = ((), (), s32[]{:S(2)}) async-start(), calls=%async_computation.4 | async-start | bytes 1966080 | tf_op jit(solution)/shard_map/reduce_scatter | solution.py:302
  12.8 20.7 %collective-permute-start = (bf16[1024,384]{1,0:T(8,128)(2,1)S(1)}, bf16[1024,384]{1,0:T(8,128)(2,1)}, u32[]{:S(2)}, u32[]{:S(2)}) collective-permute-start(bf16[1024,384]{1,0:T(8,128)(2,1)S(1)} %fusion.8), channel_id=1, source_target_pairs={{0,4},{4,0},{8,12},{12,8},{16,20},{20,16},{24,28},{28,24},{1,5},{5... | collective-permute-start | bytes 2359304 | tf_op jit(solution)/shard_map/ppermute | solution.py:259
  36.3 35.9 %collective-permute-start.1 = (bf16[2048,384]{1,0:T(8,128)(2,1)}, bf16[2048,384]{1,0:T(8,128)(2,1)}, u32[]{:S(2)}, u32[]{:S(2)}) collective-permute-start(bf16[2048,384]{1,0:T(8,128)(2,1)} %maximum_select_fusion.1), channel_id=1, source_target_pairs={{0,8},{4,12},{8,0},{12,4},{16,24},{20,28},{24,16},{28,20},{1,9},{5... | collective-permute-start | bytes 4718600 | tf_op jit(solution)/shard_map/ppermute | solution.py:259
  43.3 32.7 %copy-start.4 = (bf16[1024,256]{1,0:T(8,128)(2,1)}, bf16[1024,256]{1,0:T(8,128)(2,1)S(1)}, u32[]{:S(2)}) copy-start(bf16[1024,256]{1,0:T(8,128)(2,1)S(1)} %pad.6.q_ref) | copy-start | bytes 1572868
  93.8 30.0 %copy-start.30 = (f32[768]{0:T(1024)S(1)}, f32[768]{0:T(1024)}, u32[]{:S(2)}) copy-start(f32[768]{0:T(1024)} %param.27) | copy-start | bytes 9220
  94.6 31.7 %copy-start.31 = (f32[768]{0:T(1024)S(1)}, f32[768]{0:T(1024)}, u32[]{:S(2)}) copy-start(f32[768]{0:T(1024)} %param.28) | copy-start | bytes 9220
  94.6 31.7 %copy-start.32 = (f32[768]{0:T(1024)S(1)}, f32[768]{0:T(1024)}, u32[]{:S(2)}) copy-start(f32[768]{0:T(1024)} %param.29) | copy-start | bytes 9220
  96.3 51.8 %all-gather.4.cloned.1.call-start = ((), (), s32[]{:S(2)}) async-start(), calls=%async_computation.5 | async-start | bytes 1966080 | tf_op jit(solution)/shard_map/all_gather | solution.py:308
  128.3 56.0 %reduce-scatter.7.cloned.1.call-start = ((), (), s32[]{:S(2)}) async-start(), calls=%async_computation.6 | async-start | bytes 1966080 | tf_op jit(solution)/shard_map/reduce_scatter | solution.py:311
  152.8 31.4 %copy-start.14 = (bf16[256,768]{1,0:T(8,128)(2,1)S(1)}, bf16[256,768]{1,0:T(8,128)(2,1)}, u32[]{:S(2)}) copy-start(bf16[256,768]{1,0:T(8,128)(2,1)} %reduce-scatter.5.cloned.1.call-done) | copy-start | bytes 1179652
  152.8 31.4 %copy-start.34 = (f32[768]{0:T(1024)S(1)}, f32[768]{0:T(1024)}, u32[]{:S(2)}) copy-start(f32[768]{0:T(1024)} %param.33) | copy-start | bytes 9220
  156.1 30.4 %copy-start.35 = (f32[768]{0:T(1024)S(1)}, f32[768]{0:T(1024)}, u32[]{:S(2)}) copy-start(f32[768]{0:T(1024)} %param.35) | copy-start | bytes 9220
  156.2 51.8 %all-gather.6.cloned.1.call-start = ((), (), s32[]{:S(2)}) async-start(), calls=%async_computation.7 | async-start | bytes 1966080 | tf_op jit(solution)/shard_map/all_gather | solution.py:318
  188.2 58.7 %reduce-scatter.9.cloned.1.call-start = ((), (), s32[]{:S(2)}) async-start(), calls=%async_computation.8 | async-start | bytes 1966080 | tf_op jit(solution)/shard_map/reduce_scatter | solution.py:320
  214.7 32.2 %copy-start.16 = (bf16[1024,768]{1,0:T(8,128)(2,1)S(1)}, bf16[1024,768]{1,0:T(8,128)(2,1)}, u32[]{:S(2)}) copy-start(bf16[1024,768]{1,0:T(8,128)(2,1)} %param.20) | copy-start | bytes 4718596
  214.7 32.2 %copy-start.20 = (f32[256,768]{1,0:T(8,128)S(1)}, f32[256,768]{1,0:T(8,128)}, u32[]{:S(2)}) copy-start(f32[256,768]{1,0:T(8,128)} %get-tuple-element.55) | copy-start | bytes 2359300
  218.7 52.7 %all-gather.8.cloned.1.call-start = ((), (), s32[]{:S(2)}) async-start(), calls=%async_computation.9 | async-start | bytes 1966080 | tf_op jit(solution)/shard_map/all_gather | solution.py:330
  251.6 184.4 %reduce-scatter.11.cloned.1.call-start = ((), (), s32[]{:S(2)}) async-start(), calls=%async_computation.10 | async-start | bytes 1966080 | tf_op jit(solution)/shard_map/reduce_scatter | solution.py:349
  297.9 58.1 %copy-start.12 = (bf16[1024,256]{1,0:T(8,128)(2,1)}, bf16[1024,256]{1,0:T(8,128)(2,1)S(1)}, u32[]{:S(2)}) copy-start(bf16[1024,256]{1,0:T(8,128)(2,1)S(1)} %get-tuple-element.25) | copy-start | bytes 1572868
  298.6 36.6 %collective-permute-start.2 = (bf16[2048,384]{1,0:T(8,128)(2,1)S(1)}, bf16[2048,384]{1,0:T(8,128)(2,1)S(1)}, u32[]{:S(2)}, u32[]{:S(2)}) collective-permute-start(bf16[2048,384]{1,0:T(8,128)(2,1)S(1)} %select_convert_fusion), channel_id=1, source_target_pairs={{0,8},{4,12},{8,0},{12,4},{16,24},{20,28},{24,16},{28,20},{1,9},{5... | collective-permute-start | bytes 4718600 | tf_op jit(solution)/shard_map/ppermute | solution.py:259
  335.7 18.9 %collective-permute-start.3 = (bf16[1024,384]{1,0:T(8,128)(2,1)S(1)}, bf16[1024,384]{1,0:T(8,128)(2,1)S(1)}, u32[]{:S(2)}, u32[]{:S(2)}) collective-permute-start(bf16[1024,384]{1,0:T(8,128)(2,1)S(1)} %select_convert_fusion.1), channel_id=1, source_target_pairs={{0,4},{4,0},{8,12},{12,8},{16,20},{20,16},{24,28},{28,24},{1,5},{5... | collective-permute-start | bytes 2359304 | tf_op jit(solution)/shard_map/ppermute | solution.py:259
  357.7 172.4 %all-reduce.8.cloned.1.call-start = ((), (), s32[]{:S(2)}) async-start(), calls=%async_computation.11 | async-start | bytes 7077888 | tf_op jit(solution)/shard_map/psum | solution.py:353
  369.5 66.5 %copy-start.19 = (f32[256,768]{1,0:T(8,128)S(1)}, f32[256,768]{1,0:T(8,128)}, u32[]{:S(2)}) copy-start(f32[256,768]{1,0:T(8,128)} %copy-done.18) | copy-start | bytes 2359300
  (33 other events, 306.2 us)
Sparse Core Ops, SparseCore 0:
  96.4 27.2 reduce-scatter.4
  128.4 19.6 all-gather.3
  156.3 27.9 reduce-scatter.6
  188.3 19.6 all-gather.5
  218.8 28.0 reduce-scatter.8
  251.7 19.6 all-gather.7
  357.8 26.8 reduce-scatter.10
  390.1 140.0 all-reduce.7

commit v2 on v1

--- a/solution.py
+++ b/solution.py
@@ -235,33 +235,659 @@
     )(scal, rand, q_rows, kv_slot, probs, wide_probs, d_ctx)
 
 
-def norm_forward(values_in, gain_vec, shift_vec):
-    row_mean = jnp.mean(values_in, axis=1, keepdims=True)
-    centred = values_in - row_mean
-    inv_std = lax.rsqrt(jnp.mean(centred * centred, axis=1, keepdims=True) + EPS)
-    normed = centred * inv_std
-    return (normed * gain_vec + shift_vec, normed, inv_std)
-
-
-def norm_backward(gradient, normed, inv_std, gain_vec):
-    scaled = gradient * gain_vec
-    inner_term = (
+MESH = pl.DeviceIdType.MESH
+VM = pl.BlockSpec(memory_space=pltpu.VMEM)
+LOW = jnp.bfloat16
+
+
+def flip(index, bit):
+    step = 1 << bit
+    return index + step - 2 * step * ((index // step) % 2)
+
+
+def remote(src, dst, send, recv, slot, where):
+    return pltpu.make_async_remote_copy(
+        src_ref=src, dst_ref=dst, send_sem=send.at[slot], recv_sem=recv.at[slot],
+        device_id=where, device_id_type=MESH,
+    )
+
+
+def greet(partners):
+    barrier = pltpu.get_barrier_semaphore()
+    for where in partners:
+        pl.semaphore_signal(barrier, inc=1, device_id=where, device_id_type=MESH)
+    pl.semaphore_wait(barrier, len(partners))
+
+
+def project_kernel(hid, qw, kw, vw, qb, vb, ow, q_out, kv_out, o_out, send, recv):
+    tokens = hid.shape[0]
+    half = tokens // 2
+    seq, head = lax.axis_index("seq"), lax.axis_index("head")
+    spans = SLOT_LEN // tokens
+    place = seq % spans
+    by_x, by_z = {"seq": flip(seq, 0)}, {"seq": flip(seq, 1)}
+    core, far = {"head": flip(head, 0)}, {"head": flip(head, 1)}
+    greet((by_x, by_z, core, far))
+
+    mine, theirs = o_out.at[head], o_out.at[flip(head, 1)]
+    o_core = remote(ow, mine, send, recv, 6, core)
+    o_far = remote(ow, mine, send, recv, 7, far)
+    o_relay = remote(theirs, theirs, send, recv, 8, core)
+    o_far.start()
+    o_core.start()
+    o_out[head] = ow[...]
+
+    def rows_of(owner, part):
+        at = pl.multiple_of(owner * tokens + part * half, half)
+        return kv_out.at[pl.ds(at, half)]
+
+    def fill(part):
+        rows = hid[part * half : (part + 1) * half, :]
+        keys = dot_nn(rows, kw[...])
+        values = dot_nn(rows, vw[...]) + vb[...]
+        at = pl.multiple_of(place * tokens + part * half, half)
+        kv_out[pl.ds(at, half), :] = jnp.concatenate([keys.astype(LOW), values.astype(LOW)], axis=1)
+
+    own_a, own_b = rows_of(place, 0), rows_of(place, 1)
+    fwd_a, fwd_b = rows_of(flip(place, 0), 0), rows_of(flip(place, 1), 1)
+    copies = [
+        remote(own_a, own_a, send, recv, 0, by_x),
+        remote(own_b, own_b, send, recv, 1, by_z),
+        remote(own_b, own_b, send, recv, 2, by_x),
+        remote(own_a, own_a, send, recv, 3, by_z),
+        remote(fwd_a, fwd_a, send, recv, 4, by_z),
+        remote(fwd_b, fwd_b, send, recv, 5, by_x),
+    ]
+    fill(0)
+    copies[0].start()
+    fill(1)
+    for at in (1, 2, 3):
+        copies[at].start()
+    for part in range(2):
+        rows = hid[part * half : (part + 1) * half, :]
+        query = (dot_nn(rows, qw[...]) + qb[...]).astype(LOW) * jnp.asarray(HD ** (-0.5), LOW)
+        query = jnp.concatenate([query, jnp.zeros((half, 256 - query.shape[1]), LOW)], axis=1)
+        q_out[part * half : (part + 1) * half, :] = query
+    copies[0].wait_recv()
+    copies[4].start()
+    copies[1].wait_recv()
+    copies[5].start()
+    o_far.wait_recv()
+    o_relay.start()
+    for at in (2, 3, 4, 5):
+        copies[at].wait_recv()
+    o_core.wait_recv()
+    o_relay.wait_recv()
+    for copy in copies + [o_core, o_far, o_relay]:
+        copy.wait_send()
+
+
+def project(hid, qw, kw, vw, qb, vb, ow):
+    tokens, width = hid.shape
+    heads = lax.axis_size("head")
+    return pl.pallas_call(
+        project_kernel,
+        name="project_gather",
+        out_shape=(
+            jax.ShapeDtypeStruct((tokens, 256), LOW),
+            jax.ShapeDtypeStruct((SLOT_LEN, 2 * kw.shape[1]), LOW),
+            jax.ShapeDtypeStruct((heads, ow.shape[0], width), LOW),
+        ),
+        in_specs=[VM] * 7,
+        out_specs=(VM,) * 3,
+        scratch_shapes=[pltpu.SemaphoreType.DMA((9,)), pltpu.SemaphoreType.DMA((9,))],
+        compiler_params=pltpu.CompilerParams(
+            collective_id=0, has_side_effects=True, vmem_limit_bytes=32 << 20
+        ),
+    )(hid, qw, kw, vw, qb.reshape(1, -1), vb.reshape(1, -1), ow)
+
+
+def norm_fwd(values, gain, shift):
+    centred = values - jnp.mean(values, axis=1, keepdims=True)
+    inv = lax.rsqrt(jnp.mean(centred * centred, axis=1, keepdims=True) + EPS)
+    unit = centred * inv
+    return unit * gain + shift, unit, inv
+
+
+def norm_bwd(grad, unit, inv, gain):
+    scaled = grad * gain
+    inner = (
         scaled
         - jnp.mean(scaled, axis=1, keepdims=True)
-        - normed * jnp.mean(scaled * normed, axis=1, keepdims=True)
-    )
-    return (inner_term * inv_std, jnp.sum(gradient * normed, axis=0), jnp.sum(gradient, axis=0))
-
-
-def partner_2(value, axis, apart):
-    mask = 2**apart
-    pairs = [(source, source ^ mask) for source in range(lax.axis_size(axis))]
-    return lax.ppermute(value, axis, pairs)
-
-
-def gelu_grad(pre_act, act_grad):
-    _, gelu_pull = jax.vjp(lambda inner_val: jax.nn.gelu(inner_val, approximate=True), pre_act)
-    return gelu_pull(act_grad)[0].astype(jnp.bfloat16)
+        - unit * jnp.mean(scaled * unit, axis=1, keepdims=True)
+    )
+    return inner * inv
+
+
+def column_sum(values):
+    return jnp.sum(values, axis=0, keepdims=True)
+
+
+CHUNKS = 2
+ROOT = 0.7978845608028654
+CUBE = 0.044715
+
+
+def middle_kernel(
+    ctx, o_full, hid, o_bias, gain1, shift1, up_w, up_b, down_w, down_b, gain2, shift2, out_grad,
+    layer_out, first_out, d_ctx, up_grad, down_grad, o_grad, vec,
+    ctx_all, normed, unit1, inv1, second, x_all, s_all, f_all, slope, act, pre_all,
+    keep, to_core, from_core, to_far, from_far, send, recv,
+):
+    share = out_grad.shape[0]
+    rows = share // CHUNKS
+    width = hid.shape[1]
+    seq, head = lax.axis_index("seq"), lax.axis_index("head")
+    core, far, both = flip(head, 0), flip(head, 1), flip(flip(head, 0), 1)
+    order = (head, core, far, both)
+    greet(tuple({"head": at} for at in order[1:]))
+    counter = [0]
+
+    def copy_to(src, dst, where):
+        slot = counter[0]
+        counter[0] += 1
+        made.append(remote(src, dst, send, recv, slot, {"head": where}))
+        return made[-1]
+
+    made = []
+
+    def own_rows(part):
+        return slice(part * rows, (part + 1) * rows)
+
+    def block_rows(owner, part):
+        return pl.ds(pl.multiple_of(owner * share + part * rows, rows), rows)
+
+    ctx_copies = []
+    for part in range(CHUNKS):
+        for at in (3, 2, 1):
+            ctx_copies.append(
+                copy_to(ctx.at[block_rows(order[at], part)], ctx_all.at[head, own_rows(part)], order[at])
+            )
+            ctx_copies[-1].start()
+    for part in range(CHUNKS):
+        ctx_all[head, own_rows(part)] = ctx[block_rows(head, part), :]
+
+    class Gather:
+        def __init__(self, buffer):
+            self.buffer = buffer
+            self.to_core, self.to_far, self.relay = [None] * CHUNKS, [None] * CHUNKS, [None] * CHUNKS
+
+        def start(self, part):
+            own = self.buffer.at[part, 0]
+            self.to_far[part] = copy_to(own, self.buffer.at[part, 2], far)
+            self.to_far[part].start()
+            self.to_core[part] = copy_to(own, self.buffer.at[part, 1], core)
+            self.to_core[part].start()
+
+        def pass_on(self, part):
+            self.to_far[part].wait_recv()
+            self.relay[part] = copy_to(self.buffer.at[part, 2], self.buffer.at[part, 3], core)
+            self.relay[part].start()
+
+        def pair(self, part, at):
+            return self.buffer[part, 2 * at : 2 * at + 2].reshape(2 * rows, width)
+
+    class Scatter:
+        def __init__(self, at):
+            self.at = at
+            self.near, self.through, self.away = [None] * CHUNKS, [None] * CHUNKS, [None] * CHUNKS
+
+        def put_near(self, part, partial):
+            keep[part, 0] = partial[:rows]
+            to_core[self.at, part, 0] = partial[rows:].astype(LOW)
+            self.near[part] = copy_to(to_core.at[self.at, part, 0], from_core.at[self.at, part, 0], core)
+            self.near[part].start()
+
+        def put_far(self, part, partial):
+            to_core[self.at, part, 1] = partial[rows:].astype(LOW)
+            self.through[part] = copy_to(to_core.at[self.at, part, 1], from_core.at[self.at, part, 1], core)
+            self.through[part].start()
+            keep[part, 1] = partial[:rows]
+
+        def pass_on(self, part):
+            self.through[part].wait_recv()
+            total = keep[part, 1] + from_core[self.at, part, 1].astype(jnp.float32)
+            to_far[self.at, part] = total.astype(LOW)
+            self.away[part] = copy_to(to_far.at[self.at, part], from_far.at[self.at, part], far)
+            self.away[part].start()
+
+        def result(self, part):
+            self.near[part].wait_recv()
+            self.away[part].wait_recv()
+            return (
+                keep[part, 0]
+                + from_core[self.at, part, 0].astype(jnp.float32)
+                + from_far[self.at, part].astype(jnp.float32)
+            )
+
+    def exchange(gather, scatter, make):
+        for part in range(CHUNKS):
+            gather.to_core[part].wait_recv()
+            scatter.put_near(part, make(part, 0))
+        gather.pass_on(0)
+        for part in range(CHUNKS):
+            gather.relay[part].wait_recv()
+            scatter.put_far(part, make(part, 1))
+            if part + 1 < CHUNKS:
+                gather.pass_on(part + 1)
+            scatter.pass_on(part)
+
+    x_gather, s_gather, f_gather = Gather(x_all), Gather(s_all), Gather(f_all)
+    ffn_scatter, branch_scatter = Scatter(0), Scatter(1)
+
+    for part in range(CHUNKS):
+        for at in range(3):
+            ctx_copies[part * 3 + at].wait_recv()
+        attn = None
+        for at in range(4):
+            rows_at = ctx_all[at, own_rows(part)]
+            weight = o_full[at]
+            weight = jnp.concatenate([jnp.zeros((256 - weight.shape[0], width), LOW), weight], axis=0)
+            term = dot_nn(rows_at, weight)
+            attn = term if attn is None else attn + term
+        token = hid[block_rows(head, part), :].astype(jnp.float32)
+        normed_f, unit_f, inv_f = norm_fwd(token + attn + o_bias[...], gain1[...], shift1[...])
+        normed[own_rows(part)] = normed_f
+        unit1[own_rows(part)] = unit_f
+        inv1[own_rows(part)] = inv_f
+        x_all[part, 0] = normed_f.astype(LOW)
+        x_gather.start(part)
+
+    def ffn_forward(part, at):
+        pre = dot_nn(x_gather.pair(part, at), up_w[...]) + up_b[...]
+        square = pre * pre
+        tanh = jnp.tanh(ROOT * (pre + CUBE * square * pre))
+        slope[part, at] = 0.5 * (1.0 + tanh) + (0.5 * ROOT) * pre * (1.0 - tanh * tanh) * (
+            1.0 + (3.0 * CUBE) * square
+        )
+        acted = (0.5 * pre * (1.0 + tanh)).astype(LOW)
+        act[part, at] = acted
+        return dot_nn(acted, down_w[...])
+
+    exchange(x_gather, ffn_scatter, ffn_forward)
+
+    gain2_sum, shift2_sum, down_sum = 0.0, 0.0, 0.0
+    for part in range(CHUNKS):
+        total = normed[own_rows(part)] + ffn_scatter.result(part) + down_b[...]
+        out, unit_f, inv_f = norm_fwd(total, gain2[...], shift2[...])
+        layer_out[own_rows(part)] = out
+        grad = out_grad[own_rows(part)]
+        second_f = norm_bwd(grad, unit_f, inv_f, gain2[...])
+        second[own_rows(part)] = second_f
+        s_all[part, 0] = second_f.astype(LOW)
+        s_gather.start(part)
+        gain2_sum += column_sum(grad * unit_f)
+        shift2_sum += column_sum(grad)
+        down_sum += column_sum(second_f)
+
+    bias_sum = [0.0]
+
+    def ffn_backward(part, at):
+        pulled = dot_nt(s_gather.pair(part, at), down_w[...])
+        pre_grad = (pulled * slope[part, at]).astype(LOW)
+        pre_all[part, at] = pre_grad
+        bias_sum[0] += column_sum(pre_grad.astype(jnp.float32))
+        return dot_nt(pre_grad, up_w[...])
+
+    exchange(s_gather, branch_scatter, ffn_backward)
+
+    tokens = 4 * share
+    step = 256
+
+    def weight_rows(at, carry):
+        cut = pl.ds(pl.multiple_of(at * step, step), step)
+        down_grad[cut, :] = dot_tn(
+            act[:, :, :, cut].reshape(tokens, step), s_all[...].reshape(tokens, width)
+        ).astype(LOW)
+        up_grad[cut, :] = dot_tn(
+            x_all[:, :, :, cut].reshape(tokens, step), pre_all[...].reshape(tokens, up_w.shape[1])
+        ).astype(LOW)
+        return carry
+
+    gain1_sum, shift1_sum, o_sum = 0.0, 0.0, 0.0
+    for part in range(CHUNKS):
+        grad = second[own_rows(part)] + branch_scatter.result(part)
+        unit_f = unit1[own_rows(part)]
+        first_f = norm_bwd(grad, unit_f, inv1[own_rows(part)], gain1[...])
+        first_out[own_rows(part)] = first_f
+        f_all[part, 0] = first_f.astype(LOW)
+        f_gather.start(part)
+        gain1_sum += column_sum(grad * unit_f)
+        shift1_sum += column_sum(grad)
+        o_sum += column_sum(first_f)
+    lax.fori_loop(0, width // step, weight_rows, 0)
+
+    weight = o_full[head]
+    weight = jnp.concatenate([jnp.zeros((256 - weight.shape[0], width), LOW), weight], axis=0)
+    o_total = None
+
+    def back(part, at):
+        rows_f = f_gather.pair(part, at)
+        grad = dot_nt(rows_f, weight).astype(LOW)
+        term = None
+        first_ctx = ctx[block_rows(order[2 * at], part), :]
+        second_ctx = ctx[block_rows(order[2 * at + 1], part), :]
+        d_ctx[block_rows(order[2 * at], part), :] = grad[:rows]
+        d_ctx[block_rows(order[2 * at + 1], part), :] = grad[rows:]
+        return dot_tn(rows_f, jnp.concatenate([first_ctx, second_ctx], axis=0))
+
+    o_total = 0.0
+    for part in range(CHUNKS):
+        f_gather.to_core[part].wait_recv()
+        o_total += back(part, 0)
+    for part in range(CHUNKS):
+        f_gather.pass_on(part)
+    for part in range(CHUNKS):
+        f_gather.relay[part].wait_recv()
+        o_total += back(part, 1)
+    o_grad[...] = o_total
+    zero = jnp.zeros((1, width), jnp.float32)
+    vec[...] = jnp.concatenate(
+        [o_sum, gain1_sum, shift1_sum, down_sum, gain2_sum, shift2_sum, bias_sum[0], zero], axis=0
+    )
+    for copy in made:
+        copy.wait_send()
+
+
+def middle(ctx, o_full, hid, o_bias, gain1, shift1, up_w, up_b, down_w, down_b, gain2, shift2, out_grad):
+    tokens, width = hid.shape
+    share = out_grad.shape[0]
+    rows = share // CHUNKS
+    hidden = up_w.shape[1]
+    f32 = jnp.float32
+    line = lambda value: value.reshape(1, -1)
+    gathered = pltpu.VMEM((CHUNKS, 4, rows, width), LOW)
+    copies = CHUNKS * (3 + 3 * 3 + 2 * 3)
+    return pl.pallas_call(
+        middle_kernel,
+        name="middle",
+        out_shape=(
+            jax.ShapeDtypeStruct((share, width), f32),
+            jax.ShapeDtypeStruct((share, width), f32),
+            jax.ShapeDtypeStruct((tokens, 256), LOW),
+            jax.ShapeDtypeStruct((width, hidden), LOW),
+            jax.ShapeDtypeStruct((hidden, width), LOW),
+            jax.ShapeDtypeStruct((width, 256), f32),
+            jax.ShapeDtypeStruct((8, width), f32),
+        ),
+        in_specs=[VM] * 13,
+        out_specs=(VM,) * 7,
+        scratch_shapes=[
+            pltpu.VMEM((4, share, 256), LOW),
+            pltpu.VMEM((share, width), f32),
+            pltpu.VMEM((share, width), f32),
+            pltpu.VMEM((share, 1), f32),
+            pltpu.VMEM((share, width), f32),
+            gathered,
+            gathered,
+            gathered,
+            pltpu.VMEM((CHUNKS, 2, 2 * rows, hidden), f32),
+            pltpu.VMEM((CHUNKS, 2, 2 * rows, hidden), LOW),
+            pltpu.VMEM((CHUNKS, 2, 2 * rows, hidden), LOW),
+            pltpu.VMEM((CHUNKS, 2, rows, width), f32),
+            pltpu.VMEM((2, CHUNKS, 2, rows, width), LOW),
+            pltpu.VMEM((2, CHUNKS, 2, rows, width), LOW),
+            pltpu.VMEM((2, CHUNKS, rows, width), LOW),
+            pltpu.VMEM((2, CHUNKS, rows, width), LOW),
+            pltpu.SemaphoreType.DMA((copies,)),
+            pltpu.SemaphoreType.DMA((copies,)),
+        ],
+        compiler_params=pltpu.CompilerParams(
+            collective_id=1, has_side_effects=True, vmem_limit_bytes=48 << 20
+        ),
+    )(
+        ctx, o_full, hid, line(o_bias), line(gain1), line(shift1), up_w, line(up_b), down_w, line(down_b),
+        line(gain2), line(shift2), out_grad,
+    )
+
+
+def tail_kernel(
+    hid, dq, dkv, qw, kw, vw, first, up_grad, down_grad, o_grad, vec,
+    in_grad, big_out, small_out, vec_out,
+    pair_in, pair_out, partial, small, big_ring, small_ring, near_out, near_in, far_out, far_in,
+    vec_now, vec_send, vec_recv, send, recv, ring_send, ring_recv,
+):
+    n = lax.axis_size("seq")
+    tokens, width = hid.shape
+    half, share = tokens // 2, first.shape[0]
+    depth = big_ring.shape[2]
+    spans = SLOT_LEN // tokens
+    seq, head = lax.axis_index("seq"), lax.axis_index("head")
+    place = seq % spans
+    f32 = jnp.float32
+    side, along = seq % 2, seq // 2
+    spot = along + side * (n - 1 - 2 * along)
+
+    def member(pos):
+        turn = pos // (n // 2)
+        return 2 * (pos + turn * (n - 1 - 2 * pos)) + turn
+
+    ways = ({"seq": member((spot + 1) % n)}, {"seq": member((spot + n - 1) % n)})
+    signs = (-1, 1)
+    by_x, by_z = {"seq": flip(seq, 0)}, {"seq": flip(seq, 1)}
+    core, far = flip(head, 0), flip(head, 1)
+    both = flip(core, 1)
+    seq_bits = n.bit_length() - 1
+    vec_peers = [{"seq": flip(seq, bit)} for bit in range(seq_bits)] + [{"head": core}, {"head": far}]
+    greet((by_x, by_z, *ways, *vec_peers))
+
+    def rows_of(owner, part):
+        return pl.ds(pl.multiple_of(owner * tokens + part * half, half), half)
+
+    x_at, z_at = flip(place, 0), flip(place, 1)
+    d_at = flip(x_at, 1)
+    copies = [
+        remote(dkv.at[rows_of(d_at, 0)], pair_in.at[0], send, recv, 0, by_z),
+        remote(dkv.at[rows_of(d_at, 1)], pair_in.at[1], send, recv, 1, by_x),
+        remote(dkv.at[rows_of(x_at, 1)], pair_in.at[2], send, recv, 2, by_x),
+        remote(dkv.at[rows_of(z_at, 0)], pair_in.at[3], send, recv, 3, by_z),
+        remote(pair_out.at[0], pair_in.at[4], send, recv, 4, by_x),
+        remote(pair_out.at[1], pair_in.at[5], send, recv, 5, by_z),
+    ]
+    for at in range(4):
+        copies[at].start()
+
+    gap = jnp.zeros((width, 256 - qw.shape[1]), LOW)
+    partial[...] = dot_nt(dq[...], jnp.concatenate([qw[...], gap], axis=1))
+    copies[0].wait_recv()
+    pair_out[0] = (dkv[rows_of(x_at, 0), :].astype(f32) + pair_in[0].astype(f32)).astype(LOW)
+    copies[4].start()
+    copies[1].wait_recv()
+    pair_out[1] = (dkv[rows_of(z_at, 1), :].astype(f32) + pair_in[1].astype(f32)).astype(LOW)
+    copies[5].start()
+
+    rings = ((big_ring, big_out, (up_grad, down_grad)), (small_ring, small_out, (small.at[0], small.at[1])))
+
+    def chunk(pos):
+        return pl.ds(pl.multiple_of(((pos + 2 * n) % n) * depth, 16), depth)
+
+    def reduce_copy(kind, way, step):
+        ring = rings[kind][0]
+        return pltpu.make_async_remote_copy(
+            src_ref=ring.at[way, step], dst_ref=ring.at[way, step + 1],
+            send_sem=ring_send.at[0, kind, way, step], recv_sem=ring_recv.at[0, kind, way, step],
+            device_id=ways[way], device_id_type=MESH,
+        )
+
+    def spread_copy(kind, way, step):
+        rows = rings[kind][1].at[way, chunk(spot + signs[way] * (step - 1))]
+        return pltpu.make_async_remote_copy(
+            src_ref=rows, dst_ref=rows,
+            send_sem=ring_send.at[1, kind, way, step], recv_sem=ring_recv.at[1, kind, way, step],
+            device_id=ways[way], device_id_type=MESH,
+        )
+
+    def open_ring(kind):
+        ring, _, source = rings[kind]
+        for way in range(2):
+            ring[way, 0] = source[way][chunk(spot), :]
+            reduce_copy(kind, way, 0).start()
+
+    def add_ring(kind, way, step):
+        ring, _, source = rings[kind]
+        reduce_copy(kind, way, step).wait_recv()
+        mine = source[way][chunk(spot + signs[way] * (step + 1)), :]
+        ring[way, step + 1] = (ring[way, step + 1].astype(f32) + mine.astype(f32)).astype(LOW)
+
+    open_ring(0)
+    q_part = dot_tn(hid[...], dq[...])
+    small[1, 0:width, 0:128] = q_part[:, 0:128].astype(LOW)
+    small[1, 0:width, 128:256] = (q_part[:, 128:256] + o_grad[:, 0:128]).astype(LOW)
+    small[1, 0:width, 256:384] = o_grad[:, 128:256].astype(LOW)
+    if n * depth > width:
+        small[:, width:, :] = jnp.zeros((2, n * depth - width, small.shape[2]), LOW)
+    for at in range(2, 6):
+        copies[at].wait_recv()
+    own = []
+    for part in range(2):
+        mine = dkv[rows_of(place, part), :].astype(f32)
+        first_in, second_in = (3, 4) if part == 0 else (2, 5)
+        own.append((mine + pair_in[first_in].astype(f32) + pair_in[second_in].astype(f32)).astype(LOW))
+    own = jnp.concatenate(own, axis=0)
+    small[0, 0:width, :] = dot_tn(hid[...], own).astype(LOW)
+    open_ring(1)
+    partial[...] += dot_nt(own[:, 0:256], jnp.concatenate([kw[...], gap], axis=1)) + dot_nt(
+        own[:, 128:384], jnp.concatenate([gap, vw[...]], axis=1)
+    )
+
+    def share_rows(owner):
+        return partial[pl.ds(pl.multiple_of(owner * share, share), share), :]
+
+    near_out[0] = share_rows(both).astype(LOW)
+    near_out[1] = share_rows(core).astype(LOW)
+    near = [remote(near_out.at[at], near_in.at[at], send, recv, 6 + at, {"head": core}) for at in range(2)]
+    near[0].start()
+    near[1].start()
+    sums = jnp.concatenate(
+        [
+            jnp.concatenate(
+                [column_sum(dq[...].astype(f32)), jnp.zeros((1, width - dq.shape[1]), f32)], axis=1
+            ),
+            jnp.concatenate(
+                [column_sum(own.astype(f32)), jnp.zeros((1, width - own.shape[1]), f32)], axis=1
+            ),
+            jnp.zeros((6, width), f32),
+        ],
+        axis=0,
+    )
+    vec_now[0:8] = vec[...]
+    vec_now[8:16] = sums
+    far_copy = remote(far_out, far_in, send, recv, 8, {"head": far})
+
+    def vec_copy(at):
+        return remote(vec_send.at[at], vec_recv.at[at], send, recv, 9 + at, vec_peers[at])
+
+    def ring_step(step):
+        for kind in range(2):
+            for way in range(2):
+                add_ring(kind, way, step)
+                reduce_copy(kind, way, step + 1).start()
+
+    steps = seq_bits + 2
+    for at in range(steps):
+        vec_send[at] = vec_now[...]
+        vec_copy(at).start()
+        if at < n - 2:
+            ring_step(at)
+        if at == 0:
+            near[0].wait_recv()
+            far_out[...] = (share_rows(far) + near_in[0].astype(f32)).astype(LOW)
+            far_copy.start()
+        vec_copy(at).wait_recv()
+        if at == seq_bits - 1:
+            total = vec_now[...] + vec_recv[at]
+            vec_now[...] = total
+            vec_out[8:16] = total[8:16]
+            vec_out[16:24] = total[0:8]
+        else:
+            vec_now[...] += vec_recv[at]
+    vec_out[0:8] = vec_now[0:8]
+
+    def ring_body(step, carry):
+        ring_step(step)
+        return carry
+
+    lax.fori_loop(min(steps, n - 2), n - 2, ring_body, 0)
+    for kind in range(2):
+        ring, out, _ = rings[kind]
+        for way in range(2):
+            add_ring(kind, way, n - 2)
+            out[way, chunk(spot - signs[way])] = ring[way, n - 1]
+            spread_copy(kind, way, 0).start()
+    near[1].wait_recv()
+    far_copy.wait_recv()
+    in_grad[...] = first[...] + share_rows(head) + near_in[1].astype(f32) + far_in[...].astype(f32)
+
+    def spread_body(step, carry):
+        for kind in range(2):
+            for way in range(2):
+                spread_copy(kind, way, step).wait_recv()
+                spread_copy(kind, way, step + 1).start()
+        return carry
+
+    lax.fori_loop(0, n - 2, spread_body, 0)
+    for kind in range(2):
+        for way in range(2):
+            spread_copy(kind, way, n - 2).wait_recv()
+
+    def close_body(step, carry):
+        for kind in range(2):
+            for way in range(2):
+                reduce_copy(kind, way, step).wait_send()
+                spread_copy(kind, way, step).wait_send()
+        return carry
+
+    lax.fori_loop(0, n - 1, close_body, 0)
+    for copy in copies + near + [far_copy] + [vec_copy(at) for at in range(steps)]:
+        copy.wait_send()
+
+
+def tail(hid, dq, dkv, qw, kw, vw, first, up_grad, down_grad, o_grad, vec):
+    n = lax.axis_size("seq")
+    tokens, width = hid.shape
+    share = first.shape[0]
+    pair = dkv.shape[1]
+    depth = 16 * (-(-width // (16 * n)))
+    rows = n * depth
+    f32 = jnp.float32
+    if rows > width:
+        up_grad = jnp.pad(up_grad, ((0, rows - width), (0, 0)))
+        down_grad = jnp.pad(down_grad, ((0, rows - width), (0, 0)))
+    steps = n.bit_length() + 1
+    return pl.pallas_call(
+        tail_kernel,
+        name="tail",
+        out_shape=(
+            jax.ShapeDtypeStruct((share, width), f32),
+            jax.ShapeDtypeStruct((2, rows, up_grad.shape[1]), LOW),
+            jax.ShapeDtypeStruct((2, rows, pair), LOW),
+            jax.ShapeDtypeStruct((24, width), f32),
+        ),
+        in_specs=[VM] * 11,
+        out_specs=(VM,) * 4,
+        scratch_shapes=[
+            pltpu.VMEM((6, tokens // 2, pair), LOW),
+            pltpu.VMEM((2, tokens // 2, pair), LOW),
+            pltpu.VMEM((tokens, width), f32),
+            pltpu.VMEM((2, rows, pair), LOW),
+            pltpu.VMEM((2, n, depth, up_grad.shape[1]), LOW),
+            pltpu.VMEM((2, n, depth, pair), LOW),
+            pltpu.VMEM((2, share, width), LOW),
+            pltpu.VMEM((2, share, width), LOW),
+            pltpu.VMEM((share, width), LOW),
+            pltpu.VMEM((share, width), LOW),
+            pltpu.VMEM((16, width), f32),
+            pltpu.VMEM((steps, 16, width), f32),
+            pltpu.VMEM((steps, 16, width), f32),
+            pltpu.SemaphoreType.DMA((9 + steps,)),
+            pltpu.SemaphoreType.DMA((9 + steps,)),
+            pltpu.SemaphoreType.DMA((2, 2, 2, n - 1)),
+            pltpu.SemaphoreType.DMA((2, 2, 2, n - 1)),
+        ],
+        compiler_params=pltpu.CompilerParams(
+            collective_id=2, has_side_effects=True, vmem_limit_bytes=48 << 20
+        ),
+    )(hid, dq, dkv, qw, kw, vw, first, up_grad, down_grad, o_grad, vec)
 
 
 def per_device(
@@ -269,100 +895,31 @@
     up_weight, up_bias, down_weight, down_bias, norm2_gain, norm2_shift, doc_mask, doc_blocks, rand_blocks,
     out_grad,
 ):
-    low = jnp.bfloat16
-    tok_dev = hidden_in.shape[0]
-    local_width = q_weight.shape[1]
-    share_rows = out_grad.shape[0]
-    slot_span = SLOT_LEN // tok_dev
-    group_bits = slot_span.bit_length() - 1
+    f32 = jnp.float32
+    tokens, width = hidden_in.shape
+    local = q_weight.shape[1]
+    slot_span = SLOT_LEN // tokens
     seq_index = lax.axis_index("seq")
-    head_index = lax.axis_index("head")
-    slot_place = seq_index % slot_span
     slot_index = seq_index // slot_span
-    scale = HD ** (-0.5)
-    query = ((dot_nn(hidden_in, q_weight) + q_bias).astype(low) * jnp.asarray(scale, low))
-    query = jnp.pad(query, ((0, 0), (0, 256 - local_width)))
-    kv_weight = jnp.concatenate([k_weight, v_weight], axis=1)
-    kv_bias = jnp.concatenate([jnp.zeros_like(v_bias), v_bias])
-    slot_pair = (dot_nn(hidden_in, kv_weight) + kv_bias).astype(low)
-    for bit_index in range(group_bits):
-        partner = partner_2(slot_pair, "seq", bit_index)
-        upper_half = seq_index // 2**bit_index % 2 == 1
-        slot_pair = jnp.where(
-            upper_half,
-            jnp.concatenate([partner, slot_pair], axis=0),
-            jnp.concatenate([slot_pair, partner], axis=0),
-        )
     slot_mask = lax.dynamic_slice_in_dim(doc_mask, slot_index * SLOT_LEN, SLOT_LEN, 0)
     count = jnp.minimum(jnp.sum(slot_mask), doc_blocks[slot_index] * BLOCK)
-    scal = jnp.stack([slot_place, count]).astype(jnp.int32)
+    scal = jnp.stack([seq_index % slot_span, count]).astype(jnp.int32)
     rand = rand_blocks.reshape(-1)
+    query, slot_pair, o_full = project(hidden_in, q_weight, k_weight, v_weight, q_bias, v_bias, o_weight)
     context, probs, wide_probs = attend_forward(scal, rand, query, slot_pair)
-    o_pad = jnp.concatenate([jnp.zeros((256 - local_width, o_weight.shape[1]), low), o_weight], axis=0)
-    attn_share = lax.psum_scatter(
-        dot_nn(context, o_pad).astype(low), "head", scatter_dimension=0, tiled=True
-    ).astype(jnp.float32)
-    token_share = lax.dynamic_slice_in_dim(hidden_in, head_index * share_rows, share_rows, 0)
-    first_sum = token_share.astype(jnp.float32) + attn_share + o_bias
-    normed_one, unit_one, inv_one = norm_forward(first_sum, norm1_gain, norm1_shift)
-    normed_low = lax.all_gather(normed_one.astype(low), "head", axis=0, tiled=True)
-    pre_act = dot_nn(normed_low, up_weight) + up_bias
-    act_low = jax.nn.gelu(pre_act, approximate=True).astype(low)
-    ffn_share = lax.psum_scatter(
-        dot_nn(act_low, down_weight).astype(low), "head", scatter_dimension=0, tiled=True
-    ).astype(jnp.float32)
-    second_sum = normed_one + ffn_share + down_bias
-    layer_out, unit_two, inv_two = norm_forward(second_sum, norm2_gain, norm2_shift)
-    second_grad, gain_two_grad, shift_two_grad = norm_backward(out_grad, unit_two, inv_two, norm2_gain)
-    down_bias_grad = jnp.sum(second_grad, axis=0)
-    second_low = lax.all_gather(second_grad.astype(low), "head", axis=0, tiled=True)
-    pre_grad = gelu_grad(pre_act, dot_nt(second_low, down_weight))
-    branch_grad = lax.psum_scatter(
-        dot_nt(pre_grad, up_weight).astype(low), "head", scatter_dimension=0, tiled=True
-    ).astype(jnp.float32)
-    down_grad = dot_tn(act_low, second_low)
-    up_grad = dot_tn(normed_low, pre_grad)
-    up_bias_grad = jnp.sum(pre_grad.astype(jnp.float32), axis=0)
-    first_grad, gain_one_grad, shift_one_grad = norm_backward(
-        second_grad + branch_grad, unit_one, inv_one, norm1_gain
-    )
-    o_bias_grad = jnp.sum(first_grad, axis=0)
-    first_full = lax.all_gather(first_grad.astype(low), "head", axis=0, tiled=True)
-    o_grad = dot_tn(context, first_full)[256 - local_width :]
-    d_ctx = dot_nt(first_full, o_pad).astype(low)
-    query_low, slot_grad = attend_backward(scal, rand, query, slot_pair, probs, wide_probs, d_ctx)
-    query_low = query_low[:, :local_width]
-    own_grad = slot_grad.astype(jnp.float32)
-    for bit_index in reversed(range(group_bits)):
-        half_len = own_grad.shape[0] // 2
-        upper_half = seq_index // 2**bit_index % 2 == 1
-        lower_part = own_grad[:half_len]
-        upper_part = own_grad[half_len:]
-        kept_half = jnp.where(upper_half, upper_part, lower_part)
-        given_half = jnp.where(upper_half, lower_part, upper_part)
-        own_grad = kept_half + partner_2(given_half.astype(low), "seq", bit_index).astype(jnp.float32)
-    kv_low = own_grad.astype(low)
-    q_grad = dot_tn(hidden_in, query_low)
-    q_bias_grad = jnp.sum(query_low.astype(jnp.float32), axis=0)
-    kv_grad = dot_tn(hidden_in, kv_low)
-    v_bias_grad = jnp.sum(kv_low[:, local_width:].astype(jnp.float32), axis=0)
-    in_grad = first_grad + lax.psum_scatter(
-        (dot_nt(query_low, q_weight) + dot_nt(kv_low, kv_weight)).astype(low),
-        "head", scatter_dimension=0, tiled=True,
-    ).astype(jnp.float32)
-    summed = lax.psum(
-        tuple(part.astype(low) for part in (q_grad, kv_grad, o_grad, up_grad, down_grad)), "seq"
-    )
-    summed = [part.astype(jnp.float32) for part in summed]
-    bias_sums = lax.psum((q_bias_grad, v_bias_grad, up_bias_grad), "seq")
-    norm_sums = lax.psum(
-        (o_bias_grad, gain_one_grad, shift_one_grad, down_bias_grad, gain_two_grad, shift_two_grad),
-        ("seq", "head"),
-    )
+    layer_out, first, d_ctx, up_part, down_part, o_part, vec = middle(
+        context, o_full, hidden_in, o_bias, norm1_gain, norm1_shift, up_weight, up_bias, down_weight,
+        down_bias, norm2_gain, norm2_shift, out_grad,
+    )
+    dq, dkv = attend_backward(scal, rand, query, slot_pair, probs, wide_probs, d_ctx)
+    in_grad, big, small, vecs = tail(
+        hidden_in, dq, dkv, q_weight, k_weight, v_weight, first, up_part, down_part, o_part, vec
+    )
+    small = small[:, :width].astype(f32)
     return (
-        layer_out, in_grad, summed[0], bias_sums[0], summed[1][:, :local_width], summed[1][:, local_width:],
-        bias_sums[1], summed[2], norm_sums[0], norm_sums[1], norm_sums[2], summed[3], bias_sums[2], summed[4],
-        norm_sums[3], norm_sums[4], norm_sums[5],
+        layer_out, in_grad, small[1, :, :local], vecs[8, :local], small[0, :, :local], small[0, :, local:],
+        vecs[9, local : 2 * local], small[1, :, local:].T, vecs[0], vecs[1], vecs[2],
+        big[0, :width].astype(f32), vecs[22], big[1, :width].astype(f32), vecs[3], vecs[4], vecs[5],
     )
 
 

time: 546 us -> 265 us (0.49)
  waiting for transfers between devices: 337 us -> 0 us
  Pallas kernels: 33.3 us -> 230 us
  blocking collectives: 66.1 us -> 0 us
  matrix products: 37.1 us -> 0 us
  other arithmetic: 30.9 us -> 5.16 us
  between operations: 16 us -> 2.18 us
  local copies, waits for them, and re-layouts: 19.2 us -> 27.8 us
  starting transfers between devices: 5.73 us -> 0 us
    pallas_call x0 -> x3, Pallas kernels: none -> 196 us  [the longest x1 105 us: tail(): pl.pallas_call(tail_kernel, name='tail', out_shape=(jax.ShapeDtypeStruct(...]
    ppermute x4 -> x0, waiting for transfers between devices: 102 us -> none  [partner_2(): return lax.ppermute(value, axis, pairs)]
    psum x1 -> x0, waiting for transfers between devices: 92.2 us -> none  [per_device(): lax.psum(tuple((part.astype(low) for part in (q_grad, kv_grad, o_grad, up...]
    reduce_scatter x4 -> x0, waiting for transfers between devices: 83.6 us -> none  [the longest x1 28.2 us: per_device(): lax.psum_scatter(dot_nt(pre_grad, up_weight).astype(low), 'head', scatter...]
    psum x2 -> x0, blocking collectives: 66.1 us -> none  [the longest x1 42.7 us: per_device(): lax.psum((o_bias_grad, gain_one_grad, shift_one_grad, down_bias_grad, gai...]
    all_gather x3 -> x0, waiting for transfers between devices: 59 us -> none  [the longest x1 19.7 us: per_device(): lax.all_gather(first_grad.astype(low), 'head', axis=0, tiled=True)]
    dot_general x15 -> x0, matrix products: 37.1 us -> none  [the longest x5 14.3 us: dot_nt(): lax.dot_general(left, right, (((1,), (1,)), ((), ())), preferred_element_...]
    reduce_sum x9 -> x0, other arithmetic: 8.01 us -> none  [the longest x2 2.74 us: norm_forward(): row_mean = jnp.mean(values_in, axis=1, keepdims=True)]
  transfers between devices with their start and end apart: 12 -> 0, of which waited for: 11 -> 0; matrix products, arithmetic and copies ran while one was open for 3% -> 0% of each run, Pallas kernels for 0% -> 0%
where the time goes in v2:
time: 265 us
  Pallas kernels  230 us (87%)
  local copies, waits for them, and re-layouts  27.8 us (10%)
  other arithmetic  5.16 us (2%)
    pallas_call x1, Pallas kernels, tail(): pl.pallas_call(tail_kernel, name='tail', out_shape=(jax.ShapeDtypeStruct(...  105 us
    pallas_call x1, Pallas kernels, middle(): pl.pallas_call(middle_kernel, name='middle', out_shape=(jax.ShapeDtypeStr...  59.3 us
    pallas_call x1, Pallas kernels, project(): pl.pallas_call(project_kernel, name='project_gather', out_shape=(jax.Shap...  31.7 us
    pallas_call x1, Pallas kernels, attend_backward(): pl.pallas_call(attend_bwd_kernel, name='attend_backward', out_shape=(jax....  20.6 us
    unnamed x40, local copies, waits for them, and re-layouts  19.7 us
    pallas_call x1, Pallas kernels, attend_forward(): pl.pallas_call(attend_fwd_kernel, name='attend_forward', out_shape=(jax.S...  12.9 us

profile of v2, /device:TPU:0, one launch (start us, length us, event | category | flops | bytes accessed | tf_op | source)
XLA Modules:
  0.0 264.9 jit_solution(3049405836304165513)
XLA Ops:
  0.7 1.4 dynamic_slice.7
  9.0 0.8 copy.48
  9.8 1.1 copy.49.qw
  10.9 1.1 copy.50.kw
  12.1 1.1 copy.51.vw
  14.6 31.7 %project_gather.1 = (bf16[1024,256]{1,0:T(8,128)(2,1)S(1)}, bf16[4096,384]{1,0:T(8,128)(2,1)S(1)}, bf16[4,192,768]{2,1,0:T(8,128)(2,1)S(1)}) custom-call(bf16[1024,768]{1,0:T(8,128)(2,1)S(1)} %copy-done.1, bf16[768,192]{1,0:T(8,128)(2,1)S(1)} %copy.49.qw, bf16[768,192]{1,0:T(8,128)(2,1)S(1)} %copy.50.kw, bf16[768,192]{1,0:T(8,128)(2,1)S(1)} %copy.51.vw, ...), custom_call_target="tpu_custom_call" | custom-call | tf_op jit(solution)/shard_map/project_gather/pallas_call | solution.py:328
  46.3 1.0 copy-done.6
  47.4 12.9 %attend_forward.1 = (bf16[1024,256]{1,0:T(8,128)(2,1)S(1)}, bf16[16,192,512]{2,1,0:T(8,128)(2,1)S(1)}, bf16[8,384,512]{2,1,0:T(8,128)(2,1)S(1)}) custom-call(s32[2]{0:T(128)S(1)} %pad_add_fusion.scal_ref, s32[48]{0:T(128)S(1)} %reshape.70.rand_ref, bf16[1024,256]{1,0:T(8,128)(2,1)S(1)} %get-tuple-element.36.q_ref, bf16[4096,384]{1,0:T(8,128)(2,1)S(1)} %get-tuple-element.37.kv_ref), custom_call_target="tpu_custom_call" | custom-call | tf_op jit(solution)/shard_map/attend_forward/pallas_call | solution.py:141
  60.3 1.7 copy-done.2
  61.9 59.3 %middle.1 = (f32[256,768]{1,0:T(8,128)S(1)}, f32[256,768]{1,0:T(8,128)S(1)}, bf16[1024,256]{1,0:T(8,128)(2,1)S(1)}, bf16[768,768]{1,0:T(8,128)(2,1)S(1)}, bf16[7...) custom-call(bf16[1024,256]{1,0:T(8,128)(2,1)S(1)} %get-tuple-element.38.ctx, ...), custom_call_target="tpu_custom_call" | custom-call | tf_op jit(solution)/shard_map/middle/pallas_call | solution.py:601
  121.3 1.0 copy-done.5
  122.3 0.9 copy-done.8
  123.1 1.9 copy-done.3
  125.0 20.6 %attend_backward.1 = (bf16[1024,256]{1,0:T(8,128)(2,1)S(1)}, bf16[4096,384]{1,0:T(8,128)(2,1)S(1)}) custom-call(s32[2]{0:T(128)S(1)} %pad_add_fusion.scal_ref, s32[48]{0:T(128)S(1)} %reshape.70.rand_ref, bf16[1024,256]{1,0:T(8,128)(2,1)S(1)} %get-tuple-element.36.q_ref, bf16[4096,384]{1,0:T(8,128)(2,1)S(1)} %get-tuple-element.37.kv_ref, ...), custom_call_target="tpu_custom_call" | custom-call | tf_op jit(solution)/shard_map/attend_backward/pallas_call | solution.py:224
  145.7 1.7 copy-done.4
  147.3 105.2 %tail.1 = (f32[256,768]{1,0:T(8,128)S(1)}, bf16[2,768,768]{2,1,0:T(8,128)(2,1)}, bf16[2,768,384]{2,1,0:T(8,128)(2,1)S(1)}, f32[24,768]{1,0:T(8,128)S(1)}) custom-call(bf16[1024,768]{1,0:T(8,128)(2,1)} %hid.5, bf16[1024,256]{1,0:T(8,128)(2,1)S(1)} %get-tuple-element.44.dq, bf16[4096,384]{1,0:T(8,128)(2,1)} %copy-done.4, bf16[768,192]{1,0:T(8,128)(2,1)S(1)} %copy.49.qw, ...), custom_call_target="tpu_custom_call" | custom-call | tf_op jit(solution)/shard_map/tail/pallas_call | solution.py:857
  252.5 0.7 fusion
  254.6 1.1 copy.58
  255.6 1.1 copy.57
  256.7 1.1 copy.56
  257.8 1.1 copy.55
  258.8 4.3 %bitcast_convert_fusion = (f32[768,768]{1,0:T(8,128)}, f32[768,768]{1,0:T(8,128)}) fusion(bf16[2,768,768]{2,1,0:T(8,128)(2,1)} %get-tuple-element.54), kind=kLoop, calls=%fused_computation | loop fusion | flops 1179648 | bytes 7077888 | tf_op jit(solution)/shard_map/convert_element_type | solution.py:922
  263.1 0.9 copy.61
  264.0 0.9 copy.62
  (37 shorter events, 8.3 us)
Async XLA Ops:
  0.7 2.1 copy-start
  0.7 12.5 %copy-start.1 = (bf16[1024,768]{1,0:T(8,128)(2,1)S(1)}, bf16[1024,768]{1,0:T(8,128)(2,1)}, u32[]{:S(2)}) copy-start(bf16[1024,768]{1,0:T(8,128)(2,1)} %hid.5) | copy-start | bytes 4718596
  0.7 12.5 %copy-start.12 = (bf16[192,768]{1,0:T(8,128)(2,1)S(1)}, bf16[192,768]{1,0:T(8,128)(2,1)}, u32[]{:S(2)}) copy-start(bf16[192,768]{1,0:T(8,128)(2,1)} %ow.1) | copy-start | bytes 884740
  13.2 0.7 copy-start.13
  13.9 0.7 copy-start.14
  46.3 1.0 copy-start.6
  47.4 14.6 %copy-start.7 = (f32[256,768]{1,0:T(8,128)S(1)}, f32[256,768]{1,0:T(8,128)}, u32[]{:S(2)}) copy-start(f32[256,768]{1,0:T(8,128)} %out_grad.1) | copy-start | bytes 2359300
  60.3 1.7 copy-start.2
  121.2 1.0 copy-start.5
  122.3 0.9 copy-start.8
  123.1 1.9 copy-start.3
  145.7 1.7 copy-start.4
  252.5 2.1 copy-start.10
  258.8 4.3 %copy-start.9 = (f32[256,768]{1,0:T(8,128)S(1)}, f32[256,768]{1,0:T(8,128)}, u32[]{:S(2)}) copy-start(f32[256,768]{1,0:T(8,128)} %copy-done.8) | copy-start | bytes 2359300
  258.8 5.2 %copy-start.11 = (f32[256,768]{1,0:T(8,128)S(1)}, f32[256,768]{1,0:T(8,128)}, u32[]{:S(2)}) copy-start(f32[256,768]{1,0:T(8,128)} %copy-done.10) | copy-start | bytes 2359300

commit v3 on v2

--- a/solution.py
+++ b/solution.py
@@ -44,8 +44,13 @@
     return total
 
 
-def window_ids(scal_ref, rand_ref, step, local_blocks):
-    place, count = scal_ref[0], scal_ref[1]
+def slot_spot(tokens):
+    spans = SLOT_LEN // tokens
+    seq = lax.axis_index("seq")
+    return seq % spans, seq // spans
+
+
+def window_ids(place, count, rand_ref, step, local_blocks):
     mine = place * local_blocks + step
     last = SLOT_LEN // BLOCK - 1
     ids, limits = [], []
@@ -56,7 +61,7 @@
         ids.append(at)
         limits.append(jnp.where(good, jnp.clip(count - at * BLOCK, 0, BLOCK), 0))
     for slot in range(3):
-        at = rand_ref[step * 3 + slot]
+        at = rand_ref[slot, step]
         ids.append(at)
         limits.append(jnp.clip(count - at * BLOCK, 0, BLOCK))
     for at in (0, 1):
@@ -70,13 +75,16 @@
     return jnp.concatenate(parts, axis=0)
 
 
-def attend_fwd_kernel(scal_ref, rand_ref, q_ref, kv_ref, ctx_ref, p_ref, pg_ref, wide_ref):
+def attend_fwd_kernel(blocks_ref, rand_ref, mask_ref, q_ref, kv_ref, ctx_ref, p_ref, pg_ref, wide_ref):
     local_blocks = q_ref.shape[0] // BLOCK
-    place, count = scal_ref[0], scal_ref[1]
+    place, slot = slot_spot(q_ref.shape[0])
+    lines = SLOT_LEN // mask_ref.shape[1]
+    marked = jnp.sum(mask_ref[pl.ds(pl.multiple_of(slot * lines, lines), lines), :])
+    count = jnp.minimum(marked, blocks_ref[slot] * BLOCK)
     half = lax.broadcasted_iota(jnp.int32, (1, 128), 1)
 
     def one_block(step):
-        ids, limits = window_ids(scal_ref, rand_ref, step, local_blocks)
+        ids, limits = window_ids(place, count, rand_ref, step, local_blocks)
         rows = pl.ds(pl.multiple_of(step * BLOCK, BLOCK), BLOCK)
         q_all = spread_heads(q_ref[rows, :], 0)
         raw = dot_nt(q_all, take_blocks(kv_ref, ids, 0))
@@ -133,7 +141,7 @@
     lax.fori_loop(jnp.where(place == 0, 1, 0), local_blocks // 2, pair, 0)
 
 
-def attend_forward(scal, rand, q_rows, kv_slot):
+def attend_forward(doc_blocks, rand, doc_mask, q_rows, kv_slot):
     tokens = q_rows.shape[0]
     blocks = tokens // BLOCK
     vmem = pl.BlockSpec(memory_space=pltpu.VMEM)
@@ -146,16 +154,16 @@
             jax.ShapeDtypeStruct((blocks, 3 * BLOCK, WIN * BLOCK), jnp.bfloat16),
             jax.ShapeDtypeStruct((SLOT_LEN // (WIN * BLOCK), 6 * BLOCK, WIN * BLOCK), jnp.bfloat16),
         ),
-        in_specs=[smem, smem, vmem, vmem],
+        in_specs=[smem, smem, vmem, vmem, vmem],
         out_specs=(vmem, vmem, vmem),
         scratch_shapes=[pltpu.VMEM((SLOT_LEN // (WIN * BLOCK), 6 * BLOCK, WIN * BLOCK), jnp.float32)],
-        compiler_params=pltpu.CompilerParams(vmem_limit_bytes=40 << 20),
-    )(scal, rand, q_rows, kv_slot)
-
-
-def attend_bwd_kernel(scal_ref, rand_ref, q_ref, kv_ref, p_ref, pg_ref, do_ref, dq_ref, dkv_ref, acc_ref):
+        compiler_params=pltpu.CompilerParams(vmem_limit_bytes=16 << 20),
+    )(doc_blocks, rand, doc_mask, q_rows, kv_slot)
+
+
+def attend_bwd_kernel(rand_ref, q_ref, kv_ref, p_ref, pg_ref, do_ref, dq_ref, dkv_ref, acc_ref):
     local_blocks = q_ref.shape[0] // BLOCK
-    place = scal_ref[0]
+    place, _ = slot_spot(q_ref.shape[0])
     scale = HD ** (-0.5)
     acc_ref[...] = jnp.zeros_like(acc_ref)
 
@@ -166,7 +174,7 @@
         acc_ref[where_at, 256:384] += d_value[:, 128:256]
 
     def one_block(step):
-        ids, _ = window_ids(scal_ref, rand_ref, step, local_blocks)
+        ids, _ = window_ids(place, 0, rand_ref, step, local_blocks)
         rows = pl.ds(pl.multiple_of(step * BLOCK, BLOCK), BLOCK)
         q_all = spread_heads(q_ref[rows, :], 0)
         do_all = spread_heads(do_ref[rows, :], 1)
@@ -217,7 +225,7 @@
     dkv_ref[...] = acc_ref[...].astype(jnp.bfloat16)
 
 
-def attend_backward(scal, rand, q_rows, kv_slot, probs, wide_probs, d_ctx):
+def attend_backward(rand, q_rows, kv_slot, probs, wide_probs, d_ctx):
     tokens = q_rows.shape[0]
     vmem = pl.BlockSpec(memory_space=pltpu.VMEM)
     smem = pl.BlockSpec(memory_space=pltpu.SMEM)
@@ -228,11 +236,11 @@
             jax.ShapeDtypeStruct((tokens, 256), jnp.bfloat16),
             jax.ShapeDtypeStruct((SLOT_LEN, 384), jnp.bfloat16),
         ),
-        in_specs=[smem, smem] + [vmem] * 5,
+        in_specs=[smem] + [vmem] * 5,
         out_specs=(vmem, vmem),
         scratch_shapes=[pltpu.VMEM((SLOT_LEN, 384), jnp.float32)],
-        compiler_params=pltpu.CompilerParams(vmem_limit_bytes=40 << 20),
-    )(scal, rand, q_rows, kv_slot, probs, wide_probs, d_ctx)
+        compiler_params=pltpu.CompilerParams(vmem_limit_bytes=16 << 20),
+    )(rand, q_rows, kv_slot, probs, wide_probs, d_ctx)
 
 
 MESH = pl.DeviceIdType.MESH
@@ -283,8 +291,8 @@
 
     def fill(part):
         rows = hid[part * half : (part + 1) * half, :]
-        keys = dot_nn(rows, kw[...])
-        values = dot_nn(rows, vw[...]) + vb[...]
+        keys = dot_nt(rows, kw[...])
+        values = dot_nt(rows, vw[...]) + vb[...][None, :]
         at = pl.multiple_of(place * tokens + part * half, half)
         kv_out[pl.ds(at, half), :] = jnp.concatenate([keys.astype(LOW), values.astype(LOW)], axis=1)
 
@@ -305,7 +313,7 @@
         copies[at].start()
     for part in range(2):
         rows = hid[part * half : (part + 1) * half, :]
-        query = (dot_nn(rows, qw[...]) + qb[...]).astype(LOW) * jnp.asarray(HD ** (-0.5), LOW)
+        query = (dot_nt(rows, qw[...]) + qb[...][None, :]).astype(LOW) * jnp.asarray(HD ** (-0.5), LOW)
         query = jnp.concatenate([query, jnp.zeros((half, 256 - query.shape[1]), LOW)], axis=1)
         q_out[part * half : (part + 1) * half, :] = query
     copies[0].wait_recv()
@@ -330,16 +338,16 @@
         name="project_gather",
         out_shape=(
             jax.ShapeDtypeStruct((tokens, 256), LOW),
-            jax.ShapeDtypeStruct((SLOT_LEN, 2 * kw.shape[1]), LOW),
+            jax.ShapeDtypeStruct((SLOT_LEN, 2 * kw.shape[0]), LOW),
             jax.ShapeDtypeStruct((heads, ow.shape[0], width), LOW),
         ),
         in_specs=[VM] * 7,
         out_specs=(VM,) * 3,
         scratch_shapes=[pltpu.SemaphoreType.DMA((9,)), pltpu.SemaphoreType.DMA((9,))],
         compiler_params=pltpu.CompilerParams(
-            collective_id=0, has_side_effects=True, vmem_limit_bytes=32 << 20
+            collective_id=0, has_side_effects=True, vmem_limit_bytes=12 << 20
         ),
-    )(hid, qw, kw, vw, qb.reshape(1, -1), vb.reshape(1, -1), ow)
+    )(hid, qw, kw, vw, qb, vb, ow)
 
 
 def norm_fwd(values, gain, shift):
@@ -377,7 +385,10 @@
     share = out_grad.shape[0]
     rows = share // CHUNKS
     width = hid.shape[1]
-    seq, head = lax.axis_index("seq"), lax.axis_index("head")
+    head = lax.axis_index("head")
+    o_bias, gain1, shift1, up_b, down_b, gain2, shift2 = (
+        ref[...][None, :] for ref in (o_bias, gain1, shift1, up_b, down_b, gain2, shift2)
+    )
     core, far, both = flip(head, 0), flip(head, 1), flip(flip(head, 0), 1)
     order = (head, core, far, both)
     greet(tuple({"head": at} for at in order[1:]))
@@ -486,7 +497,7 @@
             term = dot_nn(rows_at, weight)
             attn = term if attn is None else attn + term
         token = hid[block_rows(head, part), :].astype(jnp.float32)
-        normed_f, unit_f, inv_f = norm_fwd(token + attn + o_bias[...], gain1[...], shift1[...])
+        normed_f, unit_f, inv_f = norm_fwd(token + attn + o_bias, gain1, shift1)
         normed[own_rows(part)] = normed_f
         unit1[own_rows(part)] = unit_f
         inv1[own_rows(part)] = inv_f
@@ -494,7 +505,7 @@
         x_gather.start(part)
 
     def ffn_forward(part, at):
-        pre = dot_nn(x_gather.pair(part, at), up_w[...]) + up_b[...]
+        pre = dot_nn(x_gather.pair(part, at), up_w[...]) + up_b
         square = pre * pre
         tanh = jnp.tanh(ROOT * (pre + CUBE * square * pre))
         slope[part, at] = 0.5 * (1.0 + tanh) + (0.5 * ROOT) * pre * (1.0 - tanh * tanh) * (
@@ -508,11 +519,11 @@
 
     gain2_sum, shift2_sum, down_sum = 0.0, 0.0, 0.0
     for part in range(CHUNKS):
-        total = normed[own_rows(part)] + ffn_scatter.result(part) + down_b[...]
-        out, unit_f, inv_f = norm_fwd(total, gain2[...], shift2[...])
+        total = normed[own_rows(part)] + ffn_scatter.result(part) + down_b
+        out, unit_f, inv_f = norm_fwd(total, gain2, shift2)
         layer_out[own_rows(part)] = out
         grad = out_grad[own_rows(part)]
-        second_f = norm_bwd(grad, unit_f, inv_f, gain2[...])
+        second_f = norm_bwd(grad, unit_f, inv_f, gain2)
         second[own_rows(part)] = second_f
         s_all[part, 0] = second_f.astype(LOW)
         s_gather.start(part)
@@ -548,7 +559,7 @@
     for part in range(CHUNKS):
         grad = second[own_rows(part)] + branch_scatter.result(part)
         unit_f = unit1[own_rows(part)]
-        first_f = norm_bwd(grad, unit_f, inv1[own_rows(part)], gain1[...])
+        first_f = norm_bwd(grad, unit_f, inv1[own_rows(part)], gain1)
         first_out[own_rows(part)] = first_f
         f_all[part, 0] = first_f.astype(LOW)
         f_gather.start(part)
@@ -569,7 +580,7 @@
         second_ctx = ctx[block_rows(order[2 * at + 1], part), :]
         d_ctx[block_rows(order[2 * at], part), :] = grad[:rows]
         d_ctx[block_rows(order[2 * at + 1], part), :] = grad[rows:]
-        return dot_tn(rows_f, jnp.concatenate([first_ctx, second_ctx], axis=0))
+        return dot_tn(jnp.concatenate([first_ctx, second_ctx], axis=0), rows_f)
 
     o_total = 0.0
     for part in range(CHUNKS):
@@ -580,7 +591,7 @@
     for part in range(CHUNKS):
         f_gather.relay[part].wait_recv()
         o_total += back(part, 1)
-    o_grad[...] = o_total
+    o_grad[...] = o_total[256 - o_grad.shape[0] :].astype(LOW)
     zero = jnp.zeros((1, width), jnp.float32)
     vec[...] = jnp.concatenate(
         [o_sum, gain1_sum, shift1_sum, down_sum, gain2_sum, shift2_sum, bias_sum[0], zero], axis=0
@@ -593,9 +604,8 @@
     tokens, width = hid.shape
     share = out_grad.shape[0]
     rows = share // CHUNKS
-    hidden = up_w.shape[1]
+    hidden, local = up_w.shape[1], o_full.shape[1]
     f32 = jnp.float32
-    line = lambda value: value.reshape(1, -1)
     gathered = pltpu.VMEM((CHUNKS, 4, rows, width), LOW)
     copies = CHUNKS * (3 + 3 * 3 + 2 * 3)
     return pl.pallas_call(
@@ -607,7 +617,7 @@
             jax.ShapeDtypeStruct((tokens, 256), LOW),
             jax.ShapeDtypeStruct((width, hidden), LOW),
             jax.ShapeDtypeStruct((hidden, width), LOW),
-            jax.ShapeDtypeStruct((width, 256), f32),
+            jax.ShapeDtypeStruct((local, width), LOW),
             jax.ShapeDtypeStruct((8, width), f32),
         ),
         in_specs=[VM] * 13,
@@ -633,11 +643,10 @@
             pltpu.SemaphoreType.DMA((copies,)),
         ],
         compiler_params=pltpu.CompilerParams(
-            collective_id=1, has_side_effects=True, vmem_limit_bytes=48 << 20
+            collective_id=1, has_side_effects=True, vmem_limit_bytes=30 << 20
         ),
     )(
-        ctx, o_full, hid, line(o_bias), line(gain1), line(shift1), up_w, line(up_b), down_w, line(down_b),
-        line(gain2), line(shift2), out_grad,
+        ctx, o_full, hid, o_bias, gain1, shift1, up_w, up_b, down_w, down_b, gain2, shift2, out_grad
     )
 
 
@@ -650,7 +659,7 @@
     n = lax.axis_size("seq")
     tokens, width = hid.shape
     half, share = tokens // 2, first.shape[0]
-    depth = big_ring.shape[2]
+    depths = (big_ring.shape[2], small_ring.shape[2])
     spans = SLOT_LEN // tokens
     seq, head = lax.axis_index("seq"), lax.axis_index("head")
     place = seq % spans
@@ -687,8 +696,9 @@
     for at in range(4):
         copies[at].start()
 
-    gap = jnp.zeros((width, 256 - qw.shape[1]), LOW)
-    partial[...] = dot_nt(dq[...], jnp.concatenate([qw[...], gap], axis=1))
+    local = qw.shape[0]
+    gap = jnp.zeros((256 - local, width), LOW)
+    partial[...] = dot_nn(dq[...], jnp.concatenate([qw[...], gap], axis=0))
     copies[0].wait_recv()
     pair_out[0] = (dkv[rows_of(x_at, 0), :].astype(f32) + pair_in[0].astype(f32)).astype(LOW)
     copies[4].start()
@@ -698,8 +708,8 @@
 
     rings = ((big_ring, big_out, (up_grad, down_grad)), (small_ring, small_out, (small.at[0], small.at[1])))
 
-    def chunk(pos):
-        return pl.ds(pl.multiple_of(((pos + 2 * n) % n) * depth, 16), depth)
+    def chunk(kind, pos):
+        return pl.ds(pl.multiple_of(((pos + 2 * n) % n) * depths[kind], 16), depths[kind])
 
     def reduce_copy(kind, way, step):
         ring = rings[kind][0]
@@ -710,7 +720,7 @@
         )
 
     def spread_copy(kind, way, step):
-        rows = rings[kind][1].at[way, chunk(spot + signs[way] * (step - 1))]
+        rows = rings[kind][1].at[way, chunk(kind, spot + signs[way] * (step - 1))]
         return pltpu.make_async_remote_copy(
             src_ref=rows, dst_ref=rows,
             send_sem=ring_send.at[1, kind, way, step], recv_sem=ring_recv.at[1, kind, way, step],
@@ -720,22 +730,21 @@
     def open_ring(kind):
         ring, _, source = rings[kind]
         for way in range(2):
-            ring[way, 0] = source[way][chunk(spot), :]
+            ring[way, 0] = source[way][chunk(kind, spot), :]
             reduce_copy(kind, way, 0).start()
 
     def add_ring(kind, way, step):
         ring, _, source = rings[kind]
         reduce_copy(kind, way, step).wait_recv()
-        mine = source[way][chunk(spot + signs[way] * (step + 1)), :]
+        mine = source[way][chunk(kind, spot + signs[way] * (step + 1)), :]
         ring[way, step + 1] = (ring[way, step + 1].astype(f32) + mine.astype(f32)).astype(LOW)
 
     open_ring(0)
-    q_part = dot_tn(hid[...], dq[...])
-    small[1, 0:width, 0:128] = q_part[:, 0:128].astype(LOW)
-    small[1, 0:width, 128:256] = (q_part[:, 128:256] + o_grad[:, 0:128]).astype(LOW)
-    small[1, 0:width, 256:384] = o_grad[:, 128:256].astype(LOW)
-    if n * depth > width:
-        small[:, width:, :] = jnp.zeros((2, n * depth - width, small.shape[2]), LOW)
+    small[1, 0:local] = dot_tn(dq[...], hid[...])[0:local].astype(LOW)
+    small[1, local : 2 * local] = o_grad[...]
+    spare = small.shape[1] - 2 * local
+    if spare:
+        small[:, 2 * local :] = jnp.zeros((2, spare, width), LOW)
     for at in range(2, 6):
         copies[at].wait_recv()
     own = []
@@ -744,10 +753,10 @@
         first_in, second_in = (3, 4) if part == 0 else (2, 5)
         own.append((mine + pair_in[first_in].astype(f32) + pair_in[second_in].astype(f32)).astype(LOW))
     own = jnp.concatenate(own, axis=0)
-    small[0, 0:width, :] = dot_tn(hid[...], own).astype(LOW)
+    small[0, 0 : 2 * local] = dot_tn(own, hid[...]).astype(LOW)
     open_ring(1)
-    partial[...] += dot_nt(own[:, 0:256], jnp.concatenate([kw[...], gap], axis=1)) + dot_nt(
-        own[:, 128:384], jnp.concatenate([gap, vw[...]], axis=1)
+    partial[...] += dot_nn(own[:, 0:256], jnp.concatenate([kw[...], gap], axis=0)) + dot_nn(
+        own[:, 128:384], jnp.concatenate([gap, vw[...]], axis=0)
     )
 
     def share_rows(owner):
@@ -812,7 +821,7 @@
         ring, out, _ = rings[kind]
         for way in range(2):
             add_ring(kind, way, n - 2)
-            out[way, chunk(spot - signs[way])] = ring[way, n - 1]
+            out[way, chunk(kind, spot - signs[way])] = ring[way, n - 1]
             spread_copy(kind, way, 0).start()
     near[1].wait_recv()
     far_copy.wait_recv()
@@ -847,7 +856,7 @@
     tokens, width = hid.shape
     share = first.shape[0]
     pair = dkv.shape[1]
-    depth = 16 * (-(-width // (16 * n)))
+    depth, less = 16 * (-(-width // (16 * n))), 16 * (-(-pair // (16 * n)))
     rows = n * depth
     f32 = jnp.float32
     if rows > width:
@@ -860,7 +869,7 @@
         out_shape=(
             jax.ShapeDtypeStruct((share, width), f32),
             jax.ShapeDtypeStruct((2, rows, up_grad.shape[1]), LOW),
-            jax.ShapeDtypeStruct((2, rows, pair), LOW),
+            jax.ShapeDtypeStruct((2, n * less, width), LOW),
             jax.ShapeDtypeStruct((24, width), f32),
         ),
         in_specs=[VM] * 11,
@@ -869,9 +878,9 @@
             pltpu.VMEM((6, tokens // 2, pair), LOW),
             pltpu.VMEM((2, tokens // 2, pair), LOW),
             pltpu.VMEM((tokens, width), f32),
-            pltpu.VMEM((2, rows, pair), LOW),
+            pltpu.VMEM((2, n * less, width), LOW),
             pltpu.VMEM((2, n, depth, up_grad.shape[1]), LOW),
-            pltpu.VMEM((2, n, depth, pair), LOW),
+            pltpu.VMEM((2, n, less, width), LOW),
             pltpu.VMEM((2, share, width), LOW),
             pltpu.VMEM((2, share, width), LOW),
             pltpu.VMEM((share, width), LOW),
@@ -885,7 +894,7 @@
             pltpu.SemaphoreType.DMA((2, 2, 2, n - 1)),
         ],
         compiler_params=pltpu.CompilerParams(
-            collective_id=2, has_side_effects=True, vmem_limit_bytes=48 << 20
+            collective_id=2, has_side_effects=True, vmem_limit_bytes=28 << 20
         ),
     )(hid, dq, dkv, qw, kw, vw, first, up_grad, down_grad, o_grad, vec)
 
@@ -898,28 +907,26 @@
     f32 = jnp.float32
     tokens, width = hidden_in.shape
     local = q_weight.shape[1]
-    slot_span = SLOT_LEN // tokens
-    seq_index = lax.axis_index("seq")
-    slot_index = seq_index // slot_span
-    slot_mask = lax.dynamic_slice_in_dim(doc_mask, slot_index * SLOT_LEN, SLOT_LEN, 0)
-    count = jnp.minimum(jnp.sum(slot_mask), doc_blocks[slot_index] * BLOCK)
-    scal = jnp.stack([seq_index % slot_span, count]).astype(jnp.int32)
-    rand = rand_blocks.reshape(-1)
-    query, slot_pair, o_full = project(hidden_in, q_weight, k_weight, v_weight, q_bias, v_bias, o_weight)
-    context, probs, wide_probs = attend_forward(scal, rand, query, slot_pair)
+    rand = rand_blocks.T
+    qw, kw, vw = q_weight.T, k_weight.T, v_weight.T
+    query, slot_pair, o_full = project(hidden_in, qw, kw, vw, q_bias, v_bias, o_weight)
+    context, probs, wide_probs = attend_forward(
+        doc_blocks, rand, doc_mask.reshape(-1, 128), query, slot_pair
+    )
     layer_out, first, d_ctx, up_part, down_part, o_part, vec = middle(
         context, o_full, hidden_in, o_bias, norm1_gain, norm1_shift, up_weight, up_bias, down_weight,
         down_bias, norm2_gain, norm2_shift, out_grad,
     )
-    dq, dkv = attend_backward(scal, rand, query, slot_pair, probs, wide_probs, d_ctx)
+    dq, dkv = attend_backward(rand, query, slot_pair, probs, wide_probs, d_ctx)
     in_grad, big, small, vecs = tail(
-        hidden_in, dq, dkv, q_weight, k_weight, v_weight, first, up_part, down_part, o_part, vec
-    )
-    small = small[:, :width].astype(f32)
+        hidden_in, dq, dkv, qw, kw, vw, first, up_part, down_part, o_part, vec
+    )
+    small = small.astype(f32)
     return (
-        layer_out, in_grad, small[1, :, :local], vecs[8, :local], small[0, :, :local], small[0, :, local:],
-        vecs[9, local : 2 * local], small[1, :, local:].T, vecs[0], vecs[1], vecs[2],
-        big[0, :width].astype(f32), vecs[22], big[1, :width].astype(f32), vecs[3], vecs[4], vecs[5],
+        layer_out, in_grad, small[1, :local].T, vecs[8, :local], small[0, :local].T,
+        small[0, local : 2 * local].T, vecs[9, local : 2 * local], small[1, local : 2 * local],
+        vecs[0], vecs[1], vecs[2], big[0, :width].astype(f32), vecs[22], big[1, :width].astype(f32),
+        vecs[3], vecs[4], vecs[5],
     )
 
 

time: 265 us -> 238 us (0.90)
  local copies, waits for them, and re-layouts: 27.8 us -> 11.2 us
  Pallas kernels: 230 us -> 222 us
    unnamed x40 -> x50, local copies, waits for them, and re-layouts: 19.7 us -> 8.47 us
    reshape x8 -> x0, local copies, waits for them, and re-layouts: 4.91 us -> none  [the longest x7 4.82 us: middle(): line = lambda value: value.reshape(1, -1)]
    pallas_call x1, Pallas kernels: 105 us -> 101 us  [tail(): pl.pallas_call(tail_kernel, name='tail', out_shape=(jax.ShapeDtypeStruct(...]
    pallas_call x1, Pallas kernels: 59.3 us -> 55.9 us  [middle(): pl.pallas_call(middle_kernel, name='middle', out_shape=(jax.ShapeDtypeStr...]
where the time goes in v3:
time: 238 us; the launch traced here: 237 us
  Pallas kernels  222 us (93%)
  local copies, waits for them, and re-layouts  11.2 us (5%)
  other arithmetic  2.71 us (1%)
    pallas_call x1, Pallas kernels, tail(): pl.pallas_call(tail_kernel, name='tail', out_shape=(jax.ShapeDtypeStruct(...  101 us
    pallas_call x1, Pallas kernels, middle(): pl.pallas_call(middle_kernel, name='middle', out_shape=(jax.ShapeDtypeStr...  55.9 us
    pallas_call x1, Pallas kernels, project(): pl.pallas_call(project_kernel, name='project_gather', out_shape=(jax.Shap...  31.8 us
    pallas_call x1, Pallas kernels, attend_backward(): pl.pallas_call(attend_bwd_kernel, name='attend_backward', out_shape=(jax....  20.5 us
    pallas_call x1, Pallas kernels, attend_forward(): pl.pallas_call(attend_fwd_kernel, name='attend_forward', out_shape=(jax.S...  13.1 us
    unnamed x50, local copies, waits for them, and re-layouts  8.47 us

profile of v3, /device:TPU:0, one launch (start us, length us, event | category | flops | bytes accessed | tf_op | source)
XLA Modules:
  0.0 237.3 jit_solution(7885728168560565221)
XLA Ops:
  0.7 0.0 copy-start
  0.7 1.4 copy-done
  2.1 1.0 copy-done.2
  3.1 1.0 copy-done.4
  4.0 1.0 copy-done.6
  5.0 1.0 copy-done.11
  5.9 0.7 copy-done.21
  6.6 0.7 copy-done.22
  7.3 31.8 %project_gather.1 = (bf16[1024,256]{1,0:T(8,128)(2,1)S(1)}, bf16[4096,384]{1,0:T(8,128)(2,1)S(1)}, bf16[4,192,768]{2,1,0:T(8,128)(2,1)S(1)}) custom-call(bf16[1024,768]{1,0:T(8,128)(2,1)S(1)} %copy-done, bf16[192,768]{1,0:T(8,128)(2,1)S(1)} %bitcast.27, bf16[192,768]{1,0:T(8,128)(2,1)S(1)} %bitcast.29, bf16[192,768]{1,0:T(8,128)(2,1)S(1)} %bitcast.31, ...), custom_call_target="tpu_custom_call" | custom-call | tf_op jit(solution)/shard_map/project_gather/pallas_call | solution.py:336
  39.1 0.0 copy-start.8
  39.1 0.0 copy-start.10
  39.1 0.0 copy-start.16
  39.2 0.0 copy-start.17
  39.2 13.1 %attend_forward.1 = (bf16[1024,256]{1,0:T(8,128)(2,1)S(1)}, bf16[16,192,512]{2,1,0:T(8,128)(2,1)S(1)}, bf16[8,384,512]{2,1,0:T(8,128)(2,1)S(1)}) custom-call(s32[2]{0:T(128)S(1)} %copy-done.23, s32[3,16]{1,0:T(4,128)S(1)} %bitcast.34, s32[64,128]{1,0:T(8,128)S(1)} %bitcast.33, bf16[1024,256]{1,0:T(8,128)(2,1)S(1)} %get-tuple-element.36.q_ref, ...), custom_call_target="tpu_custom_call" | custom-call | tf_op jit(solution)/shard_map/attend_forward/pallas_call | solution.py:149
  52.4 55.9 %middle.1 = (f32[256,768]{1,0:T(8,128)S(1)}, f32[256,768]{1,0:T(8,128)S(1)}, bf16[1024,256]{1,0:T(8,128)(2,1)S(1)}, bf16[768,768]{1,0:T(8,128)(2,1)S(1)}, bf16[7...) custom-call(bf16[1024,256]{1,0:T(8,128)(2,1)S(1)} %get-tuple-element.38.ctx, ...), custom_call_target="tpu_custom_call" | custom-call | tf_op jit(solution)/shard_map/middle/pallas_call | solution.py:611
  108.4 20.5 %attend_backward.1 = (bf16[1024,256]{1,0:T(8,128)(2,1)S(1)}, bf16[4096,384]{1,0:T(8,128)(2,1)S(1)}) custom-call(s32[3,16]{1,0:T(4,128)S(1)} %bitcast.35, bf16[1024,256]{1,0:T(8,128)(2,1)S(1)} %get-tuple-element.36.q_ref, bf16[4096,384]{1,0:T(8,128)(2,1)S(1)} %get-tuple-element.37.kv_ref, bf16[16,192,512]{2,1,0:T(8,128)(2,1)S(1)} %get-tuple-element.41.p_ref, ...), custom_call_target="tpu_custom_call" | custom-call | tf_op jit(solution)/shard_map/attend_backward/pallas_call | solution.py:232
  128.9 101.1 %tail.1 = (f32[256,768]{1,0:T(8,128)S(1)}, bf16[2,768,768]{2,1,0:T(8,128)(2,1)S(1)}, bf16[2,384,768]{2,1,0:T(8,128)(2,1)S(1)}, f32[24,768]{1,0:T(8,128)S(1)}) custom-call(bf16[1024,768]{1,0:T(8,128)(2,1)S(1)} %copy-done.1, bf16[1024,256]{1,0:T(8,128)(2,1)S(1)} %get-tuple-element.44.dq, bf16[4096,384]{1,0:T(8,128)(2,1)S(1)} %get-tuple-element.45.dkv, ...), custom_call_target="tpu_custom_call" | custom-call | tf_op jit(solution)/shard_map/tail/pallas_call | solution.py:866
  230.1 0.6 fusion
  230.7 0.7 slice_reduce_fusion
  231.3 0.2 convert_element_type.15
  231.5 1.4 slice_bitcast_fusion
  233.0 2.5 %bitcast_convert_fusion = (f32[768,768]{1,0:T(8,128)}, f32[768,768]{1,0:T(8,128)}) fusion(bf16[2,768,768]{2,1,0:T(8,128)(2,1)S(1)} %get-tuple-element.54), kind=kLoop, calls=%fused_computation | loop fusion | flops 1179648 | bytes 7077888 | tf_op jit(solution)/shard_map/convert_element_type | solution.py:928
  235.5 0.9 copy.39
  236.4 0.9 copy.40
  (36 shorter events, 0.1 us)
Async XLA Ops:
  0.7 38.5 %copy-start.13 = (s32[16,3]{0,1:T(4,128)S(1)}, s32[16,3]{0,1:T(4,128)}, u32[]{:S(2)}) copy-start(s32[16,3]{0,1:T(4,128)} %param.38) | copy-start | bytes 580
  0.7 38.5 %copy-start.23 = (s32[2]{0:T(128)S(1)}, s32[2]{0:T(128)}, u32[]{:S(2)}) copy-start(s32[2]{0:T(128)} %blocks_ref.1) | copy-start | bytes 28
  0.7 1.4 copy-start
  2.1 1.0 copy-start.2
  3.1 1.0 copy-start.4
  4.0 1.0 copy-start.6
  5.0 1.0 copy-start.11
  5.9 0.7 copy-start.21
  6.6 0.7 copy-start.22
  7.3 31.9 %copy-start.12 = (s32[8192]{0:T(1024)S(1)}, s32[8192]{0:T(1024)}, u32[]{:S(2)}) copy-start(s32[8192]{0:T(1024)} %param.36) | copy-start | bytes 98308
  7.3 45.0 %copy-start.9 = (bf16[768,768]{1,0:T(8,128)(2,1)S(1)}, bf16[768,768]{1,0:T(8,128)(2,1)}, u32[]{:S(2)}) copy-start(bf16[768,768]{1,0:T(8,128)(2,1)} %down_w.1) | copy-start | bytes 3538948
  39.1 13.2 %copy-start.1 = (bf16[1024,768]{1,0:T(8,128)(2,1)S(1)}, bf16[1024,768]{1,0:T(8,128)(2,1)}, u32[]{:S(2)}) copy-start(bf16[1024,768]{1,0:T(8,128)(2,1)} %hid.5) | copy-start | bytes 4718596
  39.1 13.2 %copy-start.8 = (bf16[768,768]{1,0:T(8,128)(2,1)S(1)}, bf16[768,768]{1,0:T(8,128)(2,1)}, u32[]{:S(2)}) copy-start(bf16[768,768]{1,0:T(8,128)(2,1)} %up_w.1) | copy-start | bytes 3538948
  39.1 13.2 %copy-start.10 = (f32[256,768]{1,0:T(8,128)S(1)}, f32[256,768]{1,0:T(8,128)}, u32[]{:S(2)}) copy-start(f32[256,768]{1,0:T(8,128)} %out_grad.1) | copy-start | bytes 2359300
  39.1 13.2 %copy-start.14 = (f32[768]{0:T(1024)S(1)}, f32[768]{0:T(1024)}, u32[]{:S(2)}) copy-start(f32[768]{0:T(1024)} %o_bias.1) | copy-start | bytes 9220
  39.1 13.2 %copy-start.15 = (f32[768]{0:T(1024)S(1)}, f32[768]{0:T(1024)}, u32[]{:S(2)}) copy-start(f32[768]{0:T(1024)} %gain1.1) | copy-start | bytes 9220
  39.1 13.2 %copy-start.16 = (f32[768]{0:T(1024)S(1)}, f32[768]{0:T(1024)}, u32[]{:S(2)}) copy-start(f32[768]{0:T(1024)} %shift1.1) | copy-start | bytes 9220
  39.2 13.2 %copy-start.17 = (f32[768]{0:T(1024)S(1)}, f32[768]{0:T(1024)}, u32[]{:S(2)}) copy-start(f32[768]{0:T(1024)} %up_b.1) | copy-start | bytes 9220
  39.2 13.2 %copy-start.18 = (f32[768]{0:T(1024)S(1)}, f32[768]{0:T(1024)}, u32[]{:S(2)}) copy-start(f32[768]{0:T(1024)} %down_b.1) | copy-start | bytes 9220
  39.2 13.2 %copy-start.19 = (f32[768]{0:T(1024)S(1)}, f32[768]{0:T(1024)}, u32[]{:S(2)}) copy-start(f32[768]{0:T(1024)} %gain2.1) | copy-start | bytes 9220
  39.2 13.2 %copy-start.20 = (f32[768]{0:T(1024)S(1)}, f32[768]{0:T(1024)}, u32[]{:S(2)}) copy-start(f32[768]{0:T(1024)} %shift2.1) | copy-start | bytes 9220
  108.3 20.5 %copy-start.3 = (bf16[768,192]{0,1:T(8,128)(2,1)S(1)}, bf16[768,192]{0,1:T(8,128)(2,1)}, u32[]{:S(2)}) copy-start(bf16[768,192]{0,1:T(8,128)(2,1)} %param.21) | copy-start | bytes 884740
  108.3 20.5 %copy-start.5 = (bf16[768,192]{0,1:T(8,128)(2,1)S(1)}, bf16[768,192]{0,1:T(8,128)(2,1)}, u32[]{:S(2)}) copy-start(bf16[768,192]{0,1:T(8,128)(2,1)} %param.23) | copy-start | bytes 884740
  108.4 20.5 %copy-start.7 = (bf16[768,192]{0,1:T(8,128)(2,1)S(1)}, bf16[768,192]{0,1:T(8,128)(2,1)}, u32[]{:S(2)}) copy-start(bf16[768,192]{0,1:T(8,128)(2,1)} %param.24) | copy-start | bytes 884740

commit v4 on v3

--- a/solution.py
+++ b/solution.py
@@ -75,15 +75,22 @@
     return jnp.concatenate(parts, axis=0)
 
 
-def attend_fwd_kernel(blocks_ref, rand_ref, mask_ref, q_ref, kv_ref, ctx_ref, p_ref, pg_ref, wide_ref):
+def attend_fwd_kernel(blocks_ref, rand_ref, mask_ref, q_ref, kv_ref, ctx_ref, p_ref, pg_ref, wide_ctx_ref, link_ref, wide_ref):
     local_blocks = q_ref.shape[0] // BLOCK
     place, slot = slot_spot(q_ref.shape[0])
     lines = SLOT_LEN // mask_ref.shape[1]
     marked = jnp.sum(mask_ref[pl.ds(pl.multiple_of(slot * lines, lines), lines), :])
     count = jnp.minimum(marked, blocks_ref[slot] * BLOCK)
     half = lax.broadcasted_iota(jnp.int32, (1, 128), 1)
+    slot_blocks = SLOT_LEN // BLOCK
+    for at in range(slot_blocks + 3 * local_blocks):
+        link_ref[at] = 3 * local_blocks
 
     def one_block(step):
+        for slot in range(3):
+            owner = rand_ref[slot, step]
+            link_ref[slot_blocks + step * 3 + slot] = link_ref[owner]
+            link_ref[owner] = step * 3 + slot
         ids, limits = window_ids(place, count, rand_ref, step, local_blocks)
         rows = pl.ds(pl.multiple_of(step * BLOCK, BLOCK), BLOCK)
         q_all = spread_heads(q_ref[rows, :], 0)
@@ -131,7 +138,13 @@
             return out + dot_nn(probs, kv_ref[pl.ds(at, chunk), 128:384])
 
         out = lax.fori_loop(0, parts, scan_out, jnp.zeros((rows_all, 256), jnp.float32))
-        ctx_ref[0 : 2 * BLOCK, :] = fold_heads(out, 1).astype(jnp.bfloat16)
+        folded = fold_heads(out, 1)
+        wide_ctx_ref[...] = folded
+        ctx_ref[0 : 2 * BLOCK, :] = folded.astype(jnp.bfloat16)
+
+    @pl.when(place != 0)
+    def _():
+        wide_ctx_ref[...] = jnp.zeros_like(wide_ctx_ref)
 
     def pair(at, carry):
         one_block(2 * at)
@@ -153,94 +166,14 @@
             jax.ShapeDtypeStruct((tokens, 256), jnp.bfloat16),
             jax.ShapeDtypeStruct((blocks, 3 * BLOCK, WIN * BLOCK), jnp.bfloat16),
             jax.ShapeDtypeStruct((SLOT_LEN // (WIN * BLOCK), 6 * BLOCK, WIN * BLOCK), jnp.bfloat16),
+            jax.ShapeDtypeStruct((2 * BLOCK, 256), jnp.float32),
+            jax.ShapeDtypeStruct((SLOT_LEN // BLOCK + 3 * blocks,), jnp.int32),
         ),
         in_specs=[smem, smem, vmem, vmem, vmem],
-        out_specs=(vmem, vmem, vmem),
+        out_specs=(vmem,) * 4 + (smem,),
         scratch_shapes=[pltpu.VMEM((SLOT_LEN // (WIN * BLOCK), 6 * BLOCK, WIN * BLOCK), jnp.float32)],
         compiler_params=pltpu.CompilerParams(vmem_limit_bytes=16 << 20),
     )(doc_blocks, rand, doc_mask, q_rows, kv_slot)
-
-
-def attend_bwd_kernel(rand_ref, q_ref, kv_ref, p_ref, pg_ref, do_ref, dq_ref, dkv_ref, acc_ref):
-    local_blocks = q_ref.shape[0] // BLOCK
-    place, _ = slot_spot(q_ref.shape[0])
-    scale = HD ** (-0.5)
-    acc_ref[...] = jnp.zeros_like(acc_ref)
-
-    def add_rows(at, size, d_key, d_value):
-        where_at = pl.ds(pl.multiple_of(at, BLOCK), size)
-        acc_ref[where_at, 0:128] += d_key[:, 0:128]
-        acc_ref[where_at, 128:256] += d_key[:, 128:256] + d_value[:, 0:128]
-        acc_ref[where_at, 256:384] += d_value[:, 128:256]
-
-    def one_block(step):
-        ids, _ = window_ids(place, 0, rand_ref, step, local_blocks)
-        rows = pl.ds(pl.multiple_of(step * BLOCK, BLOCK), BLOCK)
-        q_all = spread_heads(q_ref[rows, :], 0)
-        do_all = spread_heads(do_ref[rows, :], 1)
-        probs = p_ref[step]
-        d_prob = dot_nt(do_all, take_blocks(kv_ref, ids, 128))
-        wide = probs.astype(jnp.float32)
-        mean = jnp.sum(d_prob * wide, axis=1, keepdims=True)
-        d_score = (wide * (d_prob - mean)).astype(jnp.bfloat16)
-        dq = dot_nn(d_score, take_blocks(kv_ref, ids, 0))
-        dq_ref[rows, :] = (fold_heads(dq, 0) * scale).astype(jnp.bfloat16)
-        d_key = dot_tn(d_score, q_all)
-        d_value = dot_tn(probs, do_all)
-        for slot in range(WIN):
-            cut = slice(slot * BLOCK, (slot + 1) * BLOCK)
-            add_rows(ids[slot] * BLOCK, BLOCK, d_key[cut], d_value[cut])
-
-    @pl.when(place == 0)
-    def _():
-        chunk = WIN * BLOCK
-        parts = SLOT_LEN // chunk
-        q_all = spread_heads(q_ref[0 : 2 * BLOCK, :], 0)
-        do_all = spread_heads(do_ref[0 : 2 * BLOCK, :], 1)
-
-        def scan_mean(part, mean):
-            at = pl.multiple_of(part * chunk, chunk)
-            d_prob = dot_nt(do_all, kv_ref[pl.ds(at, chunk), 128:384])
-            return mean + jnp.sum(d_prob * pg_ref[part].astype(jnp.float32), axis=1, keepdims=True)
-
-        mean = lax.fori_loop(0, parts, scan_mean, jnp.zeros((q_all.shape[0], 1), jnp.float32))
-
-        def scan_grad(part, dq):
-            at = pl.multiple_of(part * chunk, chunk)
-            probs = pg_ref[part]
-            d_prob = dot_nt(do_all, kv_ref[pl.ds(at, chunk), 128:384])
-            d_score = (probs.astype(jnp.float32) * (d_prob - mean)).astype(jnp.bfloat16)
-            add_rows(at, chunk, dot_tn(d_score, q_all), dot_tn(probs, do_all))
-            return dq + dot_nn(d_score, kv_ref[pl.ds(at, chunk), 0:256])
-
-        dq = lax.fori_loop(0, parts, scan_grad, jnp.zeros((q_all.shape[0], 256), jnp.float32))
-        dq_ref[0 : 2 * BLOCK, :] = (fold_heads(dq, 0) * scale).astype(jnp.bfloat16)
-
-    def pair(at, carry):
-        one_block(2 * at)
-        one_block(2 * at + 1)
-        return carry
-
-    lax.fori_loop(jnp.where(place == 0, 1, 0), local_blocks // 2, pair, 0)
-    dkv_ref[...] = acc_ref[...].astype(jnp.bfloat16)
-
-
-def attend_backward(rand, q_rows, kv_slot, probs, wide_probs, d_ctx):
-    tokens = q_rows.shape[0]
-    vmem = pl.BlockSpec(memory_space=pltpu.VMEM)
-    smem = pl.BlockSpec(memory_space=pltpu.SMEM)
-    return pl.pallas_call(
-        attend_bwd_kernel,
-        name="attend_backward",
-        out_shape=(
-            jax.ShapeDtypeStruct((tokens, 256), jnp.bfloat16),
-            jax.ShapeDtypeStruct((SLOT_LEN, 384), jnp.bfloat16),
-        ),
-        in_specs=[smem] + [vmem] * 5,
-        out_specs=(vmem, vmem),
-        scratch_shapes=[pltpu.VMEM((SLOT_LEN, 384), jnp.float32)],
-        compiler_params=pltpu.CompilerParams(vmem_limit_bytes=16 << 20),
-    )(rand, q_rows, kv_slot, probs, wide_probs, d_ctx)
 
 
 MESH = pl.DeviceIdType.MESH
@@ -267,9 +200,11 @@
     pl.semaphore_wait(barrier, len(partners))
 
 
-def project_kernel(hid, qw, kw, vw, qb, vb, ow, q_out, kv_out, o_out, send, recv):
+def project_kernel(hid, weights, biases, q_out, kv_out, o_out, send, recv):
     tokens = hid.shape[0]
     half = tokens // 2
+    local = weights.shape[0] // 4
+    qw, kw, vw, ow = (weights.at[pl.ds(at * local, local)] for at in range(4))
     seq, head = lax.axis_index("seq"), lax.axis_index("head")
     spans = SLOT_LEN // tokens
     place = seq % spans
@@ -292,7 +227,7 @@
     def fill(part):
         rows = hid[part * half : (part + 1) * half, :]
         keys = dot_nt(rows, kw[...])
-        values = dot_nt(rows, vw[...]) + vb[...][None, :]
+        values = dot_nt(rows, vw[...]) + biases[1:2, :]
         at = pl.multiple_of(place * tokens + part * half, half)
         kv_out[pl.ds(at, half), :] = jnp.concatenate([keys.astype(LOW), values.astype(LOW)], axis=1)
 
@@ -313,7 +248,7 @@
         copies[at].start()
     for part in range(2):
         rows = hid[part * half : (part + 1) * half, :]
-        query = (dot_nt(rows, qw[...]) + qb[...][None, :]).astype(LOW) * jnp.asarray(HD ** (-0.5), LOW)
+        query = (dot_nt(rows, qw[...]) + biases[0:1, :]).astype(LOW) * jnp.asarray(HD ** (-0.5), LOW)
         query = jnp.concatenate([query, jnp.zeros((half, 256 - query.shape[1]), LOW)], axis=1)
         q_out[part * half : (part + 1) * half, :] = query
     copies[0].wait_recv()
@@ -330,24 +265,24 @@
         copy.wait_send()
 
 
-def project(hid, qw, kw, vw, qb, vb, ow):
+def project(hid, weights, biases):
     tokens, width = hid.shape
-    heads = lax.axis_size("head")
+    heads, local = lax.axis_size("head"), weights.shape[0] // 4
     return pl.pallas_call(
         project_kernel,
         name="project_gather",
         out_shape=(
             jax.ShapeDtypeStruct((tokens, 256), LOW),
-            jax.ShapeDtypeStruct((SLOT_LEN, 2 * kw.shape[0]), LOW),
-            jax.ShapeDtypeStruct((heads, ow.shape[0], width), LOW),
+            jax.ShapeDtypeStruct((SLOT_LEN, 2 * local), LOW),
+            jax.ShapeDtypeStruct((heads, local, width), LOW),
         ),
-        in_specs=[VM] * 7,
+        in_specs=[VM] * 3,
         out_specs=(VM,) * 3,
         scratch_shapes=[pltpu.SemaphoreType.DMA((9,)), pltpu.SemaphoreType.DMA((9,))],
         compiler_params=pltpu.CompilerParams(
             collective_id=0, has_side_effects=True, vmem_limit_bytes=12 << 20
         ),
-    )(hid, qw, kw, vw, qb, vb, ow)
+    )(hid, weights, biases)
 
 
 def norm_fwd(values, gain, shift):
@@ -371,7 +306,7 @@
     return jnp.sum(values, axis=0, keepdims=True)
 
 
-CHUNKS = 2
+CHUNKS = 4
 ROOT = 0.7978845608028654
 CUBE = 0.044715
 
@@ -651,15 +586,15 @@
 
 
 def tail_kernel(
-    hid, dq, dkv, qw, kw, vw, first, up_grad, down_grad, o_grad, vec,
-    in_grad, big_out, small_out, vec_out,
-    pair_in, pair_out, partial, small, big_ring, small_ring, near_out, near_in, far_out, far_in,
+    rand, links, q_rows, kv, probs, wide_probs, wide_ctx, d_ctx, hid, weights, first, up_grad, down_grad, o_grad,
+    vec, in_grad, big_out, small_out, vec_out,
+    dq, acc, loose, wide_dq, wide_mean, pair_send, pair_in, pair_out, partial, small, big_ring, small_ring, near_out, near_in, far_out, far_in,
     vec_now, vec_send, vec_recv, send, recv, ring_send, ring_recv,
 ):
     n = lax.axis_size("seq")
     tokens, width = hid.shape
     half, share = tokens // 2, first.shape[0]
-    depths = (big_ring.shape[2], small_ring.shape[2])
+    depths = (big_ring.shape[3], big_ring.shape[3], small_ring.shape[2])
     spans = SLOT_LEN // tokens
     seq, head = lax.axis_index("seq"), lax.axis_index("head")
     place = seq % spans
@@ -685,28 +620,16 @@
 
     x_at, z_at = flip(place, 0), flip(place, 1)
     d_at = flip(x_at, 1)
-    copies = [
-        remote(dkv.at[rows_of(d_at, 0)], pair_in.at[0], send, recv, 0, by_z),
-        remote(dkv.at[rows_of(d_at, 1)], pair_in.at[1], send, recv, 1, by_x),
-        remote(dkv.at[rows_of(x_at, 1)], pair_in.at[2], send, recv, 2, by_x),
-        remote(dkv.at[rows_of(z_at, 0)], pair_in.at[3], send, recv, 3, by_z),
-        remote(pair_out.at[0], pair_in.at[4], send, recv, 4, by_x),
-        remote(pair_out.at[1], pair_in.at[5], send, recv, 5, by_z),
-    ]
-    for at in range(4):
-        copies[at].start()
-
-    local = qw.shape[0]
-    gap = jnp.zeros((256 - local, width), LOW)
-    partial[...] = dot_nn(dq[...], jnp.concatenate([qw[...], gap], axis=0))
-    copies[0].wait_recv()
-    pair_out[0] = (dkv[rows_of(x_at, 0), :].astype(f32) + pair_in[0].astype(f32)).astype(LOW)
-    copies[4].start()
-    copies[1].wait_recv()
-    pair_out[1] = (dkv[rows_of(z_at, 1), :].astype(f32) + pair_in[1].astype(f32)).astype(LOW)
-    copies[5].start()
-
-    rings = ((big_ring, big_out, (up_grad, down_grad)), (small_ring, small_out, (small.at[0], small.at[1])))
+
+    side_cols = up_grad.shape[1] // 2
+    left, right, full = pl.ds(0, side_cols), pl.ds(side_cols, side_cols), pl.ds(0, width)
+    pair_of = (up_grad, down_grad)
+    rings = (
+        (big_ring.at[0], big_out, pair_of, left),
+        (big_ring.at[1], big_out, pair_of, right),
+        (small_ring, small_out, (small.at[0], small.at[1]), full),
+    )
+    kinds = len(rings)
 
     def chunk(kind, pos):
         return pl.ds(pl.multiple_of(((pos + 2 * n) % n) * depths[kind], 16), depths[kind])
@@ -720,7 +643,7 @@
         )
 
     def spread_copy(kind, way, step):
-        rows = rings[kind][1].at[way, chunk(kind, spot + signs[way] * (step - 1))]
+        rows = rings[kind][1].at[way, chunk(kind, spot + signs[way] * (step - 1)), rings[kind][3]]
         return pltpu.make_async_remote_copy(
             src_ref=rows, dst_ref=rows,
             send_sem=ring_send.at[1, kind, way, step], recv_sem=ring_recv.at[1, kind, way, step],
@@ -728,18 +651,161 @@
         )
 
     def open_ring(kind):
-        ring, _, source = rings[kind]
+        ring, _, source, cols = rings[kind]
         for way in range(2):
-            ring[way, 0] = source[way][chunk(kind, spot), :]
+            ring[way, 0] = source[way][chunk(kind, spot), cols]
             reduce_copy(kind, way, 0).start()
 
     def add_ring(kind, way, step):
-        ring, _, source = rings[kind]
+        ring, _, source, cols = rings[kind]
         reduce_copy(kind, way, step).wait_recv()
-        mine = source[way][chunk(kind, spot + signs[way] * (step + 1)), :]
+        mine = source[way][chunk(kind, spot + signs[way] * (step + 1)), cols]
         ring[way, step + 1] = (ring[way, step + 1].astype(f32) + mine.astype(f32)).astype(LOW)
 
     open_ring(0)
+    open_ring(1)
+    local_blocks = tokens // BLOCK
+    chunk_rows = WIN * BLOCK
+    turns = local_blocks // 2
+    assert turns == SLOT_LEN // chunk_rows
+    scale = HD ** (-0.5)
+    acc[...] = jnp.zeros_like(acc)
+    loose[:, 3 * local_blocks] = jnp.zeros((3, BLOCK, 128), f32)
+
+    def add_rows(at, size, d_key, d_value):
+        where_at = pl.ds(pl.multiple_of(at, BLOCK), size)
+        acc[0, where_at] += d_key[:, 0:128]
+        acc[1, where_at] += d_key[:, 128:256] + d_value[:, 0:128]
+        acc[2, where_at] += d_value[:, 128:256]
+
+    def acc_rows(owner, part):
+        first_block = owner * local_blocks + part * (local_blocks // 2)
+        blocks = []
+        for more in range(local_blocks // 2):
+            block = first_block + more
+            here = pl.ds(pl.multiple_of(block * BLOCK, BLOCK), BLOCK)
+            there = links[block]
+            blocks.append(jnp.concatenate([acc[at, here] + loose[at, there] for at in range(3)], axis=1))
+        return jnp.concatenate(blocks, axis=0)
+
+    def pick_blocks(ids, low):
+        return jnp.concatenate([kv[at, :, low : low + 256] for at in ids], axis=0)
+
+    def wide_rows(at, low):
+        return kv[pl.ds(at * WIN, WIN), :, low : low + 256].reshape(chunk_rows, 256)
+
+    def one_block(step):
+        near = [(place * local_blocks + step + shift + SLOT_LEN // BLOCK) % (SLOT_LEN // BLOCK) for shift in (-1, 0, 1)]
+        ids = near + [rand[slot, step] for slot in range(3)] + [0, 1]
+        rows = pl.ds(pl.multiple_of(step * BLOCK, BLOCK), BLOCK)
+        q_all = spread_heads(q_rows[rows, :], 0)
+        do_all = spread_heads(d_ctx[rows, :], 1)
+        low_probs = probs[step]
+        d_prob = dot_nt(do_all, pick_blocks(ids, 128))
+        wide = low_probs.astype(f32)
+        mean = jnp.sum(d_prob * wide, axis=1, keepdims=True)
+        d_score = (wide * (d_prob - mean)).astype(LOW)
+        dq[rows, :] = (fold_heads(dot_nn(d_score, pick_blocks(ids, 0)), 0) * scale).astype(LOW)
+        d_key = dot_tn(d_score, q_all)
+        d_value = dot_tn(low_probs, do_all)
+        for slot in (0, 1, 2, 6, 7):
+            cut = slice(slot * BLOCK, (slot + 1) * BLOCK)
+            add_rows(ids[slot] * BLOCK, BLOCK, d_key[cut], d_value[cut])
+        for slot in range(3):
+            cut = slice((3 + slot) * BLOCK, (4 + slot) * BLOCK)
+            to = step * 3 + slot
+            old = links[SLOT_LEN // BLOCK + to]
+            loose[0, to] = d_key[cut, 0:128] + loose[0, old]
+            loose[1, to] = d_key[cut, 128:256] + d_value[cut, 0:128] + loose[1, old]
+            loose[2, to] = d_value[cut, 128:256] + loose[2, old]
+
+    @pl.when(place == 0)
+    def _():
+        wide_dq[...] = jnp.zeros_like(wide_dq)
+        product = d_ctx[0 : 2 * BLOCK, :].astype(f32) * wide_ctx[...]
+        lane = lax.broadcasted_iota(jnp.int32, (1, 256), 1) // HD
+        wide_mean[...] = jnp.concatenate(
+            [jnp.sum(jnp.where(lane == 1 + at, product, 0.0), axis=1, keepdims=True) for at in range(3)], axis=0
+        )
+
+    def reduce_step(kind, step):
+        for way in range(2):
+            add_ring(kind, way, step)
+            reduce_copy(kind, way, step + 1).start()
+
+    def turn(at, carry):
+        @pl.when(place == 0)
+        def _():
+            q_all = spread_heads(q_rows[0 : 2 * BLOCK, :], 0)
+            do_all = spread_heads(d_ctx[0 : 2 * BLOCK, :], 1)
+            from_row = pl.multiple_of(at * chunk_rows, chunk_rows)
+            low_probs = wide_probs[at]
+            d_prob = dot_nt(do_all, wide_rows(at, 128))
+            d_score = (low_probs.astype(f32) * (d_prob - wide_mean[...])).astype(LOW)
+            add_rows(from_row, chunk_rows, dot_tn(d_score, q_all), dot_tn(low_probs, do_all))
+            wide_dq[...] += dot_nn(d_score, wide_rows(at, 0))
+
+        @pl.when(at < n - 2)
+        def _():
+            reduce_step(0, at)
+
+        @pl.when(jnp.logical_or(place != 0, at != 0))
+        def _():
+            one_block(2 * at)
+            one_block(2 * at + 1)
+
+        @pl.when(at < n - 2)
+        def _():
+            reduce_step(1, at)
+
+        return carry
+
+    lax.fori_loop(0, turns, turn, 0)
+
+    @pl.when(place == 0)
+    def _():
+        dq[0 : 2 * BLOCK, :] = (fold_heads(wide_dq[...], 0) * scale).astype(LOW)
+
+    sends = ((d_at, 0, by_z), (d_at, 1, by_x), (x_at, 1, by_x), (z_at, 0, by_z))
+    copies = []
+    for at, (owner, part, where_to) in enumerate(sends):
+        pair_send[at] = acc_rows(owner, part).astype(LOW)
+        copies.append(remote(pair_send.at[at], pair_in.at[at], send, recv, at, where_to))
+        copies[-1].start()
+    copies.append(remote(pair_out.at[0], pair_in.at[4], send, recv, 4, by_x))
+    copies.append(remote(pair_out.at[1], pair_in.at[5], send, recv, 5, by_z))
+
+    def late_ring(step, carry):
+        reduce_step(0, step)
+        reduce_step(1, step)
+        return carry
+
+    lax.fori_loop(min(turns, n - 2), n - 2, late_ring, 0)
+
+    def open_spread(kind):
+        ring, out, _, cols = rings[kind]
+        for way in range(2):
+            add_ring(kind, way, n - 2)
+            out[way, chunk(kind, spot - signs[way]), cols] = ring[way, n - 1]
+            spread_copy(kind, way, 0).start()
+
+    def spread_step(kind, step):
+        for way in range(2):
+            spread_copy(kind, way, step).wait_recv()
+            spread_copy(kind, way, step + 1).start()
+
+    open_spread(0)
+    open_spread(1)
+    local = weights.shape[0] // 4
+    qw, kw, vw = (weights.at[pl.ds(at * local, local)] for at in range(3))
+    gap = jnp.zeros((256 - local, width), LOW)
+    partial[...] = dot_nn(dq[...], jnp.concatenate([qw[...], gap], axis=0))
+    copies[0].wait_recv()
+    pair_out[0] = (acc_rows(x_at, 0) + pair_in[0].astype(f32)).astype(LOW)
+    copies[4].start()
+    copies[1].wait_recv()
+    pair_out[1] = (acc_rows(z_at, 1) + pair_in[1].astype(f32)).astype(LOW)
+    copies[5].start()
     small[1, 0:local] = dot_tn(dq[...], hid[...])[0:local].astype(LOW)
     small[1, local : 2 * local] = o_grad[...]
     spare = small.shape[1] - 2 * local
@@ -749,32 +815,39 @@
         copies[at].wait_recv()
     own = []
     for part in range(2):
-        mine = dkv[rows_of(place, part), :].astype(f32)
+        mine = acc_rows(place, part)
         first_in, second_in = (3, 4) if part == 0 else (2, 5)
         own.append((mine + pair_in[first_in].astype(f32) + pair_in[second_in].astype(f32)).astype(LOW))
     own = jnp.concatenate(own, axis=0)
     small[0, 0 : 2 * local] = dot_tn(own, hid[...]).astype(LOW)
-    open_ring(1)
-    partial[...] += dot_nn(own[:, 0:256], jnp.concatenate([kw[...], gap], axis=0)) + dot_nn(
-        own[:, 128:384], jnp.concatenate([gap, vw[...]], axis=0)
-    )
+    open_ring(2)
 
     def share_rows(owner):
         return partial[pl.ds(pl.multiple_of(owner * share, share), share), :]
 
-    near_out[0] = share_rows(both).astype(LOW)
-    near_out[1] = share_rows(core).astype(LOW)
     near = [remote(near_out.at[at], near_in.at[at], send, recv, 6 + at, {"head": core}) for at in range(2)]
-    near[0].start()
-    near[1].start()
+
+    def key_term():
+        partial[...] += dot_nn(own[:, 0:256], jnp.concatenate([kw[...], gap], axis=0))
+
+    def value_term():
+        partial[...] += dot_nn(own[:, 128:384], jnp.concatenate([gap, vw[...]], axis=0))
+
+    def send_near():
+        for at, owner in enumerate((both, core)):
+            near_out[at] = share_rows(owner).astype(LOW)
+            near[at].start()
+
+    def send_far():
+        near[0].wait_recv()
+        far_out[...] = (share_rows(far) + near_in[0].astype(f32)).astype(LOW)
+        far_copy.start()
+
+    tasks = [key_term, value_term, send_near, send_far]
+    fill_row = lambda rows: jnp.concatenate([rows, jnp.zeros((1, width - rows.shape[1]), f32)], axis=1)
     sums = jnp.concatenate(
         [
-            jnp.concatenate(
-                [column_sum(dq[...].astype(f32)), jnp.zeros((1, width - dq.shape[1]), f32)], axis=1
-            ),
-            jnp.concatenate(
-                [column_sum(own.astype(f32)), jnp.zeros((1, width - own.shape[1]), f32)], axis=1
-            ),
+            fill_row(column_sum(dq[...].astype(f32))), fill_row(column_sum(own.astype(f32))),
             jnp.zeros((6, width), f32),
         ],
         axis=0,
@@ -786,61 +859,65 @@
     def vec_copy(at):
         return remote(vec_send.at[at], vec_recv.at[at], send, recv, 9 + at, vec_peers[at])
 
-    def ring_step(step):
-        for kind in range(2):
-            for way in range(2):
-                add_ring(kind, way, step)
-                reduce_copy(kind, way, step + 1).start()
-
     steps = seq_bits + 2
-    for at in range(steps):
+
+    def vec_start(at):
         vec_send[at] = vec_now[...]
         vec_copy(at).start()
-        if at < n - 2:
-            ring_step(at)
-        if at == 0:
-            near[0].wait_recv()
-            far_out[...] = (share_rows(far) + near_in[0].astype(f32)).astype(LOW)
-            far_copy.start()
+
+    def vec_finish(at):
         vec_copy(at).wait_recv()
+        total = vec_now[...] + vec_recv[at]
+        vec_now[...] = total
         if at == seq_bits - 1:
-            total = vec_now[...] + vec_recv[at]
-            vec_now[...] = total
             vec_out[8:16] = total[8:16]
             vec_out[16:24] = total[0:8]
-        else:
-            vec_now[...] += vec_recv[at]
-    vec_out[0:8] = vec_now[0:8]
+        if at == steps - 1:
+            vec_out[0:8] = total[0:8]
+
+    spread_done = 0
+    vec_start(0)
+    for at in range(min(steps, n - 2)):
+        reduce_step(2, at)
+        spread_step(at % 2, at // 2)
+        if at < len(tasks):
+            tasks[at]()
+        vec_finish(at)
+        if at + 1 < steps:
+            vec_start(at + 1)
 
     def ring_body(step, carry):
-        ring_step(step)
+        reduce_step(2, step)
         return carry
 
-    lax.fori_loop(min(steps, n - 2), n - 2, ring_body, 0)
-    for kind in range(2):
-        ring, out, _ = rings[kind]
-        for way in range(2):
-            add_ring(kind, way, n - 2)
-            out[way, chunk(kind, spot - signs[way])] = ring[way, n - 1]
-            spread_copy(kind, way, 0).start()
+    lax.fori_loop(steps, n - 2, ring_body, 0)
+    open_spread(2)
     near[1].wait_recv()
     far_copy.wait_recv()
     in_grad[...] = first[...] + share_rows(head) + near_in[1].astype(f32) + far_in[...].astype(f32)
-
-    def spread_body(step, carry):
-        for kind in range(2):
-            for way in range(2):
-                spread_copy(kind, way, step).wait_recv()
-                spread_copy(kind, way, step + 1).start()
+    done_left, done_right = (steps + 1) // 2, steps // 2
+
+    def spread_all(step, carry):
+        spread_step(0, step + done_left)
+        spread_step(2, step)
+        spread_step(1, step + done_left)
         return carry
 
-    lax.fori_loop(0, n - 2, spread_body, 0)
-    for kind in range(2):
+    def spread_last(step, carry):
+        spread_step(2, step)
+        return carry
+
+    for step in range(done_right, done_left):
+        spread_step(1, step)
+    rest = n - 2 - done_left
+    lax.fori_loop(0, rest, spread_all, 0)
+    lax.fori_loop(rest, n - 2, spread_last, 0)
+    for kind in range(kinds):
         for way in range(2):
             spread_copy(kind, way, n - 2).wait_recv()
 
     def close_body(step, carry):
-        for kind in range(2):
+        for kind in range(kinds):
             for way in range(2):
                 reduce_copy(kind, way, step).wait_send()
                 spread_copy(kind, way, step).wait_send()
@@ -851,11 +928,11 @@
         copy.wait_send()
 
 
-def tail(hid, dq, dkv, qw, kw, vw, first, up_grad, down_grad, o_grad, vec):
+def tail(rand, links, q_rows, kv, probs, wide_probs, wide_ctx, d_ctx, hid, weights, first, up_grad, down_grad, o_grad, vec):
     n = lax.axis_size("seq")
     tokens, width = hid.shape
     share = first.shape[0]
-    pair = dkv.shape[1]
+    pair = kv.shape[2]
     depth, less = 16 * (-(-width // (16 * n))), 16 * (-(-pair // (16 * n)))
     rows = n * depth
     f32 = jnp.float32
@@ -872,14 +949,20 @@
             jax.ShapeDtypeStruct((2, n * less, width), LOW),
             jax.ShapeDtypeStruct((24, width), f32),
         ),
-        in_specs=[VM] * 11,
+        in_specs=[pl.BlockSpec(memory_space=pltpu.SMEM)] * 2 + [VM] * 13,
         out_specs=(VM,) * 4,
         scratch_shapes=[
+            pltpu.VMEM((tokens, 256), LOW),
+            pltpu.VMEM((3, SLOT_LEN, 128), f32),
+            pltpu.VMEM((3, 3 * tokens // BLOCK + 1, BLOCK, 128), f32),
+            pltpu.VMEM((6 * BLOCK, 256), f32),
+            pltpu.VMEM((6 * BLOCK, 1), f32),
+            pltpu.VMEM((4, tokens // 2, pair), LOW),
             pltpu.VMEM((6, tokens // 2, pair), LOW),
             pltpu.VMEM((2, tokens // 2, pair), LOW),
             pltpu.VMEM((tokens, width), f32),
             pltpu.VMEM((2, n * less, width), LOW),
-            pltpu.VMEM((2, n, depth, up_grad.shape[1]), LOW),
+            pltpu.VMEM((2, 2, n, depth, up_grad.shape[1] // 2), LOW),
             pltpu.VMEM((2, n, less, width), LOW),
             pltpu.VMEM((2, share, width), LOW),
             pltpu.VMEM((2, share, width), LOW),
@@ -890,13 +973,13 @@
             pltpu.VMEM((steps, 16, width), f32),
             pltpu.SemaphoreType.DMA((9 + steps,)),
             pltpu.SemaphoreType.DMA((9 + steps,)),
-            pltpu.SemaphoreType.DMA((2, 2, 2, n - 1)),
-            pltpu.SemaphoreType.DMA((2, 2, 2, n - 1)),
+            pltpu.SemaphoreType.DMA((2, 3, 2, n - 1)),
+            pltpu.SemaphoreType.DMA((2, 3, 2, n - 1)),
         ],
         compiler_params=pltpu.CompilerParams(
-            collective_id=2, has_side_effects=True, vmem_limit_bytes=28 << 20
+            collective_id=2, has_side_effects=True, vmem_limit_bytes=(33 if n <= 16 else 60) << 20
         ),
-    )(hid, dq, dkv, qw, kw, vw, first, up_grad, down_grad, o_grad, vec)
+    )(rand, links, q_rows, kv, probs, wide_probs, wide_ctx, d_ctx, hid, weights, first, up_grad, down_grad, o_grad, vec)
 
 
 def per_device(
@@ -908,18 +991,18 @@
     tokens, width = hidden_in.shape
     local = q_weight.shape[1]
     rand = rand_blocks.T
-    qw, kw, vw = q_weight.T, k_weight.T, v_weight.T
-    query, slot_pair, o_full = project(hidden_in, qw, kw, vw, q_bias, v_bias, o_weight)
-    context, probs, wide_probs = attend_forward(
+    weights = jnp.concatenate([q_weight.T, k_weight.T, v_weight.T, o_weight], axis=0)
+    query, slot_pair, o_full = project(hidden_in, weights, jnp.stack([q_bias, v_bias]))
+    context, probs, wide_probs, wide_ctx, links = attend_forward(
         doc_blocks, rand, doc_mask.reshape(-1, 128), query, slot_pair
     )
     layer_out, first, d_ctx, up_part, down_part, o_part, vec = middle(
         context, o_full, hidden_in, o_bias, norm1_gain, norm1_shift, up_weight, up_bias, down_weight,
         down_bias, norm2_gain, norm2_shift, out_grad,
     )
-    dq, dkv = attend_backward(rand, query, slot_pair, probs, wide_probs, d_ctx)
     in_grad, big, small, vecs = tail(
-        hidden_in, dq, dkv, qw, kw, vw, first, up_part, down_part, o_part, vec
+        rand, links, query, slot_pair.reshape(-1, BLOCK, 2 * local), probs, wide_probs, wide_ctx, d_ctx, hidden_in, weights, first, up_part,
+        down_part, o_part, vec,
     )
     small = small.astype(f32)
     return (

time: 238 us -> 229 us (0.962)
  local copies, waits for them, and re-layouts: 11.2 us -> 4.85 us
  Pallas kernels: 222 us -> 219 us
    pallas_call x1 -> x0, Pallas kernels: 20.5 us -> none  [attend_backward(): pl.pallas_call(attend_bwd_kernel, name='attend_backward', out_shape=(jax....]
    pallas_call x1, Pallas kernels: 101 us -> 118 us  [tail(): pl.pallas_call(tail_kernel, name='tail', out_shape=(jax.ShapeDtypeStruct(...]
    unnamed x50 -> x34, local copies, waits for them, and re-layouts: 8.47 us -> 2.12 us
where the time goes in v4:
time: 229 us
  Pallas kernels  219 us (96%)
  local copies, waits for them, and re-layouts  4.85 us (2%)
  other arithmetic  4.14 us (2%)
    pallas_call x1, Pallas kernels, tail(): pl.pallas_call(tail_kernel, name='tail', out_shape=(jax.ShapeDtypeStruct(...  118 us
    pallas_call x1, Pallas kernels, middle(): pl.pallas_call(middle_kernel, name='middle', out_shape=(jax.ShapeDtypeStr...  55.5 us
    pallas_call x1, Pallas kernels, project(): pl.pallas_call(project_kernel, name='project_gather', out_shape=(jax.Shap...  31.8 us
    pallas_call x1, Pallas kernels, attend_forward(): pl.pallas_call(attend_fwd_kernel, name='attend_forward', out_shape=(jax.S...  13.3 us

profile of v4, /device:TPU:0, one launch (start us, length us, event | category | flops | bytes accessed | tf_op | source)
XLA Modules:
  0.0 228.8 jit_solution(8505011477577839566)
XLA Ops:
  0.7 0.0 copy-start
  0.7 1.4 pad_maximum_fusion.weights
  2.2 0.3 copy-done
  2.5 31.8 %project_gather.1 = (bf16[1024,256]{1,0:T(8,128)(2,1)S(1)}, bf16[4096,384]{1,0:T(8,128)(2,1)S(1)}, bf16[4,192,768]{2,1,0:T(8,128)(2,1)S(1)}) custom-call(bf16[1024,768]{1,0:T(8,128)(2,1)S(1)} %copy-done, bf16[768,768]{1,0:T(8,128)(2,1)S(1)} %pad_maximum_fusion.weights, f32[2,192]{1,0:T(2,128)S(1)} %pad_maximum_fusion.1.biases), custom_call_target="tpu_custom_call" | custom-call | tf_op jit(solution)/shard_map/project_gather/pallas_call | solution.py:271
  34.2 0.0 copy-start.1
  34.2 0.0 copy-start.2
  34.3 0.0 copy-start.3
  34.3 0.0 copy-start.6
  34.3 0.0 copy-start.7
  34.3 0.0 copy-start.8
  34.3 0.0 copy-start.9
  34.3 0.0 copy-start.10
  34.3 0.0 copy-start.11
  34.3 0.0 copy-start.12
  34.4 13.3 %attend_forward.1 = (bf16[1024,256]{1,0:T(8,128)(2,1)S(1)}, bf16[16,192,512]{2,1,0:T(8,128)(2,1)S(1)}, bf16[8,384,512]{2,1,0:T(8,128)(2,1)S(1)}, f32[128,256]{1,0:T(8,128)S(1)}, s32[112]{0:T(128)S(1)}) custom-call(s32[2]{0:T(128)S(1)} %copy-done.13, s32[3,16]{1,0:T(4,128)S(1)} %bitcast.32, s32[64,128]{1,0:T(8,128)S(1)} %bitcast.31, ...), custom_call_target="tpu_custom_call" | custom-call | tf_op jit(solution)/shard_map/attend_forward/pallas_call | solution.py:162
  47.7 55.5 %middle.1 = (f32[256,768]{1,0:T(8,128)S(1)}, f32[256,768]{1,0:T(8,128)S(1)}, bf16[1024,256]{1,0:T(8,128)(2,1)S(1)}, bf16[768,768]{1,0:T(8,128)(2,1)S(1)}, bf16[7...) custom-call(bf16[1024,256]{1,0:T(8,128)(2,1)S(1)} %get-tuple-element.38.ctx, ...), custom_call_target="tpu_custom_call" | custom-call | tf_op jit(solution)/shard_map/middle/pallas_call | solution.py:546
  103.2 118.4 %tail.1 = (f32[256,768]{1,0:T(8,128)S(1)}, bf16[2,768,768]{2,1,0:T(8,128)(2,1)S(1)}, bf16[2,384,768]{2,1,0:T(8,128)(2,1)S(1)}, f32[24,768]{1,0:T(8,128)S(1)}) custom-call(s32[3,16]{1,0:T(4,128)S(1)} %bitcast.33, s32[112]{0:T(128)S(1)} %get-tuple-element.41.links, bf16[1024,256]{1,0:T(8,128)(2,1)S(1)} %get-tuple-element.36.q_ref.q_rows, ...), custom_call_target="tpu_custom_call" | custom-call | tf_op jit(solution)/shard_map/tail/pallas_call | solution.py:943
  221.6 0.2 convert_element_type.15
  221.8 1.4 slice_bitcast_fusion
  223.3 0.6 fusion
  223.9 0.7 slice_reduce_fusion
  224.5 2.5 %bitcast_convert_fusion = (f32[768,768]{1,0:T(8,128)}, f32[768,768]{1,0:T(8,128)}) fusion(bf16[2,768,768]{2,1,0:T(8,128)(2,1)S(1)} %get-tuple-element.54), kind=kLoop, calls=%fused_computation.1 | loop fusion | flops 1179648 | bytes 7077888 | tf_op jit(solution)/shard_map/convert_element_type | solution.py:1011
  227.1 0.9 copy.39
  228.0 0.9 copy.40
  (21 shorter events, 0.1 us)
Async XLA Ops:
  0.7 1.8 copy-start
  0.7 1.5 copy-start.14
  0.7 1.5 copy-start.15
  0.7 33.7 %copy-start.4 = (s32[8192]{0:T(1024)S(1)}, s32[8192]{0:T(1024)}, u32[]{:S(2)}) copy-start(s32[8192]{0:T(1024)} %param.36) | copy-start | bytes 98308
  0.7 33.7 %copy-start.5 = (s32[16,3]{0,1:T(4,128)S(1)}, s32[16,3]{0,1:T(4,128)}, u32[]{:S(2)}) copy-start(s32[16,3]{0,1:T(4,128)} %param.38) | copy-start | bytes 580
  0.7 33.7 %copy-start.13 = (s32[2]{0:T(128)S(1)}, s32[2]{0:T(128)}, u32[]{:S(2)}) copy-start(s32[2]{0:T(128)} %blocks_ref.1) | copy-start | bytes 28
  34.2 13.4 %copy-start.1 = (bf16[768,768]{1,0:T(8,128)(2,1)S(1)}, bf16[768,768]{1,0:T(8,128)(2,1)}, u32[]{:S(2)}) copy-start(bf16[768,768]{1,0:T(8,128)(2,1)} %up_w.1) | copy-start | bytes 3538948
  34.2 13.4 %copy-start.2 = (bf16[768,768]{1,0:T(8,128)(2,1)S(1)}, bf16[768,768]{1,0:T(8,128)(2,1)}, u32[]{:S(2)}) copy-start(bf16[768,768]{1,0:T(8,128)(2,1)} %down_w.1) | copy-start | bytes 3538948
  34.3 13.4 %copy-start.3 = (f32[256,768]{1,0:T(8,128)S(1)}, f32[256,768]{1,0:T(8,128)}, u32[]{:S(2)}) copy-start(f32[256,768]{1,0:T(8,128)} %out_grad.1) | copy-start | bytes 2359300
  34.3 13.4 %copy-start.6 = (f32[768]{0:T(1024)S(1)}, f32[768]{0:T(1024)}, u32[]{:S(2)}) copy-start(f32[768]{0:T(1024)} %o_bias.1) | copy-start | bytes 9220
  34.3 13.4 %copy-start.7 = (f32[768]{0:T(1024)S(1)}, f32[768]{0:T(1024)}, u32[]{:S(2)}) copy-start(f32[768]{0:T(1024)} %gain1.1) | copy-start | bytes 9220
  34.3 13.4 %copy-start.8 = (f32[768]{0:T(1024)S(1)}, f32[768]{0:T(1024)}, u32[]{:S(2)}) copy-start(f32[768]{0:T(1024)} %shift1.1) | copy-start | bytes 9220
  34.3 13.4 %copy-start.9 = (f32[768]{0:T(1024)S(1)}, f32[768]{0:T(1024)}, u32[]{:S(2)}) copy-start(f32[768]{0:T(1024)} %up_b.1) | copy-start | bytes 9220
  34.3 13.4 %copy-start.10 = (f32[768]{0:T(1024)S(1)}, f32[768]{0:T(1024)}, u32[]{:S(2)}) copy-start(f32[768]{0:T(1024)} %down_b.1) | copy-start | bytes 9220
  34.3 13.4 %copy-start.11 = (f32[768]{0:T(1024)S(1)}, f32[768]{0:T(1024)}, u32[]{:S(2)}) copy-start(f32[768]{0:T(1024)} %gain2.1) | copy-start | bytes 9220
  34.3 13.4 %copy-start.12 = (f32[768]{0:T(1024)S(1)}, f32[768]{0:T(1024)}, u32[]{:S(2)}) copy-start(f32[768]{0:T(1024)} %shift2.1) | copy-start | bytes 9220

commit v5 on v4

--- a/solution.py
+++ b/solution.py
@@ -1,3 +1,5 @@
+import functools
+
 import jax
 import jax.numpy as jnp
 from jax import lax
@@ -307,15 +309,38 @@
 
 
 CHUNKS = 4
+EARLY = (1, 1)
+
+
+def ring_place(n):
+    seq = lax.axis_index("seq")
+    side, along = seq % 2, seq // 2
+    spot = along + side * (n - 1 - 2 * along)
+
+    def member(pos):
+        turn = pos // (n // 2)
+        return 2 * (pos + turn * (n - 1 - 2 * pos)) + turn
+
+    return spot, ({"seq": member((spot + 1) % n)}, {"seq": member((spot + n - 1) % n)})
+
+
+def ring_rows(n, spot, depth):
+    return pl.ds(pl.multiple_of(((spot + 2 * n) % n) * depth, 16), depth)
+
+
+def ring_depth(n, rows):
+    return 16 * (-(-rows // (16 * n)))
+
+
 ROOT = 0.7978845608028654
 CUBE = 0.044715
 
 
 def middle_kernel(
     ctx, o_full, hid, o_bias, gain1, shift1, up_w, up_b, down_w, down_b, gain2, shift2, out_grad,
-    layer_out, first_out, d_ctx, up_grad, down_grad, o_grad, vec,
+    layer_out, first_out, d_ctx, up_grad, down_grad, o_grad, vec, state,
     ctx_all, normed, unit1, inv1, second, x_all, s_all, f_all, slope, act, pre_all,
-    keep, to_core, from_core, to_far, from_far, send, recv,
+    keep, to_core, from_core, to_far, from_far, ring, send, recv, ring_send, ring_recv,
 ):
     share = out_grad.shape[0]
     rows = share // CHUNKS
@@ -326,8 +351,43 @@
     )
     core, far, both = flip(head, 0), flip(head, 1), flip(flip(head, 0), 1)
     order = (head, core, far, both)
-    greet(tuple({"head": at} for at in order[1:]))
+    n = lax.axis_size("seq")
+    spot, ways = ring_place(n)
+    greet(tuple({"head": at} for at in order[1:]) + ways)
     counter = [0]
+    ring_from = (down_grad, up_grad)
+    depth, side_cols = ring.shape[3], ring.shape[4]
+
+    def ring_chunk(kind, way, back):
+        rows_at = ring_rows(n, spot + (-back, back)[way], depth)
+        return ring_from[kind][rows_at, way * side_cols : (way + 1) * side_cols]
+
+    def ring_copy(kind, way, at):
+        return pltpu.make_async_remote_copy(
+            src_ref=ring.at[kind, way, at], dst_ref=ring.at[kind, way, at + 1],
+            send_sem=ring_send.at[kind, way, at], recv_sem=ring_recv.at[kind, way, at],
+            device_id=ways[way], device_id_type=MESH,
+        )
+
+    def ring_open(kind):
+        for way in range(2):
+            ring[kind, way, 0] = ring_chunk(kind, way, 0)
+            ring_copy(kind, way, 0).start()
+
+    def ring_step(kind, at):
+        for way in range(2):
+            ring_copy(kind, way, at).wait_recv()
+            total = ring[kind, way, at + 1].astype(jnp.float32) + ring_chunk(kind, way, at + 1).astype(jnp.float32)
+            if at + 1 < EARLY[kind]:
+                ring[kind, way, at + 1] = total.astype(LOW)
+                ring_copy(kind, way, at + 1).start()
+            else:
+                state[kind, way] = total.astype(LOW)
+
+    spare = up_grad.shape[0] - width
+    if spare:
+        up_grad[width:] = jnp.zeros((spare, up_grad.shape[1]), LOW)
+        down_grad[width:] = jnp.zeros((spare, width), LOW)
 
     def copy_to(src, dst, where):
         slot = counter[0]
@@ -480,15 +540,26 @@
     tokens = 4 * share
     step = 256
 
-    def weight_rows(at, carry):
-        cut = pl.ds(pl.multiple_of(at * step, step), step)
+    def down_rows(at):
+        cut = slice(at * step, (at + 1) * step)
         down_grad[cut, :] = dot_tn(
             act[:, :, :, cut].reshape(tokens, step), s_all[...].reshape(tokens, width)
         ).astype(LOW)
+
+    def up_rows(at):
+        cut = slice(at * step, (at + 1) * step)
         up_grad[cut, :] = dot_tn(
             x_all[:, :, :, cut].reshape(tokens, step), pre_all[...].reshape(tokens, up_w.shape[1])
         ).astype(LOW)
-        return carry
+
+    blocks = width // step
+    work = [functools.partial(down_rows, at) for at in range(blocks)] + [functools.partial(ring_open, 0)]
+    later = [functools.partial(up_rows, at) for at in range(blocks)] + [functools.partial(ring_open, 1)]
+    later.insert(2, functools.partial(ring_step, 0, 0))
+    moves = []
+    for at in range(max(EARLY)):
+        moves += [functools.partial(ring_step, 0, at)] if 0 < at < EARLY[0] else []
+        moves += [functools.partial(ring_step, 1, at)] if at < EARLY[1] else []
 
     gain1_sum, shift1_sum, o_sum = 0.0, 0.0, 0.0
     for part in range(CHUNKS):
@@ -501,7 +572,10 @@
         gain1_sum += column_sum(grad * unit_f)
         shift1_sum += column_sum(grad)
         o_sum += column_sum(first_f)
-    lax.fori_loop(0, width // step, weight_rows, 0)
+        if work:
+            work.pop(0)()
+    for task in work + later:
+        task()
 
     weight = o_full[head]
     weight = jnp.concatenate([jnp.zeros((256 - weight.shape[0], width), LOW), weight], axis=0)
@@ -521,11 +595,16 @@
     for part in range(CHUNKS):
         f_gather.to_core[part].wait_recv()
         o_total += back(part, 0)
+    f_gather.pass_on(0)
     for part in range(CHUNKS):
-        f_gather.pass_on(part)
-    for part in range(CHUNKS):
+        if part + 1 < CHUNKS:
+            f_gather.pass_on(part + 1)
+        if moves:
+            moves.pop(0)()
         f_gather.relay[part].wait_recv()
         o_total += back(part, 1)
+    for task in moves:
+        task()
     o_grad[...] = o_total[256 - o_grad.shape[0] :].astype(LOW)
     zero = jnp.zeros((1, width), jnp.float32)
     vec[...] = jnp.concatenate(
@@ -533,6 +612,10 @@
     )
     for copy in made:
         copy.wait_send()
+    for kind in range(2):
+        for way in range(2):
+            for at in range(EARLY[kind]):
+                ring_copy(kind, way, at).wait_send()
 
 
 def middle(ctx, o_full, hid, o_bias, gain1, shift1, up_w, up_b, down_w, down_b, gain2, shift2, out_grad):
@@ -540,6 +623,9 @@
     share = out_grad.shape[0]
     rows = share // CHUNKS
     hidden, local = up_w.shape[1], o_full.shape[1]
+    n = lax.axis_size("seq")
+    depth = ring_depth(n, width)
+    assert hidden == width
     f32 = jnp.float32
     gathered = pltpu.VMEM((CHUNKS, 4, rows, width), LOW)
     copies = CHUNKS * (3 + 3 * 3 + 2 * 3)
@@ -550,13 +636,14 @@
             jax.ShapeDtypeStruct((share, width), f32),
             jax.ShapeDtypeStruct((share, width), f32),
             jax.ShapeDtypeStruct((tokens, 256), LOW),
-            jax.ShapeDtypeStruct((width, hidden), LOW),
-            jax.ShapeDtypeStruct((hidden, width), LOW),
+            jax.ShapeDtypeStruct((n * depth, hidden), LOW),
+            jax.ShapeDtypeStruct((n * depth, width), LOW),
             jax.ShapeDtypeStruct((local, width), LOW),
             jax.ShapeDtypeStruct((8, width), f32),
+            jax.ShapeDtypeStruct((2, 2, depth, width // 2), LOW),
         ),
         in_specs=[VM] * 13,
-        out_specs=(VM,) * 7,
+        out_specs=(VM,) * 8,
         scratch_shapes=[
             pltpu.VMEM((4, share, 256), LOW),
             pltpu.VMEM((share, width), f32),
@@ -574,8 +661,11 @@
             pltpu.VMEM((2, CHUNKS, 2, rows, width), LOW),
             pltpu.VMEM((2, CHUNKS, rows, width), LOW),
             pltpu.VMEM((2, CHUNKS, rows, width), LOW),
+            pltpu.VMEM((2, 2, max(EARLY) + 1, depth, width // 2), LOW),
             pltpu.SemaphoreType.DMA((copies,)),
             pltpu.SemaphoreType.DMA((copies,)),
+            pltpu.SemaphoreType.DMA((2, 2, max(EARLY))),
+            pltpu.SemaphoreType.DMA((2, 2, max(EARLY))),
         ],
         compiler_params=pltpu.CompilerParams(
             collective_id=1, has_side_effects=True, vmem_limit_bytes=30 << 20
@@ -585,28 +675,24 @@
     )
 
 
+FILL = ((), (1, 0), (0, 1))
+
+
 def tail_kernel(
     rand, links, q_rows, kv, probs, wide_probs, wide_ctx, d_ctx, hid, weights, first, up_grad, down_grad, o_grad,
-    vec, in_grad, big_out, small_out, vec_out,
+    vec, state, in_grad, big_out, small_out, vec_out,
     dq, acc, loose, wide_dq, wide_mean, pair_send, pair_in, pair_out, partial, small, big_ring, small_ring, near_out, near_in, far_out, far_in,
-    vec_now, vec_send, vec_recv, send, recv, ring_send, ring_recv,
+    vec_now, vec_send, vec_recv, send, recv, ring_send, ring_recv, fold_send, fold_recv,
 ):
     n = lax.axis_size("seq")
     tokens, width = hid.shape
     half, share = tokens // 2, first.shape[0]
-    depths = (big_ring.shape[3], big_ring.shape[3], small_ring.shape[2])
+    depths = (big_ring.shape[3],) * 2 + (small_ring.shape[3],) * 2
     spans = SLOT_LEN // tokens
     seq, head = lax.axis_index("seq"), lax.axis_index("head")
     place = seq % spans
     f32 = jnp.float32
-    side, along = seq % 2, seq // 2
-    spot = along + side * (n - 1 - 2 * along)
-
-    def member(pos):
-        turn = pos // (n // 2)
-        return 2 * (pos + turn * (n - 1 - 2 * pos)) + turn
-
-    ways = ({"seq": member((spot + 1) % n)}, {"seq": member((spot + n - 1) % n)})
+    spot, ways = ring_place(n)
     signs = (-1, 1)
     by_x, by_z = {"seq": flip(seq, 0)}, {"seq": flip(seq, 1)}
     core, far = flip(head, 0), flip(head, 1)
@@ -621,18 +707,82 @@
     x_at, z_at = flip(place, 0), flip(place, 1)
     d_at = flip(x_at, 1)
 
-    side_cols = up_grad.shape[1] // 2
-    left, right, full = pl.ds(0, side_cols), pl.ds(side_cols, side_cols), pl.ds(0, width)
-    pair_of = (up_grad, down_grad)
+    side_cols = width // 2
+    sides = (pl.ds(0, side_cols), pl.ds(side_cols, side_cols))
     rings = (
-        (big_ring.at[0], big_out, pair_of, left),
-        (big_ring.at[1], big_out, pair_of, right),
-        (small_ring, small_out, (small.at[0], small.at[1]), full),
+        (big_ring.at[0], (big_out.at[0],) * 2, (down_grad,) * 2, sides),
+        (big_ring.at[1], (big_out.at[1],) * 2, (up_grad,) * 2, sides),
     )
     kinds = len(rings)
 
     def chunk(kind, pos):
-        return pl.ds(pl.multiple_of(((pos + 2 * n) % n) * depths[kind], 16), depths[kind])
+        return ring_rows(n, pos, depths[kind])
+
+    reaches = ((n // 2, n // 2 - 1), (n // 2 - 1, n // 2))
+
+    def guard(holds, body):
+        if isinstance(holds, bool):
+            if holds:
+                body()
+        else:
+            pl.when(holds)(body)
+
+    def fold_copy(kind, way, step):
+        return pltpu.make_async_remote_copy(
+            src_ref=small_ring.at[kind, way, step], dst_ref=small_ring.at[kind, way, step + 1],
+            send_sem=fold_send.at[0, kind, way, step], recv_sem=fold_recv.at[0, kind, way, step],
+            device_id=ways[way], device_id_type=MESH,
+        )
+
+    def fan_copy(kind, way, step):
+        rows = small_out.at[kind, chunk(2, spot + signs[way] * step)]
+        return pltpu.make_async_remote_copy(
+            src_ref=rows, dst_ref=rows,
+            send_sem=fold_send.at[1, kind, way, step], recv_sem=fold_recv.at[1, kind, way, step],
+            device_id=ways[way], device_id_type=MESH,
+        )
+
+    def fold_mine(kind, way, step):
+        return small[kind, chunk(2, spot - signs[way] * (reaches[kind][way] - step)), :]
+
+    def fold_open(kind):
+        for way in range(2):
+            small_ring[kind, way, 0] = fold_mine(kind, way, 0)
+            fold_copy(kind, way, 0).start()
+
+    def fold_step(kind, step):
+        for way in range(2):
+
+            def body(way=way):
+                fold_copy(kind, way, step).wait_recv()
+                total = small_ring[kind, way, step + 1].astype(f32) + fold_mine(kind, way, step + 1).astype(f32)
+                small_ring[kind, way, step + 1] = total.astype(LOW)
+                fold_copy(kind, way, step + 1).start()
+
+            guard(step < reaches[kind][way] - 1, body)
+
+    def fold_close(kind):
+        total = small[kind, chunk(2, spot), :].astype(f32)
+        for way in range(2):
+            reach = reaches[kind][way]
+            fold_copy(kind, way, reach - 1).wait_recv()
+            total += small_ring[kind, way, reach].astype(f32)
+        small_out[kind, chunk(2, spot)] = total.astype(LOW)
+        for way in range(2):
+            fan_copy(kind, way, 0).start()
+
+    def fan_step(kind, step):
+        for way in range(2):
+
+            def body(way=way):
+                fan_copy(kind, way, step).wait_recv()
+                fan_copy(kind, way, step + 1).start()
+
+            guard(step < reaches[kind][way] - 1, body)
+
+    def fan_close(kind):
+        for way in range(2):
+            fan_copy(kind, way, reaches[kind][way] - 1).wait_recv()
 
     def reduce_copy(kind, way, step):
         ring = rings[kind][0]
@@ -643,7 +793,7 @@
         )
 
     def spread_copy(kind, way, step):
-        rows = rings[kind][1].at[way, chunk(kind, spot + signs[way] * (step - 1)), rings[kind][3]]
+        rows = rings[kind][1][way].at[chunk(kind, spot + signs[way] * (step - 1)), rings[kind][3][way]]
         return pltpu.make_async_remote_copy(
             src_ref=rows, dst_ref=rows,
             send_sem=ring_send.at[1, kind, way, step], recv_sem=ring_recv.at[1, kind, way, step],
@@ -653,17 +803,19 @@
     def open_ring(kind):
         ring, _, source, cols = rings[kind]
         for way in range(2):
-            ring[way, 0] = source[way][chunk(kind, spot), cols]
+            ring[way, 0] = source[way][chunk(kind, spot), cols[way]]
             reduce_copy(kind, way, 0).start()
 
     def add_ring(kind, way, step):
         ring, _, source, cols = rings[kind]
         reduce_copy(kind, way, step).wait_recv()
-        mine = source[way][chunk(kind, spot + signs[way] * (step + 1)), cols]
+        mine = source[way][chunk(kind, spot + signs[way] * (step + 1)), cols[way]]
         ring[way, step + 1] = (ring[way, step + 1].astype(f32) + mine.astype(f32)).astype(LOW)
 
-    open_ring(0)
-    open_ring(1)
+    for kind in range(2):
+        for way in range(2):
+            rings[kind][0][way, EARLY[kind]] = state[kind, way]
+            reduce_copy(kind, way, EARLY[kind]).start()
     local_blocks = tokens // BLOCK
     chunk_rows = WIN * BLOCK
     turns = local_blocks // 2
@@ -733,6 +885,31 @@
             add_ring(kind, way, step)
             reduce_copy(kind, way, step + 1).start()
 
+    def open_spread(kind):
+        ring, out, _, cols = rings[kind]
+        for way in range(2):
+            add_ring(kind, way, n - 2)
+            out[way][chunk(kind, spot - signs[way]), cols[way]] = ring[way, n - 1]
+            spread_copy(kind, way, 0).start()
+
+    def spread_step(kind, step):
+        for way in range(2):
+            spread_copy(kind, way, step).wait_recv()
+            spread_copy(kind, way, step + 1).start()
+
+    def advance(kind, at):
+        step = at + EARLY[kind]
+
+        @pl.when(step < n - 2)
+        def _():
+            reduce_step(kind, step)
+
+        if turns + EARLY[kind] > n - 2:
+
+            @pl.when(step == n - 2)
+            def _():
+                open_spread(kind)
+
     def turn(at, carry):
         @pl.when(place == 0)
         def _():
@@ -745,19 +922,14 @@
             add_rows(from_row, chunk_rows, dot_tn(d_score, q_all), dot_tn(low_probs, do_all))
             wide_dq[...] += dot_nn(d_score, wide_rows(at, 0))
 
-        @pl.when(at < n - 2)
-        def _():
-            reduce_step(0, at)
+        advance(0, at)
 
         @pl.when(jnp.logical_or(place != 0, at != 0))
         def _():
             one_block(2 * at)
             one_block(2 * at + 1)
 
-        @pl.when(at < n - 2)
-        def _():
-            reduce_step(1, at)
-
+        advance(1, at)
         return carry
 
     lax.fori_loop(0, turns, turn, 0)
@@ -775,29 +947,55 @@
     copies.append(remote(pair_out.at[0], pair_in.at[4], send, recv, 4, by_x))
     copies.append(remote(pair_out.at[1], pair_in.at[5], send, recv, 5, by_z))
 
-    def late_ring(step, carry):
-        reduce_step(0, step)
-        reduce_step(1, step)
-        return carry
-
-    lax.fori_loop(min(turns, n - 2), n - 2, late_ring, 0)
-
-    def open_spread(kind):
-        ring, out, _, cols = rings[kind]
-        for way in range(2):
-            add_ring(kind, way, n - 2)
-            out[way, chunk(kind, spot - signs[way]), cols] = ring[way, n - 1]
-            spread_copy(kind, way, 0).start()
-
-    def spread_step(kind, step):
-        for way in range(2):
-            spread_copy(kind, way, step).wait_recv()
-            spread_copy(kind, way, step + 1).start()
-
-    open_spread(0)
-    open_spread(1)
+    state_of = [
+        [min(turns + EARLY[kind], n - 1), 0] for kind in range(2)
+    ]
+
+    def one_move(kind):
+        reduced, spread = state_of[kind]
+        if reduced < n - 2:
+            reduce_step(kind, reduced)
+            state_of[kind][0] += 1
+        elif reduced == n - 2:
+            open_spread(kind)
+            state_of[kind][0] += 1
+        elif spread < n - 2:
+            spread_step(kind, spread)
+            state_of[kind][1] += 1
+        else:
+            return False
+        return True
+
+    def fill(order):
+        for kind in order:
+            one_move(kind)
+
+    def finish(kind):
+        reduced, spread = state_of[kind]
+
+        def more_reduce(step, carry):
+            reduce_step(kind, step)
+            return carry
+
+        def more_spread(step, carry):
+            spread_step(kind, step)
+            return carry
+
+        if reduced < n - 2:
+            lax.fori_loop(reduced, n - 2, more_reduce, 0)
+        if reduced <= n - 2:
+            open_spread(kind)
+        if spread < n - 2:
+            lax.fori_loop(spread, n - 2, more_spread, 0)
+
     local = weights.shape[0] // 4
     qw, kw, vw = (weights.at[pl.ds(at * local, local)] for at in range(3))
+    small[1, 0:local] = dot_tn(dq[...], hid[...])[0:local].astype(LOW)
+    small[1, local : 2 * local] = o_grad[...]
+    spare = small.shape[1] - 2 * local
+    if spare:
+        small[:, 2 * local :] = jnp.zeros((2, spare, width), LOW)
+    fold_open(1)
     gap = jnp.zeros((256 - local, width), LOW)
     partial[...] = dot_nn(dq[...], jnp.concatenate([qw[...], gap], axis=0))
     copies[0].wait_recv()
@@ -806,11 +1004,7 @@
     copies[1].wait_recv()
     pair_out[1] = (acc_rows(z_at, 1) + pair_in[1].astype(f32)).astype(LOW)
     copies[5].start()
-    small[1, 0:local] = dot_tn(dq[...], hid[...])[0:local].astype(LOW)
-    small[1, local : 2 * local] = o_grad[...]
-    spare = small.shape[1] - 2 * local
-    if spare:
-        small[:, 2 * local :] = jnp.zeros((2, spare, width), LOW)
+    fill(FILL[0])
     for at in range(2, 6):
         copies[at].wait_recv()
     own = []
@@ -820,7 +1014,8 @@
         own.append((mine + pair_in[first_in].astype(f32) + pair_in[second_in].astype(f32)).astype(LOW))
     own = jnp.concatenate(own, axis=0)
     small[0, 0 : 2 * local] = dot_tn(own, hid[...]).astype(LOW)
-    open_ring(2)
+    fold_open(0)
+    fill(FILL[1])
 
     def share_rows(owner):
         return partial[pl.ds(pl.multiple_of(owner * share, share), share), :]
@@ -843,7 +1038,12 @@
         far_out[...] = (share_rows(far) + near_in[0].astype(f32)).astype(LOW)
         far_copy.start()
 
-    tasks = [key_term, value_term, send_near, send_far]
+    def finish_rows():
+        near[1].wait_recv()
+        far_copy.wait_recv()
+        in_grad[...] = first[...] + share_rows(head) + near_in[1].astype(f32) + far_in[...].astype(f32)
+
+    tasks = [key_term, value_term, send_near, send_far, None, finish_rows]
     fill_row = lambda rows: jnp.concatenate([rows, jnp.zeros((1, width - rows.shape[1]), f32)], axis=1)
     sums = jnp.concatenate(
         [
@@ -875,43 +1075,42 @@
         if at == steps - 1:
             vec_out[0:8] = total[0:8]
 
-    spread_done = 0
+    unrolled = min(n // 2 - 1, 4)
+
+    def twice(move):
+        def body(step, carry=0):
+            move(0, step)
+            move(1, step)
+            return carry
+
+        return body
+
+    def close_fold():
+        if unrolled < n // 2 - 1:
+            lax.fori_loop(unrolled, n // 2 - 1, twice(fold_step), 0)
+        fold_close(0)
+        fold_close(1)
+
+    def close_fan():
+        if unrolled < n // 2 - 1:
+            lax.fori_loop(unrolled, n // 2 - 1, twice(fan_step), 0)
+        fan_close(0)
+        fan_close(1)
+
+    slots = [functools.partial(twice(fold_step), at) for at in range(unrolled)] + [close_fold]
+    slots += [functools.partial(twice(fan_step), at) for at in range(unrolled)] + [close_fan]
     vec_start(0)
-    for at in range(min(steps, n - 2)):
-        reduce_step(2, at)
-        spread_step(at % 2, at // 2)
-        if at < len(tasks):
+    for at, slot in enumerate(slots):
+        slot()
+        fill(FILL[2])
+        if at < len(tasks) and tasks[at]:
             tasks[at]()
-        vec_finish(at)
-        if at + 1 < steps:
-            vec_start(at + 1)
-
-    def ring_body(step, carry):
-        reduce_step(2, step)
-        return carry
-
-    lax.fori_loop(steps, n - 2, ring_body, 0)
-    open_spread(2)
-    near[1].wait_recv()
-    far_copy.wait_recv()
-    in_grad[...] = first[...] + share_rows(head) + near_in[1].astype(f32) + far_in[...].astype(f32)
-    done_left, done_right = (steps + 1) // 2, steps // 2
-
-    def spread_all(step, carry):
-        spread_step(0, step + done_left)
-        spread_step(2, step)
-        spread_step(1, step + done_left)
-        return carry
-
-    def spread_last(step, carry):
-        spread_step(2, step)
-        return carry
-
-    for step in range(done_right, done_left):
-        spread_step(1, step)
-    rest = n - 2 - done_left
-    lax.fori_loop(0, rest, spread_all, 0)
-    lax.fori_loop(rest, n - 2, spread_last, 0)
+        if at < steps:
+            vec_finish(at)
+            if at + 1 < steps:
+                vec_start(at + 1)
+    for kind in range(2):
+        finish(kind)
     for kind in range(kinds):
         for way in range(2):
             spread_copy(kind, way, n - 2).wait_recv()
@@ -919,26 +1118,35 @@
     def close_body(step, carry):
         for kind in range(kinds):
             for way in range(2):
-                reduce_copy(kind, way, step).wait_send()
+                guard(step >= EARLY[kind], lambda kind=kind, way=way: reduce_copy(kind, way, step).wait_send())
                 spread_copy(kind, way, step).wait_send()
         return carry
 
+    def close_small(step, carry):
+        for kind in range(2):
+            for way in range(2):
+
+                def body(kind=kind, way=way):
+                    fold_copy(kind, way, step).wait_send()
+                    fan_copy(kind, way, step).wait_send()
+
+                guard(step < reaches[kind][way], body)
+        return carry
+
+    lax.fori_loop(0, n // 2, close_small, 0)
     lax.fori_loop(0, n - 1, close_body, 0)
     for copy in copies + near + [far_copy] + [vec_copy(at) for at in range(steps)]:
         copy.wait_send()
 
 
-def tail(rand, links, q_rows, kv, probs, wide_probs, wide_ctx, d_ctx, hid, weights, first, up_grad, down_grad, o_grad, vec):
+def tail(rand, links, q_rows, kv, probs, wide_probs, wide_ctx, d_ctx, hid, weights, first, up_grad, down_grad, o_grad, vec, state):
     n = lax.axis_size("seq")
     tokens, width = hid.shape
     share = first.shape[0]
     pair = kv.shape[2]
-    depth, less = 16 * (-(-width // (16 * n))), 16 * (-(-pair // (16 * n)))
+    depth, less = ring_depth(n, width), ring_depth(n, pair)
     rows = n * depth
     f32 = jnp.float32
-    if rows > width:
-        up_grad = jnp.pad(up_grad, ((0, rows - width), (0, 0)))
-        down_grad = jnp.pad(down_grad, ((0, rows - width), (0, 0)))
     steps = n.bit_length() + 1
     return pl.pallas_call(
         tail_kernel,
@@ -949,7 +1157,7 @@
             jax.ShapeDtypeStruct((2, n * less, width), LOW),
             jax.ShapeDtypeStruct((24, width), f32),
         ),
-        in_specs=[pl.BlockSpec(memory_space=pltpu.SMEM)] * 2 + [VM] * 13,
+        in_specs=[pl.BlockSpec(memory_space=pltpu.SMEM)] * 2 + [VM] * 14,
         out_specs=(VM,) * 4,
         scratch_shapes=[
             pltpu.VMEM((tokens, 256), LOW),
@@ -963,7 +1171,7 @@
             pltpu.VMEM((tokens, width), f32),
             pltpu.VMEM((2, n * less, width), LOW),
             pltpu.VMEM((2, 2, n, depth, up_grad.shape[1] // 2), LOW),
-            pltpu.VMEM((2, n, less, width), LOW),
+            pltpu.VMEM((2, 2, n // 2 + 1, less, width), LOW),
             pltpu.VMEM((2, share, width), LOW),
             pltpu.VMEM((2, share, width), LOW),
             pltpu.VMEM((share, width), LOW),
@@ -973,13 +1181,15 @@
             pltpu.VMEM((steps, 16, width), f32),
             pltpu.SemaphoreType.DMA((9 + steps,)),
             pltpu.SemaphoreType.DMA((9 + steps,)),
-            pltpu.SemaphoreType.DMA((2, 3, 2, n - 1)),
-            pltpu.SemaphoreType.DMA((2, 3, 2, n - 1)),
+            pltpu.SemaphoreType.DMA((2, 2, 2, n - 1)),
+            pltpu.SemaphoreType.DMA((2, 2, 2, n - 1)),
+            pltpu.SemaphoreType.DMA((2, 2, 2, n // 2)),
+            pltpu.SemaphoreType.DMA((2, 2, 2, n // 2)),
         ],
         compiler_params=pltpu.CompilerParams(
-            collective_id=2, has_side_effects=True, vmem_limit_bytes=(33 if n <= 16 else 60) << 20
+            collective_id=2, has_side_effects=True, vmem_limit_bytes=(33 if n <= 16 else 61) << 20
         ),
-    )(rand, links, q_rows, kv, probs, wide_probs, wide_ctx, d_ctx, hid, weights, first, up_grad, down_grad, o_grad, vec)
+    )(rand, links, q_rows, kv, probs, wide_probs, wide_ctx, d_ctx, hid, weights, first, up_grad, down_grad, o_grad, vec, state)
 
 
 def per_device(
@@ -996,19 +1206,19 @@
     context, probs, wide_probs, wide_ctx, links = attend_forward(
         doc_blocks, rand, doc_mask.reshape(-1, 128), query, slot_pair
     )
-    layer_out, first, d_ctx, up_part, down_part, o_part, vec = middle(
+    layer_out, first, d_ctx, up_part, down_part, o_part, vec, state = middle(
         context, o_full, hidden_in, o_bias, norm1_gain, norm1_shift, up_weight, up_bias, down_weight,
         down_bias, norm2_gain, norm2_shift, out_grad,
     )
     in_grad, big, small, vecs = tail(
         rand, links, query, slot_pair.reshape(-1, BLOCK, 2 * local), probs, wide_probs, wide_ctx, d_ctx, hidden_in, weights, first, up_part,
-        down_part, o_part, vec,
+        down_part, o_part, vec, state,
     )
     small = small.astype(f32)
     return (
         layer_out, in_grad, small[1, :local].T, vecs[8, :local], small[0, :local].T,
         small[0, local : 2 * local].T, vecs[9, local : 2 * local], small[1, local : 2 * local],
-        vecs[0], vecs[1], vecs[2], big[0, :width].astype(f32), vecs[22], big[1, :width].astype(f32),
+        vecs[0], vecs[1], vecs[2], big[1, :width].astype(f32), vecs[22], big[0, :width].astype(f32),
         vecs[3], vecs[4], vecs[5],
     )
 

time: 229 us -> 216 us (0.943)
  Pallas kernels: 219 us -> 205 us
    pallas_call x1, Pallas kernels: 118 us -> 104 us  [tail(): pl.pallas_call(tail_kernel, name='tail', out_shape=(jax.ShapeDtypeStruct(...]
where the time goes in v5:
time: 216 us; the launch traced here: 215 us
  Pallas kernels  205 us (95%)
  local copies, waits for them, and re-layouts  4.85 us (2%)
  other arithmetic  4.14 us (2%)
    pallas_call x1, Pallas kernels, tail(): pl.pallas_call(tail_kernel, name='tail', out_shape=(jax.ShapeDtypeStruct(...  104 us
    pallas_call x1, Pallas kernels, middle(): pl.pallas_call(middle_kernel, name='middle', out_shape=(jax.ShapeDtypeStr...  56.3 us
    pallas_call x1, Pallas kernels, project(): pl.pallas_call(project_kernel, name='project_gather', out_shape=(jax.Shap...  31.8 us
    pallas_call x1, Pallas kernels, attend_forward(): pl.pallas_call(attend_fwd_kernel, name='attend_forward', out_shape=(jax.S...  13.3 us

profile of v5, /device:TPU:0, one launch (start us, length us, event | category | flops | bytes accessed | tf_op | source)
XLA Modules:
  0.0 215.4 jit_solution(6839716489866744199)
XLA Ops:
  0.7 0.0 copy-start
  0.7 1.4 pad_maximum_fusion.weights
  2.2 0.3 copy-done
  2.5 31.8 %project_gather.1 = (bf16[1024,256]{1,0:T(8,128)(2,1)S(1)}, bf16[4096,384]{1,0:T(8,128)(2,1)S(1)}, bf16[4,192,768]{2,1,0:T(8,128)(2,1)S(1)}) custom-call(bf16[1024,768]{1,0:T(8,128)(2,1)S(1)} %copy-done, bf16[768,768]{1,0:T(8,128)(2,1)S(1)} %pad_maximum_fusion.weights, f32[2,192]{1,0:T(2,128)S(1)} %pad_maximum_fusion.1.biases), custom_call_target="tpu_custom_call" | custom-call | tf_op jit(solution)/shard_map/project_gather/pallas_call | solution.py:273
  34.2 0.0 copy-start.1
  34.2 0.0 copy-start.2
  34.3 0.0 copy-start.3
  34.3 0.0 copy-start.6
  34.3 0.0 copy-start.7
  34.3 0.0 copy-start.8
  34.3 0.0 copy-start.9
  34.3 0.0 copy-start.10
  34.3 0.0 copy-start.11
  34.3 0.0 copy-start.12
  34.4 13.3 %attend_forward.1 = (bf16[1024,256]{1,0:T(8,128)(2,1)S(1)}, bf16[16,192,512]{2,1,0:T(8,128)(2,1)S(1)}, bf16[8,384,512]{2,1,0:T(8,128)(2,1)S(1)}, f32[128,256]{1,0:T(8,128)S(1)}, s32[112]{0:T(128)S(1)}) custom-call(s32[2]{0:T(128)S(1)} %copy-done.13, s32[3,16]{1,0:T(4,128)S(1)} %bitcast.32, s32[64,128]{1,0:T(8,128)S(1)} %bitcast.31, ...), custom_call_target="tpu_custom_call" | custom-call | tf_op jit(solution)/shard_map/attend_forward/pallas_call | solution.py:164
  47.7 56.3 %middle.1 = (f32[256,768]{1,0:T(8,128)S(1)}, f32[256,768]{1,0:T(8,128)S(1)}, bf16[1024,256]{1,0:T(8,128)(2,1)S(1)}, bf16[768,768]{1,0:T(8,128)(2,1)S(1)}, bf16[7...) custom-call(bf16[1024,256]{1,0:T(8,128)(2,1)S(1)} %get-tuple-element, ...), custom_call_target="tpu_custom_call" | custom-call | tf_op jit(solution)/shard_map/middle/pallas_call | solution.py:632
  104.1 104.1 %tail.1 = (f32[256,768]{1,0:T(8,128)S(1)}, bf16[2,768,768]{2,1,0:T(8,128)(2,1)S(1)}, bf16[2,384,768]{2,1,0:T(8,128)(2,1)S(1)}, f32[24,768]{1,0:T(8,128)S(1)}) custom-call(s32[3,16]{1,0:T(4,128)S(1)} %bitcast.33, s32[112]{0:T(128)S(1)} %get-tuple-element.42.links, bf16[1024,256]{1,0:T(8,128)(2,1)S(1)} %get-tuple-element.37.q_ref.q_rows, ...), custom_call_target="tpu_custom_call" | custom-call | tf_op jit(solution)/shard_map/tail/pallas_call | solution.py:1151
  208.2 0.2 convert_element_type.15
  208.3 1.4 slice_bitcast_fusion
  209.8 0.6 fusion
  210.4 0.7 slice_reduce_fusion
  211.1 2.5 %bitcast_convert_fusion = (f32[768,768]{1,0:T(8,128)}, f32[768,768]{1,0:T(8,128)}) fusion(bf16[2,768,768]{2,1,0:T(8,128)(2,1)S(1)} %get-tuple-element.56), kind=kLoop, calls=%fused_computation.1 | loop fusion | flops 1179648 | bytes 7077888 | tf_op jit(solution)/shard_map/convert_element_type | solution.py:1221
  213.6 0.9 copy.39
  214.5 0.9 copy.40
  (21 shorter events, 0.1 us)
Async XLA Ops:
  0.7 1.8 copy-start
  0.7 1.5 copy-start.14
  0.7 1.5 copy-start.15
  0.7 33.7 %copy-start.4 = (s32[8192]{0:T(1024)S(1)}, s32[8192]{0:T(1024)}, u32[]{:S(2)}) copy-start(s32[8192]{0:T(1024)} %param.36) | copy-start | bytes 98308
  0.7 33.7 %copy-start.5 = (s32[16,3]{0,1:T(4,128)S(1)}, s32[16,3]{0,1:T(4,128)}, u32[]{:S(2)}) copy-start(s32[16,3]{0,1:T(4,128)} %param.38) | copy-start | bytes 580
  0.7 33.7 %copy-start.13 = (s32[2]{0:T(128)S(1)}, s32[2]{0:T(128)}, u32[]{:S(2)}) copy-start(s32[2]{0:T(128)} %blocks_ref.1) | copy-start | bytes 28
  34.2 13.4 %copy-start.1 = (bf16[768,768]{1,0:T(8,128)(2,1)S(1)}, bf16[768,768]{1,0:T(8,128)(2,1)}, u32[]{:S(2)}) copy-start(bf16[768,768]{1,0:T(8,128)(2,1)} %up_w.1) | copy-start | bytes 3538948
  34.2 13.4 %copy-start.2 = (bf16[768,768]{1,0:T(8,128)(2,1)S(1)}, bf16[768,768]{1,0:T(8,128)(2,1)}, u32[]{:S(2)}) copy-start(bf16[768,768]{1,0:T(8,128)(2,1)} %down_w.1) | copy-start | bytes 3538948
  34.3 13.4 %copy-start.3 = (f32[256,768]{1,0:T(8,128)S(1)}, f32[256,768]{1,0:T(8,128)}, u32[]{:S(2)}) copy-start(f32[256,768]{1,0:T(8,128)} %out_grad.1) | copy-start | bytes 2359300
  34.3 13.4 %copy-start.6 = (f32[768]{0:T(1024)S(1)}, f32[768]{0:T(1024)}, u32[]{:S(2)}) copy-start(f32[768]{0:T(1024)} %o_bias.1) | copy-start | bytes 9220
  34.3 13.4 %copy-start.7 = (f32[768]{0:T(1024)S(1)}, f32[768]{0:T(1024)}, u32[]{:S(2)}) copy-start(f32[768]{0:T(1024)} %gain1.1) | copy-start | bytes 9220
  34.3 13.4 %copy-start.8 = (f32[768]{0:T(1024)S(1)}, f32[768]{0:T(1024)}, u32[]{:S(2)}) copy-start(f32[768]{0:T(1024)} %shift1.1) | copy-start | bytes 9220
  34.3 13.4 %copy-start.9 = (f32[768]{0:T(1024)S(1)}, f32[768]{0:T(1024)}, u32[]{:S(2)}) copy-start(f32[768]{0:T(1024)} %up_b.1) | copy-start | bytes 9220
  34.3 13.4 %copy-start.10 = (f32[768]{0:T(1024)S(1)}, f32[768]{0:T(1024)}, u32[]{:S(2)}) copy-start(f32[768]{0:T(1024)} %down_b.1) | copy-start | bytes 9220
  34.3 13.4 %copy-start.11 = (f32[768]{0:T(1024)S(1)}, f32[768]{0:T(1024)}, u32[]{:S(2)}) copy-start(f32[768]{0:T(1024)} %gain2.1) | copy-start | bytes 9220
  34.3 13.4 %copy-start.12 = (f32[768]{0:T(1024)S(1)}, f32[768]{0:T(1024)}, u32[]{:S(2)}) copy-start(f32[768]{0:T(1024)} %shift2.1) | copy-start | bytes 9220
